TPU v7x, 256 devices: a whole 4x4x8 slice. The times are simulated.
256 devices in a mesh: term: 8 (over z), sec: 32 (over y, x, core).
Axes of the slice: x: 4, y: 4, z: 8, core: 2. Of those that a mesh axis runs over, the one named last changes fastest.
Arguments:
- start_vectors: bfloat16 [2, 64, 256, 256], P(None, 'sec'), may hold values from -6 to 6
- left_env: bfloat16 [32, 64, 256, 256], P('term', 'sec'), may hold values from -0.375 to 0.375
- right_env: bfloat16 [32, 64, 256, 256], P('term', 'sec'), may hold values from -0.375 to 0.375
- term_shift: int32 [32], P('term'), may hold values from -1 to 1
- precond: float32 [64, 256, 256], P('sec'), may hold values from 0.25 to 4
- block_dims: int32 [64], P('sec'), may hold values from 1 to 256, 8192 in all
Outputs:
- vector: float32 [2, 64, 256, 256], P(None, 'sec', 'term')
- energy: float32 [2], replicated
Inputs may be any that keep to these rules, and one draw needn't show every extreme that they name: `block_dims`: one block has exactly 256 live states.
All inputs are finite; a program needn't handle non-finite values.
Results may differ from a plain program's by a relative error of at most 0.0036.
Values may be sent and summed in bfloat16 or wider, within the bound.
No kernel may reach another device: no remote copies, remote signals or barrier semaphores. Data moves between devices by JAX's collectives and lax.ppermute only.
A program may use at most 64 MiB of HBM per device.

v0:
```python
import jax
import jax.numpy as jnp
from jax import lax
from jax.sharding import PartitionSpec as P

ITERS = 2


def padded(x, sides, width):
    for axis, dim in sides:
        count, length = (lax.axis_size(axis), x.shape[dim])
        up = [(i, (i + 1) % count) for i in range(count - 1)]
        down = [(j, i) for i, j in up]
        last = lax.slice_in_dim(x, length - width, length, axis=dim)
        initial = lax.slice_in_dim(x, 0, width, axis=dim)
        before = lax.ppermute(last, axis, up)
        after = lax.ppermute(initial, axis, down)
        x = jnp.concatenate([before, x, after], axis=dim)
    return x


def shards(start_vectors, left_env, right_env, term_shift, precond, block_dims):
    vec_count, blocks, states, _ = start_vectors.shape
    groups = lax.axis_size("term")
    share = states // groups
    offset_row = lax.axis_index("term") * share
    factor = 1.0 / (blocks * lax.axis_size("sec") * states * states)
    position = jnp.arange(states, dtype=jnp.int32)
    live_rows = position[None, :, None] < block_dims[:, None, None]
    live_cols = position[None, None, :] < block_dims[:, None, None]
    mask = (live_rows & live_cols).astype(jnp.float32)
    shift_sel = term_shift[:, None, None, None, None]

    def apply_op(vector_bf):
        local = jnp.einsum(
            "ujab,kjcb->kujac", vector_bf, right_env, preferred_element_type=jnp.float32
        ).astype(jnp.bfloat16)
        wide = padded(local, (("sec", 2),), 1)
        chosen = jnp.where(
            shift_sel < 0,
            wide[:, :, 0:blocks],
            jnp.where(shift_sel == 0, wide[:, :, 1 : blocks + 1], wide[:, :, 2 : blocks + 2]),
        )
        partial_sum = (
            jnp.einsum("kbac,kubcd->ubad", left_env, chosen, preferred_element_type=jnp.float32)
            * mask
        )
        result = lax.psum(partial_sum, "term")
        return result

    def totals(values):
        result = lax.psum(values, "sec")
        return result

    def inner(left, right):
        return jnp.sum(left * right, axis=(1, 2, 3)) * factor

    def expand(value):
        return value[:, None, None, None]

    start = start_vectors * mask.astype(jnp.bfloat16)
    h_vec = apply_op(start)
    vector = start.astype(jnp.float32)
    pre_view = precond[None]
    length = jnp.sqrt(totals(inner(vector, vector)[None])[0] + 1e-06)
    vector = vector / expand(length)
    h_vec = h_vec / expand(length)
    energy = jnp.zeros((vec_count,), jnp.float32)
    for iteration in range(ITERS):
        rayleigh = totals(inner(vector, h_vec)[None])[0]
        resid = h_vec - expand(rayleigh) * vector
        precon_res = pre_view * resid
        correlation = totals(inner(vector, precon_res)[None])[0]
        direction = precon_res - expand(correlation) * vector
        pair = totals(jnp.stack([inner(direction, direction), inner(direction, h_vec)]))
        square, raw_coupling = (pair[0], pair[1])
        dir_norm = jnp.sqrt(square + 1e-06)
        coupling = raw_coupling / dir_norm
        direction = direction / expand(dir_norm)
        widen_result = direction.astype(jnp.bfloat16)
        h_dir = apply_op(widen_result)
        curvature = totals(inner(direction, h_dir)[None])[0]
        energy = 0.5 * (rayleigh + curvature) - jnp.sqrt(
            (0.5 * (rayleigh - curvature)) ** 2 + coupling**2
        )
        weight = energy - rayleigh
        new_size = jnp.sqrt(coupling**2 + weight**2)
        vector = (expand(coupling) * vector + expand(weight) * direction) / expand(new_size)
        h_vec = (expand(coupling) * h_vec + expand(weight) * h_dir) / expand(new_size)
    final = lax.dynamic_slice_in_dim(vector, offset_row, share, 2)
    return (final, energy)


def solution(mesh):
    return jax.shard_map(
        shards,
        mesh=mesh,
        in_specs=(
            P(None, "sec", None, None),
            P("term", "sec", None, None),
            P("term", "sec", None, None),
            P("term"),
            P("sec", None, None),
            P("sec"),
        ),
        out_specs=(P(None, "sec", "term", None), P()),
        check_vma=False,
    )
```

profile of v0, /device:TPU:1, one launch (start us, length us, event | category | flops | bytes accessed | tf_op | source)
XLA Modules:
  0.0 827.7 jit_solution(5210906045877564215)
XLA Ops:
  10.7 4.6 collective-permute-start
  17.3 9.7 %collective-permute-done = bf16[4,2,1,256,256]{4,3,0,1,2:T(8,128)(2,1)S(1)} collective-permute-done((bf16[4,2,1,256,256]{4,3,0,1,2:T(8,128)(2,1)S(1)}, bf16[4,2,1,256,256]{4,3,0,1,2:T(8,128)(2,1)S(1)}, u32[]{:S(2)}, u32[]{:S(2)}) %collective-permute-start) | collective-permute-done | bytes 1048608 | tf_op jit(solution)/shard_map/ppermute | solution.py:16
  27.1 4.4 collective-permute-done.1
  31.5 2.4 fusion.27
  34.3 61.0 %psum.85 = f32[1,2]{1,0:T(1,128)S(1)} all-reduce(f32[1,2]{1,0:T(1,128)S(1)} %multiply_bitcast_fusion.6), channel_id=1, replica_groups=mesh['term'=8,'sec'=32] {'sec'}, use_global_device_ids=true, to_apply=%region_2.3 | all-reduce | flops 2 | bytes 16 | tf_op jit(solution)/shard_map/psum | solution.py:52
  95.3 14.4 %all-reduce.4.cloned.1.call-done = f32[2,2,256,256]{2,3,0,1:T(8,128)} async-done(((f32[2,2,256,256]{2,3,0,1:T(8,128)}), f32[2,2,256,256]{2,3,0,1:T(8,128)}) %all-reduce.4.cloned.1.call-update) | async-done | bytes 1048592 | tf_op jit(solution)/shard_map/psum | solution.py:48
  112.6 67.1 %psum.86 = f32[2]{0:T(128)S(1)} all-reduce(f32[2]{0:T(128)S(1)} %broadcast_multiply_fusion.5), channel_id=1, replica_groups=mesh['term'=8,'sec'=32] {'sec'}, use_global_device_ids=true, to_apply=%region_4.5 | all-reduce | flops 2 | bytes 16 | tf_op jit(solution)/shard_map/psum | solution.py:52
  180.2 62.7 %psum.87 = f32[2]{0:T(128)S(1)} all-reduce(f32[2]{0:T(128)S(1)} %broadcast_multiply_fusion.4), channel_id=1, replica_groups=mesh['term'=8,'sec'=32] {'sec'}, use_global_device_ids=true, to_apply=%region_6.7 | all-reduce | flops 2 | bytes 16 | tf_op jit(solution)/shard_map/psum | solution.py:52
  244.5 62.7 %psum.88 = f32[2,2]{1,0:T(2,128)S(1)} all-reduce(f32[2,2]{1,0:T(2,128)S(1)} %pad_maximum_fusion.9), channel_id=1, replica_groups=mesh['term'=8,'sec'=32] {'sec'}, use_global_device_ids=true, to_apply=%region_9.10 | all-reduce | flops 4 | bytes 32 | tf_op jit(solution)/shard_map/psum | solution.py:52
  311.6 2.5 collective-permute-start.3
  314.0 9.2 %collective-permute-done.2 = bf16[4,2,1,256,256]{4,3,0,1,2:T(8,128)(2,1)S(1)} collective-permute-done((bf16[4,2,1,256,256]{4,3,0,1,2:T(8,128)(2,1)S(1)}, bf16[4,2,1,256,256]{4,3,0,1,2:T(8,128)(2,1)S(1)}, u32[]{:S(2)}, u32[]{:S(2)}) %collective-permute-start.2) | collective-permute-done | bytes 1048608 | tf_op jit(solution)/shard_map/ppermute | solution.py:16
  323.3 4.4 collective-permute-done.3
  330.1 65.6 %all-reduce.6.cloned.1.call-done = f32[2,2,256,256]{2,3,0,1:T(8,128)} async-done(((f32[2,2,256,256]{2,3,0,1:T(8,128)}), f32[2,2,256,256]{2,3,0,1:T(8,128)}) %all-reduce.6.cloned.1.call-update) | async-done | bytes 1048592 | tf_op jit(solution)/shard_map/psum | solution.py:48
  397.7 67.1 %psum.90 = f32[2]{0:T(128)S(1)} all-reduce(f32[2]{0:T(128)S(1)} %broadcast_multiply_fusion.3), channel_id=1, replica_groups=mesh['term'=8,'sec'=32] {'sec'}, use_global_device_ids=true, to_apply=%region_12.13 | all-reduce | flops 2 | bytes 16 | tf_op jit(solution)/shard_map/psum | solution.py:52
  464.8 3.5 multiply_reduce_fusion.4
  468.3 62.8 %psum.91 = f32[2]{0:T(128)S(1)} all-reduce(f32[2]{0:T(128)S(1)} %broadcast_multiply_fusion.2), channel_id=1, replica_groups=mesh['term'=8,'sec'=32] {'sec'}, use_global_device_ids=true, to_apply=%region_14.15 | all-reduce | flops 2 | bytes 16 | tf_op jit(solution)/shard_map/psum | solution.py:52
  533.0 62.7 %psum.92 = f32[2]{0:T(128)S(1)} all-reduce(f32[2]{0:T(128)S(1)} %broadcast_multiply_fusion.1), channel_id=1, replica_groups=mesh['term'=8,'sec'=32] {'sec'}, use_global_device_ids=true, to_apply=%region_16.17 | all-reduce | flops 2 | bytes 16 | tf_op jit(solution)/shard_map/psum | solution.py:52
  595.6 2.6 multiply_reduce_fusion.2
  598.2 62.7 %psum.93 = f32[2,2]{1,0:T(2,128)S(1)} all-reduce(f32[2,2]{1,0:T(2,128)S(1)} %pad_maximum_fusion.10), channel_id=1, replica_groups=mesh['term'=8,'sec'=32] {'sec'}, use_global_device_ids=true, to_apply=%region_19.20 | all-reduce | flops 4 | bytes 32 | tf_op jit(solution)/shard_map/psum | solution.py:52
  665.6 2.5 collective-permute-start.5
  668.1 9.2 %collective-permute-done.4 = bf16[4,2,1,256,256]{4,3,0,1,2:T(8,128)(2,1)S(1)} collective-permute-done((bf16[4,2,1,256,256]{4,3,0,1,2:T(8,128)(2,1)S(1)}, bf16[4,2,1,256,256]{4,3,0,1,2:T(8,128)(2,1)S(1)}, u32[]{:S(2)}, u32[]{:S(2)}) %collective-permute-start.4) | collective-permute-done | bytes 1048608 | tf_op jit(solution)/shard_map/ppermute | solution.py:16
  677.3 4.4 collective-permute-done.5
  684.1 65.3 %all-reduce.8.cloned.1.call-done = f32[2,2,256,256]{2,3,0,1:T(8,128)} async-done(((f32[2,2,256,256]{2,3,0,1:T(8,128)}), f32[2,2,256,256]{2,3,0,1:T(8,128)}) %all-reduce.8.cloned.1.call-update) | async-done | bytes 1048592 | tf_op jit(solution)/shard_map/psum | solution.py:48
  751.3 67.1 %psum.95 = f32[2]{0:T(128)S(1)} all-reduce(f32[2]{0:T(128)S(1)} %broadcast_multiply_fusion), channel_id=1, replica_groups=mesh['term'=8,'sec'=32] {'sec'}, use_global_device_ids=true, to_apply=%region_22.23 | all-reduce | flops 2 | bytes 16 | tf_op jit(solution)/shard_map/psum | solution.py:52
  (71 shorter events, 33.1 us)
Async XLA Ops:
  7.2 2.5 copy-start
  7.2 102.5 %all-reduce.4.cloned.1.call-start = ((), (), s32[]{:S(2)}) async-start(), calls=%async_computation | async-start | bytes 2097152 | tf_op jit(solution)/shard_map/psum | solution.py:48
  8.2 23.3 %copy-start.4 = (f32[2,256,256]{1,2,0:T(8,128)}, f32[2,256,256]{1,2,0:T(8,128)S(1)}, u32[]{:S(2)}) copy-start(f32[2,256,256]{1,2,0:T(8,128)S(1)} %get-tuple-element.26) | copy-start | bytes 1572868
  10.5 6.8 copy-start.10
  10.5 21.0 %copy-start.7 = (bf16[4,2,256,256]{3,2,1,0:T(8,128)(2,1)S(1)}, bf16[4,2,256,256]{3,2,1,0:T(8,128)(2,1)}, u32[]{:S(2)}) copy-start(bf16[4,2,256,256]{3,2,1,0:T(8,128)(2,1)} %param.7) | copy-start | bytes 3145732
  10.7 16.4 %collective-permute-start = (bf16[4,2,1,256,256]{4,3,0,1,2:T(8,128)(2,1)S(1)}, bf16[4,2,1,256,256]{4,3,0,1,2:T(8,128)(2,1)S(1)}, u32[]{:S(2)}, u32[]{:S(2)}) collective-permute-start(bf16[4,2,1,256,256]{4,3,0,1,2:T(8,128)(2,1)S(1)} %get-tuple-element.24), channel_id=1, source_target_pairs={{0,1},{1,2},{2,3},{3,4},{4,5},{5,6},{6,7},{7,8},{8,9},{9,10},{10,1... | collective-permute-start | bytes 3145736 | tf_op jit(solution)/shard_map/ppermute | solution.py:16
  15.3 16.1 %collective-permute-start.1 = (bf16[4,2,1,256,256]{4,3,0,1,2:T(8,128)(2,1)S(1)}, bf16[4,2,1,256,256]{4,3,0,1,2:T(8,128)(2,1)S(1)}, u32[]{:S(2)}, u32[]{:S(2)}) collective-permute-start(bf16[4,2,1,256,256]{4,3,0,1,2:T(8,128)(2,1)S(1)} %get-tuple-element.25), channel_id=1, source_target_pairs={{1,0},{2,1},{3,2},{4,3},{5,4},{6,5},{7,6},{8,7},{9,8},{10,9},{11,1... | collective-permute-start | bytes 3145736 | tf_op jit(solution)/shard_map/ppermute | solution.py:17
  33.9 361.9 %all-reduce.6.cloned.1.call-start = ((), (), s32[]{:S(2)}) async-start(), calls=%async_computation.1 | async-start | bytes 2097152 | tf_op jit(solution)/shard_map/psum | solution.py:48
  109.7 70.1 %copy-start.1 = (f32[2,2,256,256]{2,3,0,1:T(8,128)S(1)}, f32[2,2,256,256]{2,3,0,1:T(8,128)}, u32[]{:S(2)}) copy-start(f32[2,2,256,256]{2,3,0,1:T(8,128)} %all-reduce.4.cloned.1.call-done) | copy-start | bytes 3145732
  309.3 18.4 %copy-start.5 = (f32[2,256,256]{1,2,0:T(8,128)S(1)}, f32[2,256,256]{1,2,0:T(8,128)}, u32[]{:S(2)}) copy-start(f32[2,256,256]{1,2,0:T(8,128)} %copy-done.4) | copy-start | bytes 1572868
  309.3 18.4 %copy-start.8 = (bf16[4,2,256,256]{3,2,1,0:T(8,128)(2,1)S(1)}, bf16[4,2,256,256]{3,2,1,0:T(8,128)(2,1)}, u32[]{:S(2)}) copy-start(bf16[4,2,256,256]{3,2,1,0:T(8,128)(2,1)} %param.7) | copy-start | bytes 3145732
  309.5 13.8 %collective-permute-start.2 = (bf16[4,2,1,256,256]{4,3,0,1,2:T(8,128)(2,1)S(1)}, bf16[4,2,1,256,256]{4,3,0,1,2:T(8,128)(2,1)S(1)}, u32[]{:S(2)}, u32[]{:S(2)}) collective-permute-start(bf16[4,2,1,256,256]{4,3,0,1,2:T(8,128)(2,1)S(1)} %get-tuple-element.22), channel_id=1, source_target_pairs={{0,1},{1,2},{2,3},{3,4},{4,5},{5,6},{6,7},{7,8},{8,9},{9,10},{10,1... | collective-permute-start | bytes 3145736 | tf_op jit(solution)/shard_map/ppermute | solution.py:16
  311.6 16.1 %collective-permute-start.3 = (bf16[4,2,1,256,256]{4,3,0,1,2:T(8,128)(2,1)S(1)}, bf16[4,2,1,256,256]{4,3,0,1,2:T(8,128)(2,1)S(1)}, u32[]{:S(2)}, u32[]{:S(2)}) collective-permute-start(bf16[4,2,1,256,256]{4,3,0,1,2:T(8,128)(2,1)S(1)} %get-tuple-element.23), channel_id=1, source_target_pairs={{1,0},{2,1},{3,2},{4,3},{5,4},{6,5},{7,6},{8,7},{9,8},{10,9},{11,1... | collective-permute-start | bytes 3145736 | tf_op jit(solution)/shard_map/ppermute | solution.py:17
  330.1 419.3 %all-reduce.8.cloned.1.call-start = ((), (), s32[]{:S(2)}) async-start(), calls=%async_computation.2 | async-start | bytes 2097152 | tf_op jit(solution)/shard_map/psum | solution.py:48
  468.3 127.4 %copy-start.2 = (f32[2,2,256,256]{2,3,0,1:T(8,128)S(1)}, f32[2,2,256,256]{2,3,0,1:T(8,128)}, u32[]{:S(2)}) copy-start(f32[2,2,256,256]{2,3,0,1:T(8,128)} %get-tuple-element.15) | copy-start | bytes 3145732
  662.3 1.0 copy-start.3
  663.4 18.4 %copy-start.6 = (f32[2,256,256]{1,2,0:T(8,128)S(1)}, f32[2,256,256]{1,2,0:T(8,128)}, u32[]{:S(2)}) copy-start(f32[2,256,256]{1,2,0:T(8,128)} %copy-done.4) | copy-start | bytes 1572868
  663.4 18.4 %copy-start.9 = (bf16[4,2,256,256]{3,2,1,0:T(8,128)(2,1)S(1)}, bf16[4,2,256,256]{3,2,1,0:T(8,128)(2,1)}, u32[]{:S(2)}) copy-start(bf16[4,2,256,256]{3,2,1,0:T(8,128)(2,1)} %param.7) | copy-start | bytes 3145732
  663.5 13.8 %collective-permute-start.4 = (bf16[4,2,1,256,256]{4,3,0,1,2:T(8,128)(2,1)S(1)}, bf16[4,2,1,256,256]{4,3,0,1,2:T(8,128)(2,1)S(1)}, u32[]{:S(2)}, u32[]{:S(2)}) collective-permute-start(bf16[4,2,1,256,256]{4,3,0,1,2:T(8,128)(2,1)S(1)} %get-tuple-element.20), channel_id=1, source_target_pairs={{0,1},{1,2},{2,3},{3,4},{4,5},{5,6},{6,7},{7,8},{8,9},{9,10},{10,1... | collective-permute-start | bytes 3145736 | tf_op jit(solution)/shard_map/ppermute | solution.py:16
  665.6 16.1 %collective-permute-start.5 = (bf16[4,2,1,256,256]{4,3,0,1,2:T(8,128)(2,1)S(1)}, bf16[4,2,1,256,256]{4,3,0,1,2:T(8,128)(2,1)S(1)}, u32[]{:S(2)}, u32[]{:S(2)}) collective-permute-start(bf16[4,2,1,256,256]{4,3,0,1,2:T(8,128)(2,1)S(1)} %get-tuple-element.21), channel_id=1, source_target_pairs={{1,0},{2,1},{3,2},{4,3},{5,4},{6,5},{7,6},{8,7},{9,8},{10,9},{11,1... | collective-permute-start | bytes 3145736 | tf_op jit(solution)/shard_map/ppermute | solution.py:17
Sparse Core Ops, SparseCore 0:
  34.0 75.5 all-reduce.3
  330.2 65.5 all-reduce.5
  684.2 65.1 all-reduce.7
where the time goes:
time: 829 us; the launch traced here: 828 us
  blocking collectives  576 us (69%)
  waiting for transfers between devices  187 us (23%)
  other arithmetic  20.1 us (2%)
  starting transfers between devices  15.8 us (2%)
  between operations  14 us (2%)
  matrix products  11 us (1%)
    psum x9, blocking collectives, totals(): result = lax.psum(values, 'sec')  576 us
    psum x3, waiting for transfers between devices, apply_op(): result = lax.psum(partial_sum, 'term')  145 us
    ppermute x3, waiting for transfers between devices, padded(): before = lax.ppermute(last, axis, up)  28.2 us
  transfers between devices with their start and end apart: 9, of which 9 were waited for; matrix products, arithmetic and copies ran while one was open for 0% of the time, Pallas kernels for 0%

commit v1 on v0

v1 whole, which is shorter than its diff:
```python
import jax
import jax.numpy as jnp
from jax import lax
from jax.experimental import pallas as pl
from jax.experimental.pallas import tpu as pltpu
from jax.sharding import PartitionSpec as P

BF = jnp.bfloat16
F32 = jnp.float32


def apply_kernel(slot_ref, x_ref, right_ref, left_ref, out_ref):
    vecs, _, states, _ = x_ref.shape
    terms, blocks = left_ref.shape[:2]
    groups, share = out_ref.shape[0], out_ref.shape[3]
    for b in range(blocks):
        acc = jnp.zeros((states, vecs * states), F32)
        for k in range(terms):
            slot = slot_ref[k, b]
            x = x_ref[:, slot].reshape(vecs * states, states)
            z = lax.dot_general(
                x, right_ref[k, slot], (((1,), (1,)), ((), ())), preferred_element_type=F32
            ).astype(BF)
            wide = jnp.concatenate([z[u * states : (u + 1) * states] for u in range(vecs)], axis=1)
            acc = acc + jnp.dot(left_ref[k, b], wide, preferred_element_type=F32)
        for u in range(vecs):
            part = acc[:, u * states : (u + 1) * states]
            out_ref[:, u, b] = part.reshape(groups, share, states).astype(out_ref.dtype)


def shards(start_vectors, left_env, right_env, term_shift, precond, block_dims):
    vecs, blocks, states, _ = start_vectors.shape
    groups = lax.axis_size("term")
    sec = lax.axis_size("sec")
    share = states // groups
    core = lax.axis_index("sec") % 2
    term = lax.axis_index("term")
    factor = 1.0 / (blocks * sec * states * states)
    position = jnp.arange(states, dtype=jnp.int32)
    live_rows = position[None, :, None] < block_dims[:, None, None]
    live_cols = position[None, None, :] < block_dims[:, None, None]
    mask = (live_rows & live_cols).astype(F32)

    core_pairs = [(i, i ^ 1) for i in range(sec)]
    chip_pairs = [(i, i + 1) for i in range(1, sec - 1, 2)]
    chip_pairs = chip_pairs + [(j, i) for i, j in chip_pairs]
    same_core = [[2 * c + k for c in range(sec // 2)] for k in range(2)]

    def edges(x, axis):
        inner = lax.dynamic_index_in_dim(x, 1 - core, axis, keepdims=True)
        outer = lax.dynamic_index_in_dim(x, core, axis, keepdims=True)
        return lax.ppermute(inner, "sec", core_pairs), lax.ppermute(outer, "sec", chip_pairs)

    def with_edges(x, axis):
        return jnp.concatenate([x, *edges(x, axis)], axis=axis)

    def rows(x, axis):
        return lax.dynamic_slice_in_dim(x, term * share, share, axis)

    at = jnp.arange(blocks, dtype=jnp.int32)[None, :] + term_shift[:, None]
    slot = jnp.where(at < 0, 3 - core, jnp.where(at > 1, 2 + core, at)).astype(jnp.int32)

    apply_op = pl.pallas_call(
        apply_kernel,
        out_shape=jax.ShapeDtypeStruct((groups, vecs, blocks, share, states), BF),
        in_specs=[pl.BlockSpec(memory_space=pltpu.SMEM)]
        + [pl.BlockSpec(memory_space=pltpu.VMEM)] * 3,
        out_specs=pl.BlockSpec(memory_space=pltpu.VMEM),
        cost_estimate=pl.CostEstimate(
            flops=8 * vecs * blocks * states**3 * 2, bytes_accessed=5 << 20, transcendentals=0
        ),
    )

    def scatter_sum(parts):
        got = lax.all_to_all(parts, "term", 0, 0)
        return jnp.sum(got.astype(F32), axis=0) * mask_rows

    def pieces(values):
        high = lax.reduce_precision(values, 8, 7)
        rest = values - high
        middle = lax.reduce_precision(rest, 8, 7)
        low = lax.reduce_precision(rest - middle, 8, 7)
        return jnp.concatenate([high, middle, low])

    def gather(part, scalars):
        count = scalars.size
        packed = jnp.pad(pieces(scalars.reshape(-1)), (0, 16 * states - 3 * count))
        body = jnp.concatenate(
            [part.reshape(-1, states).astype(BF), packed.reshape(16, states).astype(BF)]
        )
        got = lax.all_to_all(jnp.broadcast_to(body[None], (groups,) + body.shape), "term", 0, 0)
        main = got[:, :-16].reshape(groups, vecs, blocks, share, states)
        main = main.transpose(1, 2, 0, 3, 4).reshape(vecs, blocks, states, states)
        small = got[:, -16:].reshape(groups, 16 * states)[:, : 3 * count].astype(F32)
        small = jnp.sum(small.reshape(groups, 3, count), axis=(0, 1))
        return main, small

    def sum_sec(values):
        count = values.size
        row = jnp.pad(values, (0, 128 - count))[None]
        row = row + lax.ppermute(row, "sec", core_pairs)
        got = lax.all_to_all(
            jnp.broadcast_to(row[None], (sec // 2,) + row.shape),
            "sec",
            0,
            0,
            axis_index_groups=same_core,
        )
        return jnp.sum(got, axis=0)[0, :count]

    def dots(left, right):
        return jnp.sum(left * right, axis=(1, 2, 3)) * factor

    def expand(value):
        return value[:, None, None, None]

    start = start_vectors * mask.astype(BF)
    right_all = with_edges(right_env, 1)
    start_all = with_edges(start, 1)
    pre_all = with_edges(precond, 0)
    mask_rows = rows(mask, 1)
    pre = rows(precond, 1)[None]
    vec = rows(start, 2).astype(F32)

    h_raw = scatter_sum(apply_op(slot, start_all, right_all, left_env))
    mv, mh = pre * vec, pre * h_raw
    gram = jnp.stack(
        [
            dots(vec, vec),
            dots(vec, h_raw),
            dots(vec, mv),
            dots(vec, mh),
            dots(h_raw, mh),
            dots(mv, mv),
            dots(mv, mh),
            dots(mh, mh),
        ]
    )
    h_all, small = gather(h_raw, gram)
    h_all = with_edges(h_all, 1)
    total = sum_sec(small).reshape(8, vecs)
    scale = 1.0 / jnp.sqrt(total[0] + 1e-06)
    vv, vh, vmv, vmh, hmh, mvmv, mvmh, mhmh = total * scale**2
    correlation = vmh - vh * vmv
    square = (
        mhmh
        - 2.0 * vh * mvmh
        + vh**2 * mvmv
        - 2.0 * correlation * (vmh - vh * vmv)
        + correlation**2 * vv
    )
    dir_norm = jnp.sqrt(jnp.maximum(square, 0.0) + 1e-06)
    coupling = (hmh - vh * vmh - correlation * vh) / dir_norm
    rayleigh = vh

    def direct(v, h, m):
        raw = m * (h - expand(rayleigh) * v) - expand(correlation) * v
        return raw * expand(scale / dir_norm)

    dir_all = direct(start_all.astype(F32), h_all.astype(F32), pre_all[None])
    direction = direct(vec, h_raw, pre)
    vec = vec * expand(scale)
    h_vec = h_raw * expand(scale)
    h_dir = scatter_sum(apply_op(slot, dir_all.astype(BF), right_all, left_env))

    basis = [vec, direction, h_vec, h_dir]
    weighted = [pre * x for x in basis]
    pairs = [(i, j) for i in range(4) for j in range(i, 4)]
    plain = [(0, 0), (0, 1), (1, 1), (0, 2), (0, 3), (1, 2), (1, 3)]
    gram = jnp.stack(
        [dots(basis[i], basis[j]) for i, j in plain]
        + [dots(basis[i], weighted[j]) for i, j in pairs]
        + [dots(weighted[i], weighted[j]) for i, j in pairs]
    )
    hd_all, small = gather(h_dir, gram)
    hd_all = with_edges(hd_all, 1)
    total = sum_sec(small).reshape(-1, vecs)
    one = {p: total[i] for i, p in enumerate(plain)}
    first = {p: total[len(plain) + i] for i, p in enumerate(pairs)}
    second = {p: total[len(plain) + len(pairs) + i] for i, p in enumerate(pairs)}

    def form(table, left, right):
        result = 0.0
        for i, x in left:
            for j, y in right:
                result = result + x * y * table[(min(i, j), max(i, j))]
        return result

    curvature = one[(1, 3)]
    energy = 0.5 * (rayleigh + curvature) - jnp.sqrt(
        (0.5 * (rayleigh - curvature)) ** 2 + coupling**2
    )
    weight = energy - rayleigh
    size = jnp.sqrt(coupling**2 + weight**2)
    keep, mix = coupling / size, weight / size
    v_of, h_of = [(0, keep), (1, mix)], [(2, keep), (3, mix)]
    rayleigh = form(one, v_of, h_of)
    resid_of = h_of + [(i, -rayleigh * x) for i, x in v_of]
    correlation = form(first, v_of, resid_of)
    square = (
        form(second, resid_of, resid_of)
        - 2.0 * correlation * form(first, v_of, resid_of)
        + correlation**2 * form(one, v_of, v_of)
    )
    dir_norm = jnp.sqrt(jnp.maximum(square, 0.0) + 1e-06)
    coupling = (form(first, resid_of, h_of) - correlation * rayleigh) / dir_norm

    def advance(v, d, h, hd, m):
        new_v = expand(keep) * v + expand(mix) * d
        new_h = expand(keep) * h + expand(mix) * hd
        raw = m * (new_h - expand(rayleigh) * new_v) - expand(correlation) * new_v
        return new_v, raw / expand(dir_norm)

    _, dir_all = advance(
        start_all.astype(F32) * expand(scale),
        dir_all,
        h_all.astype(F32) * expand(scale),
        hd_all.astype(F32),
        pre_all[None],
    )
    vec, direction = advance(vec, direction, h_vec, h_dir, pre)
    parts = apply_op(slot, dir_all.astype(BF), right_all, left_env)
    own = dir_all[:, :blocks].reshape(vecs, blocks, groups, share, states).transpose(2, 0, 1, 3, 4)
    curvature = jnp.sum(parts.astype(F32) * own, axis=(0, 2, 3, 4)) * factor
    row = jnp.pad(curvature, (0, 128 - vecs))[None]
    everyone = groups * sec
    got = lax.all_to_all(
        jnp.broadcast_to(row[None], (everyone,) + row.shape), ("term", "sec"), 0, 0
    )
    curvature = jnp.sum(got, axis=0)[0, :vecs]
    energy = 0.5 * (rayleigh + curvature) - jnp.sqrt(
        (0.5 * (rayleigh - curvature)) ** 2 + coupling**2
    )
    weight = energy - rayleigh
    size = jnp.sqrt(coupling**2 + weight**2)
    final = (expand(coupling) * vec + expand(weight) * direction) / expand(size)
    return (final, energy)


def solution(mesh):
    return jax.shard_map(
        shards,
        mesh=mesh,
        in_specs=(
            P(None, "sec", None, None),
            P("term", "sec", None, None),
            P("term", "sec", None, None),
            P("term"),
            P("sec", None, None),
            P("sec"),
        ),
        out_specs=(P(None, "sec", "term", None), P()),
        check_vma=False,
    )
```

time: 829 us -> 201 us (0.24)
  blocking collectives: 576 us -> 65.2 us
  waiting for transfers between devices: 187 us -> 27.5 us
  starting transfers between devices: 15.8 us -> 65 us
  Pallas kernels: 0 us -> 15.6 us
  between operations: 14 us -> 1.48 us
  matrix products: 11 us -> 0 us
    psum x9 -> x0, blocking collectives: 576 us -> none  [totals(): result = lax.psum(values, 'sec')]
    psum x3 -> x0, waiting for transfers between devices: 145 us -> none  [apply_op(): result = lax.psum(partial_sum, 'term')]
    all_to_all x0 -> x3, blocking collectives: none -> 65.2 us  [the longest x1 22.5 us: shards(): lax.all_to_all(jnp.broadcast_to(row[None], (everyone,) + row.shape), ('te...]
    all_to_all x0 -> x4, starting transfers between devices: none -> 37.3 us  [the longest x2 26.6 us: sum_sec(): lax.all_to_all(jnp.broadcast_to(row[None], (sec // 2,) + row.shape), 'sec...]
    ppermute x6 -> x12, waiting for transfers between devices: 41.4 us -> 10.8 us  [the longest x5 10.1 us: edges(): lax.ppermute(outer, 'sec', chip_pairs)]
    all_to_all x0 -> x4, waiting for transfers between devices: none -> 16.7 us  [the longest x1 11.3 us: scatter_sum(): got = lax.all_to_all(parts, 'term', 0, 0)]
    pallas_call x0 -> x3, Pallas kernels: none -> 15.6 us  [the longest x1 5.27 us: shards(): parts = apply_op(slot, dir_all.astype(BF), right_all, left_env)]
    reduce_sum x9 -> x12, other arithmetic: 15.7 us -> 1.94 us  [the longest x2 1.32 us: dots(): return jnp.sum(left * right, axis=(1, 2, 3)) * factor]
  transfers between devices with their start and end apart: 9 -> 16, of which waited for: 9 -> 10; matrix products, arithmetic and copies ran while one was open for 0% -> 5% of each run, Pallas kernels for 0% -> 0%
where the time goes in v1:
time: 201 us; the launch traced here: 200 us
  blocking collectives  65.2 us (32%)
  starting transfers between devices  65 us (32%)
  waiting for transfers between devices  27.5 us (14%)
  Pallas kernels  15.6 us (8%)
  other arithmetic  15.5 us (8%)
  local copies, waits for them, and re-layouts  10.2 us (5%)
    all_to_all x2, starting transfers between devices, sum_sec(): lax.all_to_all(jnp.broadcast_to(row[None], (sec // 2,) + row.shape), 'sec...  26.6 us
    all_to_all x1, blocking collectives, shards(): lax.all_to_all(jnp.broadcast_to(row[None], (everyone,) + row.shape), ('te...  22.5 us
    ppermute x5, starting transfers between devices, edges(): lax.ppermute(outer, 'sec', chip_pairs)  22 us
    all_to_all x1, blocking collectives, scatter_sum(): got = lax.all_to_all(parts, 'term', 0, 0)  21.6 us
    all_to_all x1, blocking collectives, gather(): lax.all_to_all(jnp.broadcast_to(body[None], (groups,) + body.shape), 'ter...  21.1 us
    all_to_all x1, waiting for transfers between devices, scatter_sum(): got = lax.all_to_all(parts, 'term', 0, 0)  11.3 us
    ppermute x5, waiting for transfers between devices, edges(): lax.ppermute(outer, 'sec', chip_pairs)  10.1 us
    all_to_all x1, starting transfers between devices, scatter_sum(): got = lax.all_to_all(parts, 'term', 0, 0)  7.17 us
  transfers between devices with their start and end apart: 16, of which 10 were waited for; matrix products, arithmetic and copies ran while one was open for 5% of the time, Pallas kernels for 0%

profile of v1, /device:TPU:1, one launch (start us, length us, event | category | flops | bytes accessed | tf_op | source)
XLA Modules:
  0.0 200.4 jit_solution(4900239155389930578)
XLA Ops:
  2.0 3.3 %collective-permute-start.2 = (bf16[4,1,256,256]{3,2,1,0:T(8,128)(2,1)S(1)}, bf16[4,1,256,256]{3,2,1,0:T(8,128)(2,1)S(1)}, u32[]{:S(2)}, u32[]{:S(2)}) collective-permute-start(bf16[4,1,256,256]{3,2,1,0:T(8,128)(2,1)S(1)} %get-tuple-element.74), channel_id=1, source_target_pairs={{0,1},{1,0},{2,3},{3,2},{4,5},{5,4},{6,7},{7,6},{8,9},{9,8},{10,11... | collective-permute-start | bytes 1572872 | tf_op jit(solution)/shard_map/ppermute | solution.py:52
  6.5 1.9 collective-permute-start.1
  8.4 3.6 %collective-permute-start.3 = (bf16[4,1,256,256]{3,2,1,0:T(8,128)(2,1)S(1)}, bf16[4,1,256,256]{3,2,1,0:T(8,128)(2,1)S(1)}, u32[]{:S(2)}, u32[]{:S(2)}) collective-permute-start(bf16[4,1,256,256]{3,2,1,0:T(8,128)(2,1)S(1)} %get-tuple-element.73), channel_id=1, source_target_pairs={{1,2},{3,4},{5,6},{7,8},{9,10},{11,12},{13,14},{15,16},{17,18},{19... | collective-permute-start | bytes 1572872 | tf_op jit(solution)/shard_map/ppermute | solution.py:52
  15.4 4.5 %collective-permute-done.3 = bf16[4,1,256,256]{3,2,1,0:T(8,128)(2,1)S(1)} collective-permute-done((bf16[4,1,256,256]{3,2,1,0:T(8,128)(2,1)S(1)}, bf16[4,1,256,256]{3,2,1,0:T(8,128)(2,1)S(1)}, u32[]{:S(2)}, u32[]{:S(2)}) %collective-permute-start.3) | collective-permute-done | bytes 524320 | tf_op jit(solution)/shard_map/ppermute | solution.py:52
  21.2 5.2 %shard_map.77 = bf16[8,2,2,32,256]{4,3,2,1,0:T(8,128)(2,1)} custom-call(s32[4,2]{1,0:T(4,128)} %fusion.77.slot_ref, bf16[2,4,256,256]{3,2,1,0:T(8,128)(2,1)} %pad_maximum_fusion.x_ref, bf16[4,4,256,256]{3,2,1,0:T(8,128)(2,1)} %copy-done, bf16[4,2,256,256]{3,2,1,0:T(8,128)(2,1)} %left_ref.5), custom_call_target="tpu_custom_call" | custom-call | flops 1073741824 | bytes 5242880 | tf_op jit(solution)/shard_map/pallas_call | solution.py:125
  26.4 7.2 %all-to-all-start = ((bf16[8,2,2,32,256]{4,3,2,1,0:T(8,128)(2,1)}), bf16[8,2,2,32,256]{4,3,2,1,0:T(8,128)(2,1)S(1)}, u32[]{:S(2)}, u32[]{:S(2)}) async-start(bf16[8,2,2,32,256]{4,3,2,1,0:T(8,128)(2,1)} %shard_map.77), calls=%async_computation | async-start | bytes 1048576 | tf_op jit(solution)/shard_map/all_to_all | solution.py:75
  34.5 11.3 %all-to-all-done = bf16[8,2,2,32,256]{4,3,2,1,0:T(8,128)(2,1)S(1)} async-done(((bf16[8,2,2,32,256]{4,3,2,1,0:T(8,128)(2,1)}), bf16[8,2,2,32,256]{4,3,2,1,0:T(8,128)(2,1)S(1)}, u32[]{:S(2)}, u32[]{:S(2)}) %all-to-all-start) | async-done | bytes 524320 | tf_op jit(solution)/shard_map/all_to_all | solution.py:75
  47.2 3.5 %all-to-all-start.1 = ((bf16[8,144,256]{2,1,0:T(8,128)(2,1)}), bf16[8,144,256]{2,1,0:T(8,128)(2,1)S(1)}, u32[]{:S(2)}, u32[]{:S(2)}) async-start(bf16[8,144,256]{2,1,0:T(8,128)(2,1)} %broadcast_in_dim.27), calls=%async_computation.1 | async-start | bytes 1179648 | tf_op jit(solution)/shard_map/all_to_all | solution.py:91
  50.9 9.4 %collective-permute-start.6 = (f32[1,256,256]{2,1,0:T(8,128)S(1)}, f32[1,256,256]{2,1,0:T(8,128)}, u32[]{:S(2)}, u32[]{:S(2)}) collective-permute-start(f32[1,256,256]{2,1,0:T(8,128)S(1)} %get-tuple-element.80), channel_id=1, source_target_pairs={{1,2},{3,4},{5,6},{7,8},{9,10},{11,12},{13,14},{15,16},{17,18},{19... | collective-permute-start | bytes 786440 | tf_op jit(solution)/shard_map/ppermute | solution.py:52
  60.3 2.5 %all-to-all-done.1 = bf16[8,144,256]{2,1,0:T(8,128)(2,1)S(1)} async-done(((bf16[8,144,256]{2,1,0:T(8,128)(2,1)}), bf16[8,144,256]{2,1,0:T(8,128)(2,1)S(1)}, u32[]{:S(2)}, u32[]{:S(2)}) %all-to-all-start.1) | async-done | bytes 589856 | tf_op jit(solution)/shard_map/all_to_all | solution.py:91
  66.3 19.7 %all-to-all-start.2 = ((f32[16,1,128]{2,1,0:T(1,128)}), f32[16,1,128]{2,1,0:T(1,128)S(1)}, u32[]{:S(2)}, u32[]{:S(2)}) async-start(f32[16,1,128]{2,1,0:T(1,128)} %broadcast_in_dim.30), calls=%async_computation.2 | async-start | bytes 16384 | tf_op jit(solution)/shard_map/all_to_all | solution.py:102
  87.2 3.4 %collective-permute-start.8 = (bf16[2,1,256,256]{3,2,1,0:T(8,128)(2,1)}, bf16[2,1,256,256]{3,2,1,0:T(8,128)(2,1)S(1)}, u32[]{:S(2)}, u32[]{:S(2)}) collective-permute-start(bf16[2,1,256,256]{3,2,1,0:T(8,128)(2,1)} %get-tuple-element.78), channel_id=1, source_target_pairs={{1,2},{3,4},{5,6},{7,8},{9,10},{11,12},{13,14},{15,16},{17,18},{19... | collective-permute-start | bytes 786440 | tf_op jit(solution)/shard_map/ppermute | solution.py:52
  90.6 1.8 all-to-all-done.2
  93.1 1.9 collective-permute-done.8
  95.1 1.7 fusion.11.x_ref
  96.7 5.1 %shard_map.78 = bf16[8,2,2,32,256]{4,3,2,1,0:T(8,128)(2,1)} custom-call(s32[4,2]{1,0:T(4,128)} %fusion.77.slot_ref, bf16[2,4,256,256]{3,2,1,0:T(8,128)(2,1)} %fusion.11.x_ref, bf16[4,4,256,256]{3,2,1,0:T(8,128)(2,1)} %copy-done, bf16[4,2,256,256]{3,2,1,0:T(8,128)(2,1)} %left_ref.5), custom_call_target="tpu_custom_call" | custom-call | flops 1073741824 | bytes 5242880 | tf_op jit(solution)/shard_map/pallas_call | solution.py:164
  101.8 21.6 %all_to_all.35 = bf16[8,2,2,32,256]{4,3,2,1,0:T(8,128)(2,1)S(1)} all-to-all(bf16[8,2,2,32,256]{4,3,2,1,0:T(8,128)(2,1)} %shard_map.78), channel_id=1, replica_groups=mesh['term'=8,'sec'=32] {'term'}, dimensions={0} | all-to-all | bytes 1048576 | tf_op jit(solution)/shard_map/all_to_all | solution.py:75
  125.3 21.1 %all_to_all.36 = bf16[8,144,256]{2,1,0:T(8,128)(2,1)S(1)} all-to-all(bf16[8,144,256]{2,1,0:T(8,128)(2,1)S(1)} %broadcast_in_dim.31), channel_id=1, replica_groups=mesh['term'=8,'sec'=32] {'term'}, dimensions={0} | all-to-all | bytes 1179648 | tf_op jit(solution)/shard_map/all_to_all | solution.py:91
  149.2 6.9 %all-to-all-start.5 = ((f32[16,1,128]{2,1,0:T(1,128)}), f32[16,1,128]{2,1,0:T(1,128)S(1)}, u32[]{:S(2)}, u32[]{:S(2)}) async-start(f32[16,1,128]{2,1,0:T(1,128)} %broadcast_in_dim.34), calls=%async_computation.5 | async-start | bytes 16384 | tf_op jit(solution)/shard_map/all_to_all | solution.py:102
  157.6 3.6 %collective-permute-start.11 = (bf16[2,1,256,256]{3,2,1,0:T(8,128)(2,1)}, bf16[2,1,256,256]{3,2,1,0:T(8,128)(2,1)}, u32[]{:S(2)}, u32[]{:S(2)}) collective-permute-start(bf16[2,1,256,256]{3,2,1,0:T(8,128)(2,1)} %get-tuple-element.76), channel_id=1, source_target_pairs={{1,2},{3,4},{5,6},{7,8},{9,10},{11,12},{13,14},{15,16},{17,18},{19... | collective-permute-start | bytes 786440 | tf_op jit(solution)/shard_map/ppermute | solution.py:52
  163.9 1.7 collective-permute-done.11
  165.6 4.1 %fusion.139 = (bf16[2,4,256,256]{3,2,1,0:T(8,128)(2,1)}, f32[2,4,256,256]{3,2,1,0:T(8,128)}) fusion(f32[2]{0:T(128)S(1)} %get-tuple-element.57, f32[2]{0:T(128)S(1)} %get-tuple-element.59, f32[2]{0:T(128)} %copy-done.18, f32[2]{0:T(128)S(1)} %get-tuple-element.72, f32[2]{0:T(128)} %copy-done.25, bf16[2,1,256,256]{3,2,1,0:T(8,128)(2,1)} %copy-done.4, ...), kind=kLoop, calls=%fused_computation.315 | loop fusion | flops 15728640 | bytes 7340104 | tf_op jit(solution)/shard_map/convert_element_type | solution.py:222
  169.7 5.3 %shard_map.79 = bf16[8,2,2,32,256]{4,3,2,1,0:T(8,128)(2,1)} custom-call(s32[4,2]{1,0:T(4,128)} %fusion.77.slot_ref, bf16[2,4,256,256]{3,2,1,0:T(8,128)(2,1)} %get-tuple-element.53.x_ref, bf16[4,4,256,256]{3,2,1,0:T(8,128)(2,1)} %copy-done, bf16[4,2,256,256]{3,2,1,0:T(8,128)(2,1)} %left_ref.5), custom_call_target="tpu_custom_call" | custom-call | flops 1073741824 | bytes 5242880 | tf_op jit(solution)/shard_map/pallas_call | solution.py:222
  176.4 22.5 %all_to_all.37 = f32[256,1,128]{2,1,0:T(1,128)S(1)} all-to-all(f32[256,1,128]{2,1,0:T(1,128)S(1)} %broadcast_in_dim.35), channel_id=1, replica_groups=mesh['term'=8,'sec'=32] {'term','sec'}, dimensions={0} | all-to-all | bytes 262144 | tf_op jit(solution)/shard_map/all_to_all | solution.py:227
  (185 shorter events, 26.3 us)
Async XLA Ops:
  2.0 13.3 %collective-permute-start.2 = (bf16[4,1,256,256]{3,2,1,0:T(8,128)(2,1)S(1)}, bf16[4,1,256,256]{3,2,1,0:T(8,128)(2,1)S(1)}, u32[]{:S(2)}, u32[]{:S(2)}) collective-permute-start(bf16[4,1,256,256]{3,2,1,0:T(8,128)(2,1)S(1)} %get-tuple-element.74), channel_id=1, source_target_pairs={{0,1},{1,0},{2,3},{3,2},{4,5},{5,4},{6,7},{7,6},{8,9},{9,8},{10,11... | collective-permute-start | bytes 1572872 | tf_op jit(solution)/shard_map/ppermute | solution.py:52
  6.4 6.4 %collective-permute-start = (bf16[2,1,256,256]{3,2,1,0:T(8,128)(2,1)S(1)}, bf16[2,1,256,256]{3,2,1,0:T(8,128)(2,1)S(1)}, u32[]{:S(2)}, u32[]{:S(2)}) collective-permute-start(bf16[2,1,256,256]{3,2,1,0:T(8,128)(2,1)S(1)} %get-tuple-element.81), channel_id=1, source_target_pairs={{0,1},{1,0},{2,3},{3,2},{4,5},{5,4},{6,7},{7,6},{8,9},{9,8},{10,11... | collective-permute-start | bytes 786440 | tf_op jit(solution)/shard_map/ppermute | solution.py:52
  6.5 7.7 %collective-permute-start.1 = (bf16[2,1,256,256]{3,2,1,0:T(8,128)(2,1)S(1)}, bf16[2,1,256,256]{3,2,1,0:T(8,128)(2,1)S(1)}, u32[]{:S(2)}, u32[]{:S(2)}) collective-permute-start(bf16[2,1,256,256]{3,2,1,0:T(8,128)(2,1)S(1)} %get-tuple-element.82), channel_id=1, source_target_pairs={{1,2},{3,4},{5,6},{7,8},{9,10},{11,12},{13,14},{15,16},{17,18},{19... | collective-permute-start | bytes 786440 | tf_op jit(solution)/shard_map/ppermute | solution.py:52
  8.4 11.4 %collective-permute-start.3 = (bf16[4,1,256,256]{3,2,1,0:T(8,128)(2,1)S(1)}, bf16[4,1,256,256]{3,2,1,0:T(8,128)(2,1)S(1)}, u32[]{:S(2)}, u32[]{:S(2)}) collective-permute-start(bf16[4,1,256,256]{3,2,1,0:T(8,128)(2,1)S(1)} %get-tuple-element.73), channel_id=1, source_target_pairs={{1,2},{3,4},{5,6},{7,8},{9,10},{11,12},{13,14},{15,16},{17,18},{19... | collective-permute-start | bytes 1572872 | tf_op jit(solution)/shard_map/ppermute | solution.py:52
  26.4 19.3 %all-to-all-start = ((bf16[8,2,2,32,256]{4,3,2,1,0:T(8,128)(2,1)}), bf16[8,2,2,32,256]{4,3,2,1,0:T(8,128)(2,1)S(1)}, u32[]{:S(2)}, u32[]{:S(2)}) async-start(bf16[8,2,2,32,256]{4,3,2,1,0:T(8,128)(2,1)} %shard_map.77), calls=%async_computation | async-start | bytes 1048576 | tf_op jit(solution)/shard_map/all_to_all | solution.py:75
  47.2 15.6 %all-to-all-start.1 = ((bf16[8,144,256]{2,1,0:T(8,128)(2,1)}), bf16[8,144,256]{2,1,0:T(8,128)(2,1)S(1)}, u32[]{:S(2)}, u32[]{:S(2)}) async-start(bf16[8,144,256]{2,1,0:T(8,128)(2,1)} %broadcast_in_dim.27), calls=%async_computation.1 | async-start | bytes 1179648 | tf_op jit(solution)/shard_map/all_to_all | solution.py:91
  50.8 12.2 %collective-permute-start.5 = (f32[1,256,256]{2,1,0:T(8,128)S(1)}, f32[1,256,256]{2,1,0:T(8,128)S(1)}, u32[]{:S(2)}, u32[]{:S(2)}) collective-permute-start(f32[1,256,256]{2,1,0:T(8,128)S(1)} %get-tuple-element.79), channel_id=1, source_target_pairs={{0,1},{1,0},{2,3},{3,2},{4,5},{5,4},{6,7},{7,6},{8,9},{9,8},{10,11... | collective-permute-start | bytes 786440 | tf_op jit(solution)/shard_map/ppermute | solution.py:52
  50.9 13.6 %collective-permute-start.6 = (f32[1,256,256]{2,1,0:T(8,128)S(1)}, f32[1,256,256]{2,1,0:T(8,128)}, u32[]{:S(2)}, u32[]{:S(2)}) collective-permute-start(f32[1,256,256]{2,1,0:T(8,128)S(1)} %get-tuple-element.80), channel_id=1, source_target_pairs={{1,2},{3,4},{5,6},{7,8},{9,10},{11,12},{13,14},{15,16},{17,18},{19... | collective-permute-start | bytes 786440 | tf_op jit(solution)/shard_map/ppermute | solution.py:52
  62.9 2.7 %collective-permute-start.4 = (f32[1,128]{1,0:T(1,128)S(1)}, f32[1,128]{1,0:T(1,128)S(1)}, u32[]{:S(2)}, u32[]{:S(2)}) collective-permute-start(f32[1,128]{1,0:T(1,128)S(1)} %pad_bitcast_fusion.1), channel_id=1, source_target_pairs={{0,1},{1,0},{2,3},{3,2},{4,5},{5,4},{6,7},{7,6},{8,9},{9,8},{10,11... | collective-permute-start | bytes 1544 | tf_op jit(solution)/shard_map/ppermute | solution.py:101
  65.5 29.5 %copy-start.5 = (bf16[2,1,256,256]{3,2,1,0:T(8,128)(2,1)S(1)}, bf16[2,1,256,256]{3,2,1,0:T(8,128)(2,1)}, u32[]{:S(2)}) copy-start(bf16[2,1,256,256]{3,2,1,0:T(8,128)(2,1)} %copy-done.4) | copy-start | bytes 786436
  66.3 26.1 %all-to-all-start.2 = ((f32[16,1,128]{2,1,0:T(1,128)}), f32[16,1,128]{2,1,0:T(1,128)S(1)}, u32[]{:S(2)}, u32[]{:S(2)}) async-start(f32[16,1,128]{2,1,0:T(1,128)} %broadcast_in_dim.30), calls=%async_computation.2 | async-start | bytes 16384 | tf_op jit(solution)/shard_map/all_to_all | solution.py:102
  86.9 6.3 %collective-permute-start.7 = (bf16[2,1,256,256]{3,2,1,0:T(8,128)(2,1)}, bf16[2,1,256,256]{3,2,1,0:T(8,128)(2,1)S(1)}, u32[]{:S(2)}, u32[]{:S(2)}) collective-permute-start(bf16[2,1,256,256]{3,2,1,0:T(8,128)(2,1)} %get-tuple-element.77), channel_id=1, source_target_pairs={{0,1},{1,0},{2,3},{3,2},{4,5},{5,4},{6,7},{7,6},{8,9},{9,8},{10,11... | collective-permute-start | bytes 786440 | tf_op jit(solution)/shard_map/ppermute | solution.py:52
  87.2 7.9 %collective-permute-start.8 = (bf16[2,1,256,256]{3,2,1,0:T(8,128)(2,1)}, bf16[2,1,256,256]{3,2,1,0:T(8,128)(2,1)S(1)}, u32[]{:S(2)}, u32[]{:S(2)}) collective-permute-start(bf16[2,1,256,256]{3,2,1,0:T(8,128)(2,1)} %get-tuple-element.78), channel_id=1, source_target_pairs={{1,2},{3,4},{5,6},{7,8},{9,10},{11,12},{13,14},{15,16},{17,18},{19... | collective-permute-start | bytes 786440 | tf_op jit(solution)/shard_map/ppermute | solution.py:52
  93.1 30.4 %copy-start.18 = (f32[2]{0:T(128)}, f32[2]{0:T(128)S(1)}, u32[]{:S(2)}) copy-start(f32[2]{0:T(128)S(1)} %get-tuple-element.70) | copy-start | bytes 28
  93.1 69.4 %copy-start.17 = (f32[2]{0:T(128)}, f32[2]{0:T(128)S(1)}, u32[]{:S(2)}) copy-start(f32[2]{0:T(128)S(1)} %get-tuple-element.71) | copy-start | bytes 28
  146.7 2.0 collective-permute-start.9
  149.2 13.2 %all-to-all-start.5 = ((f32[16,1,128]{2,1,0:T(1,128)}), f32[16,1,128]{2,1,0:T(1,128)S(1)}, u32[]{:S(2)}, u32[]{:S(2)}) async-start(f32[16,1,128]{2,1,0:T(1,128)} %broadcast_in_dim.34), calls=%async_computation.5 | async-start | bytes 16384 | tf_op jit(solution)/shard_map/all_to_all | solution.py:102
  157.0 7.0 %collective-permute-start.10 = (bf16[2,1,256,256]{3,2,1,0:T(8,128)(2,1)}, bf16[2,1,256,256]{3,2,1,0:T(8,128)(2,1)S(1)}, u32[]{:S(2)}, u32[]{:S(2)}) collective-permute-start(bf16[2,1,256,256]{3,2,1,0:T(8,128)(2,1)} %get-tuple-element.75), channel_id=1, source_target_pairs={{0,1},{1,0},{2,3},{3,2},{4,5},{5,4},{6,7},{7,6},{8,9},{9,8},{10,11... | collective-permute-start | bytes 786440 | tf_op jit(solution)/shard_map/ppermute | solution.py:52
  157.6 8.0 %collective-permute-start.11 = (bf16[2,1,256,256]{3,2,1,0:T(8,128)(2,1)}, bf16[2,1,256,256]{3,2,1,0:T(8,128)(2,1)}, u32[]{:S(2)}, u32[]{:S(2)}) collective-permute-start(bf16[2,1,256,256]{3,2,1,0:T(8,128)(2,1)} %get-tuple-element.76), channel_id=1, source_target_pairs={{1,2},{3,4},{5,6},{7,8},{9,10},{11,12},{13,14},{15,16},{17,18},{19... | collective-permute-start | bytes 786440 | tf_op jit(solution)/shard_map/ppermute | solution.py:52
  175.0 24.5 %copy-start.8 = (f32[2,2,32,256]{3,2,1,0:T(8,128)S(1)}, f32[2,2,32,256]{3,2,1,0:T(8,128)}, u32[]{:S(2)}) copy-start(f32[2,2,32,256]{3,2,1,0:T(8,128)} %copy-done.7) | copy-start | bytes 393220
  175.0 24.5 %copy-start.14 = (f32[2,2,32,256]{3,2,1,0:T(8,128)S(1)}, f32[2,2,32,256]{3,2,1,0:T(8,128)}, u32[]{:S(2)}) copy-start(f32[2,2,32,256]{3,2,1,0:T(8,128)} %get-tuple-element.68) | copy-start | bytes 393220
  175.0 24.5 %copy-start.15 = (f32[2,2,32,256]{3,2,1,0:T(8,128)S(1)}, f32[2,2,32,256]{3,2,1,0:T(8,128)}, u32[]{:S(2)}) copy-start(f32[2,2,32,256]{3,2,1,0:T(8,128)} %get-tuple-element.69) | copy-start | bytes 393220
  175.1 24.5 %copy-start.20 = (f32[2]{0:T(128)S(1)}, f32[2]{0:T(128)}, u32[]{:S(2)}) copy-start(f32[2]{0:T(128)} %copy-done.19) | copy-start | bytes 28
  175.1 24.5 %copy-start.22 = (f32[2]{0:T(128)S(1)}, f32[2]{0:T(128)}, u32[]{:S(2)}) copy-start(f32[2]{0:T(128)} %copy-done.21) | copy-start | bytes 28
  (24 other events, 277.5 us)

commit v2 on v1

v2 whole, which is shorter than its diff:
```python
import functools

import jax
import jax.numpy as jnp
from jax import lax
from jax.experimental import pallas as pl
from jax.experimental.pallas import tpu as pltpu
from jax.sharding import PartitionSpec as P

BF = jnp.bfloat16
F32 = jnp.float32


def apply_kernel(count, slot_ref, x_ref, right_ref, left_ref, *refs):
    field_refs, paired_refs, rest = refs[: count[0]], refs[count[0] : sum(count)], refs[sum(count) :]
    out_ref, z_ref = rest[0], rest[-1]
    vecs, _, states, _ = x_ref.shape
    terms, blocks = left_ref.shape[:2]
    for k in range(terms):
        for b in range(blocks):
            slot = slot_ref[k, b]
            x = x_ref[:, slot].reshape(vecs * states, states)
            z = lax.dot_general(
                x, right_ref[k, slot], (((1,), (1,)), ((), ())), preferred_element_type=F32
            ).astype(BF)
            for u in range(vecs):
                z_ref[b, pl.ds(k * states, states), pl.ds(u * states, states)] = z[
                    u * states : (u + 1) * states
                ]
    if sum(count):
        dot_ref = rest[-2]
        dot_ref[...] = jnp.zeros_like(dot_ref)
    for b in range(blocks):
        wide = jnp.concatenate([left_ref[k, b] for k in range(terms)], axis=1)
        acc = jnp.dot(wide, z_ref[b], preferred_element_type=F32)
        for u in range(vecs):
            part = acc[:, u * states : (u + 1) * states]
            if not sum(count):
                groups, share = out_ref.shape[0], out_ref.shape[3]
                out_ref[:, u, b] = part.reshape(groups, share, states).astype(out_ref.dtype)
            elif len(rest) == 3:
                out_ref[u, b] = part.astype(out_ref.dtype)
            products = [part * f[u, b].astype(F32) for f in field_refs]
            products += [x_ref[u, b].astype(F32) * f[u, b].astype(F32) for f in paired_refs]
            for i, product in enumerate(products):
                folded = jnp.sum(product.reshape(states // 8, 8, states), axis=0)
                dot_ref[i, u] = dot_ref[i, u] + folded[:, :128] + folded[:, 128:]


def shards(start_vectors, left_env, right_env, term_shift, precond, block_dims):
    vecs, blocks, states, _ = start_vectors.shape
    groups = lax.axis_size("term")
    sec = lax.axis_size("sec")
    share = states // groups
    core = lax.axis_index("sec") % 2
    term = lax.axis_index("term")
    factor = 1.0 / (blocks * sec * states * states)
    position = jnp.arange(states, dtype=jnp.int32)
    live_rows = position[None, :, None] < block_dims[:, None, None]
    live_cols = position[None, None, :] < block_dims[:, None, None]
    mask = (live_rows & live_cols).astype(F32)

    core_pairs = [(i, i ^ 1) for i in range(sec)]
    chip_pairs = [(i, i + 1) for i in range(1, sec - 1, 2)]
    chip_pairs = chip_pairs + [(j, i) for i, j in chip_pairs]

    def edges(x, axis):
        inner = lax.dynamic_index_in_dim(x, 1 - core, axis, keepdims=True)
        outer = lax.dynamic_index_in_dim(x, core, axis, keepdims=True)
        return lax.ppermute(inner, "sec", core_pairs), lax.ppermute(outer, "sec", chip_pairs)

    def with_edges(x, axis):
        return jnp.concatenate([x, *edges(x, axis)], axis=axis)

    def rows(x, axis):
        return lax.dynamic_slice_in_dim(x, term * share, share, axis)

    at = jnp.arange(blocks, dtype=jnp.int32)[None, :] + term_shift[:, None]
    slot = jnp.where(at < 0, 3 - core, jnp.where(at > 1, 2 + core, at)).astype(jnp.int32)

    def apply_op(x, fields=(), paired=(), keep=True):
        outs = []
        if not fields:
            outs = [jax.ShapeDtypeStruct((groups, vecs, blocks, share, states), BF)]
        elif keep:
            outs = [jax.ShapeDtypeStruct((vecs, blocks, states, states), BF)]
        count = (len(fields), len(paired))
        if sum(count):
            outs.append(jax.ShapeDtypeStruct((sum(count), vecs, 8, 128), F32))
        vmem = pl.BlockSpec(memory_space=pltpu.VMEM)
        result = pl.pallas_call(
            functools.partial(apply_kernel, count),
            out_shape=outs,
            in_specs=[pl.BlockSpec(memory_space=pltpu.SMEM)] + [vmem] * (3 + sum(count)),
            out_specs=[vmem] * len(outs),
            scratch_shapes=[pltpu.VMEM((blocks, left_env.shape[0] * states, vecs * states), BF)],
            compiler_params=pltpu.CompilerParams(vmem_limit_bytes=24 << 20),
            cost_estimate=pl.CostEstimate(
                flops=16 * vecs * blocks * states**3, bytes_accessed=5 << 20, transcendentals=0
            ),
        )(slot, x, right_all, left_env, *fields, *paired)
        return result[0] if len(outs) == 1 else result

    def exchange(parts):
        return lax.all_to_all(parts, "term", 0, 0)

    def settle(got):
        return jnp.sum(got.astype(F32), axis=0) * mask_rows

    def gather(part):
        body = part.astype(BF)
        got = exchange(jnp.broadcast_to(body[None], (groups,) + body.shape))
        return got.transpose(1, 2, 0, 3, 4).reshape(vecs, blocks, states, states)

    def sum_all(values):
        count = values.size
        row = jnp.pad(values.reshape(-1), (0, 128 - count))[None]
        everyone = groups * sec
        got = lax.all_to_all(
            jnp.broadcast_to(row[None], (everyone,) + row.shape), ("term", "sec"), 0, 0
        )
        return jnp.sum(got, axis=0)[0, :count].reshape(values.shape)

    def dots(left, right):
        return jnp.sum(left * right, axis=(1, 2, 3)) * factor

    def expand(value):
        return value[:, None, None, None]

    start = start_vectors * mask.astype(BF)
    right_all = with_edges(right_env, 1)
    start_all = with_edges(start, 1)
    mask_rows = rows(mask, 1)
    pre = rows(precond, 1)[None]
    vec = rows(start, 2).astype(F32)

    parts, pre_late = lax.optimization_barrier((apply_op(start_all), precond))
    got, pre_all = lax.optimization_barrier((exchange(parts), with_edges(pre_late, 0)))
    h_raw = settle(got)
    mv, mh = pre * vec, pre * h_raw
    gram = jnp.stack(
        [
            dots(vec, vec),
            dots(vec, h_raw),
            dots(vec, mv),
            dots(vec, mh),
            dots(h_raw, mh),
            dots(mv, mv),
            dots(mv, mh),
            dots(mh, mh),
        ]
    )
    h_all = with_edges(gather(h_raw), 1)
    total = sum_all(gram)
    scale = 1.0 / jnp.sqrt(total[0] + 1e-06)
    vv, vh, vmv, vmh, hmh, mvmv, mvmh, mhmh = total * scale**2
    correlation = vmh - vh * vmv
    square = (
        mhmh
        - 2.0 * vh * mvmh
        + vh**2 * mvmv
        - 2.0 * correlation * (vmh - vh * vmv)
        + correlation**2 * vv
    )
    dir_norm = jnp.sqrt(jnp.maximum(square, 0.0) + 1e-06)
    coupling = (hmh - vh * vmh - correlation * vh) / dir_norm
    rayleigh = vh

    def direct(v, h, m):
        raw = m * (h - expand(rayleigh) * v) - expand(correlation) * v
        return raw * expand(scale / dir_norm)

    dir_all = direct(start_all.astype(F32), h_all.astype(F32), pre_all[None])
    direction = direct(vec, h_raw, pre)
    vec = vec * expand(scale)
    h_vec = h_raw * expand(scale)
    dir_bf = dir_all.astype(BF)
    got = exchange(apply_op(dir_bf))
    m_start = (pre_all[None] * start_all.astype(F32)).astype(BF)
    m_dir = (pre_all[None] * dir_bf.astype(F32)).astype(BF)
    known = [x[:, :blocks] for x in (m_start, m_dir, dir_bf, start_all)]
    h_m_start, dots_start = apply_op(m_start, known)
    h_m_dir, dots_dir = apply_op(m_dir, known)
    got, h_m_start, h_m_dir, dots_start, dots_dir = lax.optimization_barrier(
        (got, h_m_start, h_m_dir, dots_start, dots_dir)
    )
    h_dir = settle(got)

    basis = [vec, direction, h_vec, h_dir]
    weighted = [pre * x for x in basis]
    pairs = [(i, j) for i in range(4) for j in range(i, 4)]
    plain = [(0, 0), (0, 1), (1, 1), (0, 2), (0, 3), (1, 2), (1, 3)]
    gram = jnp.stack(
        [dots(basis[i], basis[j]) for i, j in plain]
        + [dots(basis[i], weighted[j]) for i, j in pairs]
        + [dots(weighted[i], weighted[j]) for i, j in pairs]
    )
    hd_all = with_edges(gather(h_dir), 1)
    m_hd = (pre_all[None] * hd_all.astype(F32)).astype(BF)
    dots_hd = apply_op(m_hd, [m_hd[:, :blocks]] + known, [h_m_start, h_m_dir], keep=False)

    def lanes(x):
        return jnp.sum(x, axis=(2, 3)) * factor

    kernel_dots = lanes(jnp.concatenate([dots_hd, dots_start, dots_dir]))
    total = sum_all(jnp.concatenate([gram, kernel_dots]))
    far = total[gram.shape[0] :]
    one = {p: total[i] for i, p in enumerate(plain)}
    first = {p: total[len(plain) + i] for i, p in enumerate(pairs)}
    second = {p: total[len(plain) + len(pairs) + i] for i, p in enumerate(pairs)}

    def form(table, left, right):
        result = 0.0
        for i, x in left:
            for j, y in right:
                result = result + x * y * table[(min(i, j), max(i, j))]
        return result

    curvature = one[(1, 3)]
    energy = 0.5 * (rayleigh + curvature) - jnp.sqrt(
        (0.5 * (rayleigh - curvature)) ** 2 + coupling**2
    )
    weight = energy - rayleigh
    size = jnp.sqrt(coupling**2 + weight**2)
    keep, mix = coupling / size, weight / size
    v_of, h_of = [(0, keep), (1, mix)], [(2, keep), (3, mix)]
    old_rayleigh, old_correlation, old_norm = rayleigh, correlation, dir_norm
    rayleigh = form(one, v_of, h_of)
    resid_of = h_of + [(i, -rayleigh * x) for i, x in v_of]
    correlation = form(first, v_of, resid_of)
    square = (
        form(second, resid_of, resid_of)
        - 2.0 * correlation * form(first, v_of, resid_of)
        + correlation**2 * form(one, v_of, v_of)
    )
    dir_norm = jnp.sqrt(jnp.maximum(square, 0.0) + 1e-06)
    coupling = (form(first, resid_of, h_of) - correlation * rayleigh) / dir_norm

    mult = [
        mix,
        scale * keep * (old_rayleigh - rayleigh),
        -rayleigh * mix,
        keep * old_norm - correlation * mix,
        scale * keep * (old_correlation - correlation),
    ]
    on_hd = far[:5]
    on_start = [far[5]] + [far[7 + i] for i in range(4)]
    on_dir = [far[6]] + [far[11 + i] for i in range(4)]
    on_d = [first[3, 3], first[0, 3] / scale, first[1, 3], one[1, 3], one[0, 3] / scale]
    on_v = [
        first[2, 3] / scale,
        first[0, 2] / scale**2,
        first[1, 2] / scale,
        one[1, 2] / scale,
        one[0, 2] / scale**2,
    ]
    curvature = 0.0
    for j, column in enumerate([on_hd, on_start, on_dir, on_d, on_v]):
        for i in range(5):
            curvature = curvature + mult[i] * mult[j] * column[i]
    curvature = curvature / dir_norm**2

    def advance(v, d, h, hd, m):
        new_v = expand(keep) * v + expand(mix) * d
        new_h = expand(keep) * h + expand(mix) * hd
        raw = m * (new_h - expand(rayleigh) * new_v) - expand(correlation) * new_v
        return new_v, raw / expand(dir_norm)

    vec, direction = advance(vec, direction, h_vec, h_dir, pre)
    energy = 0.5 * (rayleigh + curvature) - jnp.sqrt(
        (0.5 * (rayleigh - curvature)) ** 2 + coupling**2
    )
    weight = energy - rayleigh
    size = jnp.sqrt(coupling**2 + weight**2)
    final = (expand(coupling) * vec + expand(weight) * direction) / expand(size)
    return (final, energy)


def solution(mesh):
    return jax.shard_map(
        shards,
        mesh=mesh,
        in_specs=(
            P(None, "sec", None, None),
            P("term", "sec", None, None),
            P("term", "sec", None, None),
            P("term"),
            P("sec", None, None),
            P("sec"),
        ),
        out_specs=(P(None, "sec", "term", None), P()),
        check_vma=False,
    )
```

time: 201 us -> 208 us (1.035)
  waiting for transfers between devices: 27.5 us -> 48.8 us
  starting transfers between devices: 65 us -> 46.2 us
  other arithmetic: 15.5 us -> 33.8 us
  blocking collectives: 65.2 us -> 49.7 us
  local copies, waits for them, and re-layouts: 10.2 us -> 14.7 us
  Pallas kernels: 15.6 us -> 12.1 us
    all_to_all x4, starting transfers between devices: 37.3 us -> 19.1 us  [exchange(): return lax.all_to_all(parts, 'term', 0, 0)]
    mul x31, other arithmetic: 0.12 us -> 17.9 us  [dots(): return jnp.sum(left * right, axis=(1, 2, 3)) * factor]
    all_to_all x3 -> x2, blocking collectives: 65.2 us -> 49.7 us  [sum_all(): lax.all_to_all(jnp.broadcast_to(row[None], (everyone,) + row.shape), ('te...]
    all_to_all x4, waiting for transfers between devices: 16.7 us -> 29.8 us  [exchange(): return lax.all_to_all(parts, 'term', 0, 0)]
    ppermute x5, waiting for transfers between devices: 10.1 us -> 19 us  [edges(): lax.ppermute(outer, 'sec', chip_pairs)]
    pallas_call x3 -> x5, Pallas kernels: 15.6 us -> 12.1 us  [apply_op(): pl.pallas_call(functools.partial(apply_kernel, count), out_shape=outs, in...]
    concatenate x0 -> x1, local copies, waits for them, and re-layouts: none -> 2.97 us  [shards(): total = sum_all(jnp.concatenate([gram, kernel_dots]))]
    convert_element_type x3, other arithmetic: 5.76 us -> 3.39 us  [the longest x1 2.32 us: shards(): m_dir = (pre_all[None] * dir_bf.astype(F32)).astype(BF)]
  transfers between devices with their start and end apart: 16 -> 14, of which waited for: 10 -> 9; matrix products, arithmetic and copies ran while one was open for 5% -> 7% of each run, Pallas kernels for 0% -> 2%
where the time goes in v2:
time: 208 us; the launch traced here: 207 us
  blocking collectives  49.7 us (24%)
  waiting for transfers between devices  48.8 us (23%)
  starting transfers between devices  46.2 us (22%)
  other arithmetic  33.8 us (16%)
  local copies, waits for them, and re-layouts  14.7 us (7%)
  Pallas kernels  12.1 us (6%)
    all_to_all x2, blocking collectives, sum_all(): lax.all_to_all(jnp.broadcast_to(row[None], (everyone,) + row.shape), ('te...  49.7 us
    all_to_all x4, waiting for transfers between devices, exchange(): return lax.all_to_all(parts, 'term', 0, 0)  29.8 us
    ppermute x5, starting transfers between devices, edges(): lax.ppermute(outer, 'sec', chip_pairs)  23.1 us
    all_to_all x4, starting transfers between devices, exchange(): return lax.all_to_all(parts, 'term', 0, 0)  19.1 us
    ppermute x5, waiting for transfers between devices, edges(): lax.ppermute(outer, 'sec', chip_pairs)  19 us
    mul x31, other arithmetic, dots(): return jnp.sum(left * right, axis=(1, 2, 3)) * factor  17.9 us
    pallas_call x5, Pallas kernels, apply_op(): pl.pallas_call(functools.partial(apply_kernel, count), out_shape=outs, in...  12.1 us
  transfers between devices with their start and end apart: 14, of which 9 were waited for; matrix products, arithmetic and copies ran while one was open for 7% of the time, Pallas kernels for 2%

profile of v2, /device:TPU:1, one launch (start us, length us, event | category | flops | bytes accessed | tf_op | source)
XLA Modules:
  0.0 206.6 jit_solution(16546477251991129317)
XLA Ops:
  2.0 3.3 %collective-permute-start.2 = (bf16[4,1,256,256]{3,2,1,0:T(8,128)(2,1)S(1)}, bf16[4,1,256,256]{3,2,1,0:T(8,128)(2,1)S(1)}, u32[]{:S(2)}, u32[]{:S(2)}) collective-permute-start(bf16[4,1,256,256]{3,2,1,0:T(8,128)(2,1)S(1)} %get-tuple-element.101), channel_id=1, source_target_pairs={{0,1},{1,0},{2,3},{3,2},{4,5},{5,4},{6,7},{7,6},{8,9},{9,8},{10,11... | collective-permute-start | bytes 1572872 | tf_op jit(solution)/shard_map/ppermute | solution.py:70
  8.4 3.6 %collective-permute-start.3 = (bf16[4,1,256,256]{3,2,1,0:T(8,128)(2,1)S(1)}, bf16[4,1,256,256]{3,2,1,0:T(8,128)(2,1)S(1)}, u32[]{:S(2)}, u32[]{:S(2)}) collective-permute-start(bf16[4,1,256,256]{3,2,1,0:T(8,128)(2,1)S(1)} %get-tuple-element.100), channel_id=1, source_target_pairs={{1,2},{3,4},{5,6},{7,8},{9,10},{11,12},{13,14},{15,16},{17,18},{19... | collective-permute-start | bytes 1572872 | tf_op jit(solution)/shard_map/ppermute | solution.py:70
  14.4 5.4 %collective-permute-done.3 = bf16[4,1,256,256]{3,2,1,0:T(8,128)(2,1)S(1)} collective-permute-done((bf16[4,1,256,256]{3,2,1,0:T(8,128)(2,1)S(1)}, bf16[4,1,256,256]{3,2,1,0:T(8,128)(2,1)S(1)}, u32[]{:S(2)}, u32[]{:S(2)}) %collective-permute-start.3) | collective-permute-done | bytes 524320 | tf_op jit(solution)/shard_map/ppermute | solution.py:70
  19.9 2.7 %shard_map.77 = bf16[8,2,2,32,256]{4,3,2,1,0:T(8,128)(2,1)} custom-call(s32[4,2]{1,0:T(4,128)S(1)} %fusion.60.slot_ref, bf16[2,4,256,256]{3,2,1,0:T(8,128)(2,1)S(1)} %pad_maximum_fusion.x_ref, bf16[4,4,256,256]{3,2,1,0:T(8,128)(2,1)S(1)} %constant_dynamic-update-slice_fusion.right_ref, bf16[4,2,256,256]{3,2,1,0:T(8,128)(2,1)S(1)} %copy-done), custom_call_target="tpu_custom_call" | custom-call | flops 1073741824 | bytes 5242880 | tf_op jit(solution)/shard_map/pallas_call | solution.py:91
  22.6 7.2 %all-to-all-start = ((bf16[8,2,2,32,256]{4,3,2,1,0:T(8,128)(2,1)}), bf16[8,2,2,32,256]{4,3,2,1,0:T(8,128)(2,1)}, u32[]{:S(2)}, u32[]{:S(2)}) async-start(bf16[8,2,2,32,256]{4,3,2,1,0:T(8,128)(2,1)} %shard_map.77), calls=%async_computation | async-start | bytes 1048576 | tf_op jit(solution)/shard_map/all_to_all | solution.py:105
  30.5 3.5 %collective-permute-start.5 = (f32[1,256,256]{2,1,0:T(8,128)S(1)}, f32[1,256,256]{2,1,0:T(8,128)}, u32[]{:S(2)}, u32[]{:S(2)}) collective-permute-start(f32[1,256,256]{2,1,0:T(8,128)S(1)} %get-tuple-element.107), channel_id=1, source_target_pairs={{1,2},{3,4},{5,6},{7,8},{9,10},{11,12},{13,14},{15,16},{17,18},{19... | collective-permute-start | bytes 786440 | tf_op jit(solution)/shard_map/ppermute | solution.py:70
  34.9 3.4 %collective-permute-done.5 = f32[1,256,256]{2,1,0:T(8,128)} collective-permute-done((f32[1,256,256]{2,1,0:T(8,128)S(1)}, f32[1,256,256]{2,1,0:T(8,128)}, u32[]{:S(2)}, u32[]{:S(2)}) %collective-permute-start.5) | collective-permute-done | bytes 262176 | tf_op jit(solution)/shard_map/ppermute | solution.py:70
  43.6 27.6 %all_to_all.30 = f32[256,1,128]{2,1,0:T(1,128)S(1)} all-to-all(f32[256,1,128]{2,1,0:T(1,128)S(1)} %broadcast_in_dim.17), channel_id=1, replica_groups=mesh['term'=8,'sec'=32] {'term','sec'}, dimensions={0} | all-to-all | bytes 262144 | tf_op jit(solution)/shard_map/all_to_all | solution.py:119
  72.1 3.5 %all-to-all-start.2 = ((bf16[8,2,2,32,256]{4,3,2,1,0:T(8,128)(2,1)}), bf16[8,2,2,32,256]{4,3,2,1,0:T(8,128)(2,1)S(1)}, u32[]{:S(2)}, u32[]{:S(2)}) async-start(bf16[8,2,2,32,256]{4,3,2,1,0:T(8,128)(2,1)} %broadcast_in_dim.18), calls=%async_computation.2 | async-start | bytes 1048576 | tf_op jit(solution)/shard_map/all_to_all | solution.py:105
  76.3 17.2 %all-to-all-done.2 = bf16[8,2,2,32,256]{4,3,2,1,0:T(8,128)(2,1)S(1)} async-done(((bf16[8,2,2,32,256]{4,3,2,1,0:T(8,128)(2,1)}), bf16[8,2,2,32,256]{4,3,2,1,0:T(8,128)(2,1)S(1)}, u32[]{:S(2)}, u32[]{:S(2)}) %all-to-all-start.2) | async-done | bytes 524320 | tf_op jit(solution)/shard_map/all_to_all | solution.py:105
  94.2 2.2 %collective-permute-start.7 = (bf16[2,1,256,256]{3,2,1,0:T(8,128)(2,1)S(1)}, bf16[2,1,256,256]{3,2,1,0:T(8,128)(2,1)S(1)}, u32[]{:S(2)}, u32[]{:S(2)}) collective-permute-start(bf16[2,1,256,256]{3,2,1,0:T(8,128)(2,1)S(1)} %get-tuple-element.105), channel_id=1, source_target_pairs={{1,2},{3,4},{5,6},{7,8},{9,10},{11,12},{13,14},{15,16},{17,18},{19... | collective-permute-start | bytes 786440 | tf_op jit(solution)/shard_map/ppermute | solution.py:70
  96.5 5.4 %collective-permute-done.7 = bf16[2,1,256,256]{3,2,1,0:T(8,128)(2,1)S(1)} collective-permute-done((bf16[2,1,256,256]{3,2,1,0:T(8,128)(2,1)S(1)}, bf16[2,1,256,256]{3,2,1,0:T(8,128)(2,1)S(1)}, u32[]{:S(2)}, u32[]{:S(2)}) %collective-permute-start.7) | collective-permute-done | bytes 262176 | tf_op jit(solution)/shard_map/ppermute | solution.py:70
  101.9 2.3 %multiply_convert_fusion.1 = (bf16[2,4,256,256]{3,2,1,0:T(8,128)(2,1)}, bf16[2,4,256,256]{3,2,1,0:T(8,128)(2,1)S(1)}, bf16[2,4,256,256]{3,2,1,0:T(8,128)(2,1)}) fusion(f32[4,256,256]{2,1,0:T(8,128)S(1)} %copy-done.15, f32[2]{0:T(128)S(1)} %get-tuple-element.96, f32[2]{0:T(128)S(1)} %get-tuple-element.98, bf16[2,1,256,256]{3,2,1,0:T(8,128)(2,1)S(1)} %copy-done.23, ...), kind=kLoop, calls=%fused_computation.10 | loop fusion | flops 9437184 | bytes 6291480 | tf_op jit(solution)/shard_map/convert_element_type | solution.py:180
  104.2 2.7 %shard_map.78 = bf16[8,2,2,32,256]{4,3,2,1,0:T(8,128)(2,1)} custom-call(s32[4,2]{1,0:T(4,128)S(1)} %fusion.60.slot_ref, bf16[2,4,256,256]{3,2,1,0:T(8,128)(2,1)S(1)} %get-tuple-element.95.x_ref, bf16[4,4,256,256]{3,2,1,0:T(8,128)(2,1)S(1)} %constant_dynamic-update-slice_fusion.right_ref, bf16[4,2,256,256]{3,2,1,0:T(8,128)(2,1)S(1)} %copy-done.1), custom_call_target="tpu_custom_call" | custom-call | flops 1073741824 | bytes 5242880 | tf_op jit(solution)/shard_map/pallas_call | solution.py:91
  107.9 4.3 %all-to-all-start.3 = ((bf16[8,2,2,32,256]{4,3,2,1,0:T(8,128)(2,1)}), bf16[8,2,2,32,256]{4,3,2,1,0:T(8,128)(2,1)}, u32[]{:S(2)}, u32[]{:S(2)}) async-start(bf16[8,2,2,32,256]{4,3,2,1,0:T(8,128)(2,1)} %shard_map.78), calls=%async_computation.3 | async-start | bytes 1048576 | tf_op jit(solution)/shard_map/all_to_all | solution.py:105
  120.7 2.9 %all-to-all-done.3 = bf16[8,2,2,32,256]{4,3,2,1,0:T(8,128)(2,1)} async-done(((bf16[8,2,2,32,256]{4,3,2,1,0:T(8,128)(2,1)}), bf16[8,2,2,32,256]{4,3,2,1,0:T(8,128)(2,1)}, u32[]{:S(2)}, u32[]{:S(2)}) %all-to-all-start.3) | async-done | bytes 524320 | tf_op jit(solution)/shard_map/all_to_all | solution.py:105
  125.6 2.6 %fusion.42 = (f32[2]{0:T(128)S(1)}, f32[2]{0:T(128)S(1)}, f32[2]{0:T(128)S(1)}, f32[2]{0:T(128)S(1)}, f32[2]{0:T(128)S(1)}, /*index=5*/f32[2]{0:T(128)S(1)}, f32...) fusion(f32[2,2,32,256]{3,2,1,0:T(8,128)S(1)} %get-tuple-element, ...), kind=kLoop, calls=%fused_computation.75 | loop fusion | flops 2228170 | bytes 721148 | tf_op jit(solution)/shard_map/reduce_sum | solution.py:125
  140.0 4.1 %all-to-all-start.4 = ((bf16[8,2,2,32,256]{4,3,2,1,0:T(8,128)(2,1)}), bf16[8,2,2,32,256]{4,3,2,1,0:T(8,128)(2,1)}, u32[]{:S(2)}, u32[]{:S(2)}) async-start(bf16[8,2,2,32,256]{4,3,2,1,0:T(8,128)(2,1)} %broadcast_in_dim.19), calls=%async_computation.4 | async-start | bytes 1048576 | tf_op jit(solution)/shard_map/all_to_all | solution.py:105
  149.9 8.1 %all-to-all-done.4 = bf16[8,2,2,32,256]{4,3,2,1,0:T(8,128)(2,1)} async-done(((bf16[8,2,2,32,256]{4,3,2,1,0:T(8,128)(2,1)}), bf16[8,2,2,32,256]{4,3,2,1,0:T(8,128)(2,1)}, u32[]{:S(2)}, u32[]{:S(2)}) %all-to-all-start.4) | async-done | bytes 524320 | tf_op jit(solution)/shard_map/all_to_all | solution.py:105
  159.4 11.8 %collective-permute-start.9 = (bf16[2,1,256,256]{3,2,1,0:T(8,128)(2,1)S(1)}, bf16[2,1,256,256]{3,2,1,0:T(8,128)(2,1)S(1)}, u32[]{:S(2)}, u32[]{:S(2)}) collective-permute-start(bf16[2,1,256,256]{3,2,1,0:T(8,128)(2,1)S(1)} %get-tuple-element.103), channel_id=1, source_target_pairs={{1,2},{3,4},{5,6},{7,8},{9,10},{11,12},{13,14},{15,16},{17,18},{19... | collective-permute-start | bytes 786440 | tf_op jit(solution)/shard_map/ppermute | solution.py:70
  172.3 2.8 %collective-permute-done.9 = bf16[2,1,256,256]{3,2,1,0:T(8,128)(2,1)S(1)} collective-permute-done((bf16[2,1,256,256]{3,2,1,0:T(8,128)(2,1)S(1)}, bf16[2,1,256,256]{3,2,1,0:T(8,128)(2,1)S(1)}, u32[]{:S(2)}, u32[]{:S(2)}) %collective-permute-start.9) | collective-permute-done | bytes 262176 | tf_op jit(solution)/shard_map/ppermute | solution.py:70
  175.5 2.3 %shard_map.81 = f32[7,2,8,128]{3,2,1,0:T(8,128)S(1)} custom-call(s32[4,2]{1,0:T(4,128)S(1)} %fusion.60.slot_ref, bf16[2,4,256,256]{3,2,1,0:T(8,128)(2,1)S(1)} %multiply_convert_fusion.x_ref, bf16[4,4,256,256]{3,2,1,0:T(8,128)(2,1)S(1)} %constant_dynamic-update-slice_fusion.right_ref, bf16[4,2,256,256]{3,2,1,0:T(8,128)(2,1)S(1)} %copy-done.3, ...), custom_call_target="tpu_custom_call" | custom-call | flops 1073741824 | bytes 5242880 | tf_op jit(solution)/shard_map/pallas_call | solution.py:91
  178.0 3.0 %concatenate.27 = f32[42,2]{1,0:T(8,128)S(1)} concatenate(f32[1,2]{1,0:T(1,128)} %multiply_bitcast_fusion.26, f32[1,2]{1,0:T(1,128)} %multiply_bitcast_fusion.25, f32[1,2]{1,0:T(1,128)} %multiply_bitcast_fusion.24, f32[1,2]{1,0:T(1,128)} %multiply_bitcast_fusion.23, f32[1,2]{1,0:T(1,128)} %multiply_bitcast_fusion.22, f32[1,2]{1,0:T(1,128)} %multiply_bitcast_fusion.21, ...), dimensions={0} | concatenate | bytes 672 | tf_op jit(solution)/shard_map/concatenate | solution.py:206
  181.2 22.1 %all_to_all.31 = f32[256,1,128]{2,1,0:T(1,128)S(1)} all-to-all(f32[256,1,128]{2,1,0:T(1,128)S(1)} %broadcast_in_dim.20), channel_id=1, replica_groups=mesh['term'=8,'sec'=32] {'term','sec'}, dimensions={0} | all-to-all | bytes 262144 | tf_op jit(solution)/shard_map/all_to_all | solution.py:119
  (164 shorter events, 51.1 us)
Async XLA Ops:
  2.0 10.1 %copy-start.17 = (bf16[4,2,256,256]{3,2,1,0:T(8,128)(2,1)S(1)}, bf16[4,2,256,256]{3,2,1,0:T(8,128)(2,1)}, u32[]{:S(2)}) copy-start(bf16[4,2,256,256]{3,2,1,0:T(8,128)(2,1)} %param.8) | copy-start | bytes 3145732
  2.0 12.3 %collective-permute-start.2 = (bf16[4,1,256,256]{3,2,1,0:T(8,128)(2,1)S(1)}, bf16[4,1,256,256]{3,2,1,0:T(8,128)(2,1)S(1)}, u32[]{:S(2)}, u32[]{:S(2)}) collective-permute-start(bf16[4,1,256,256]{3,2,1,0:T(8,128)(2,1)S(1)} %get-tuple-element.101), channel_id=1, source_target_pairs={{0,1},{1,0},{2,3},{3,2},{4,5},{5,4},{6,7},{7,6},{8,9},{9,8},{10,11... | collective-permute-start | bytes 1572872 | tf_op jit(solution)/shard_map/ppermute | solution.py:70
  6.4 5.9 %collective-permute-start = (bf16[2,1,256,256]{3,2,1,0:T(8,128)(2,1)S(1)}, bf16[2,1,256,256]{3,2,1,0:T(8,128)(2,1)S(1)}, u32[]{:S(2)}, u32[]{:S(2)}) collective-permute-start(bf16[2,1,256,256]{3,2,1,0:T(8,128)(2,1)S(1)} %get-tuple-element.108), channel_id=1, source_target_pairs={{0,1},{1,0},{2,3},{3,2},{4,5},{5,4},{6,7},{7,6},{8,9},{9,8},{10,11... | collective-permute-start | bytes 786440 | tf_op jit(solution)/shard_map/ppermute | solution.py:70
  6.5 7.7 %collective-permute-start.1 = (bf16[2,1,256,256]{3,2,1,0:T(8,128)(2,1)S(1)}, bf16[2,1,256,256]{3,2,1,0:T(8,128)(2,1)S(1)}, u32[]{:S(2)}, u32[]{:S(2)}) collective-permute-start(bf16[2,1,256,256]{3,2,1,0:T(8,128)(2,1)S(1)} %get-tuple-element.109), channel_id=1, source_target_pairs={{1,2},{3,4},{5,6},{7,8},{9,10},{11,12},{13,14},{15,16},{17,18},{19... | collective-permute-start | bytes 786440 | tf_op jit(solution)/shard_map/ppermute | solution.py:70
  8.4 11.4 %collective-permute-start.3 = (bf16[4,1,256,256]{3,2,1,0:T(8,128)(2,1)S(1)}, bf16[4,1,256,256]{3,2,1,0:T(8,128)(2,1)S(1)}, u32[]{:S(2)}, u32[]{:S(2)}) collective-permute-start(bf16[4,1,256,256]{3,2,1,0:T(8,128)(2,1)S(1)} %get-tuple-element.100), channel_id=1, source_target_pairs={{1,2},{3,4},{5,6},{7,8},{9,10},{11,12},{13,14},{15,16},{17,18},{19... | collective-permute-start | bytes 1572872 | tf_op jit(solution)/shard_map/ppermute | solution.py:70
  19.9 9.9 %copy-start.18 = (f32[2,256,256]{2,1,0:T(8,128)S(1)}, f32[2,256,256]{2,1,0:T(8,128)}, u32[]{:S(2)}) copy-start(f32[2,256,256]{2,1,0:T(8,128)} %param.10) | copy-start | bytes 1572868
  22.6 19.4 %all-to-all-start = ((bf16[8,2,2,32,256]{4,3,2,1,0:T(8,128)(2,1)}), bf16[8,2,2,32,256]{4,3,2,1,0:T(8,128)(2,1)}, u32[]{:S(2)}, u32[]{:S(2)}) async-start(bf16[8,2,2,32,256]{4,3,2,1,0:T(8,128)(2,1)} %shard_map.77), calls=%async_computation | async-start | bytes 1048576 | tf_op jit(solution)/shard_map/all_to_all | solution.py:105
  30.5 4.4 %collective-permute-start.4 = (f32[1,256,256]{2,1,0:T(8,128)}, f32[1,256,256]{2,1,0:T(8,128)}, u32[]{:S(2)}, u32[]{:S(2)}) collective-permute-start(f32[1,256,256]{2,1,0:T(8,128)} %get-tuple-element.106), channel_id=1, source_target_pairs={{0,1},{1,0},{2,3},{3,2},{4,5},{5,4},{6,7},{7,6},{8,9},{9,8},{10,11... | collective-permute-start | bytes 786440 | tf_op jit(solution)/shard_map/ppermute | solution.py:70
  30.5 7.8 %collective-permute-start.5 = (f32[1,256,256]{2,1,0:T(8,128)S(1)}, f32[1,256,256]{2,1,0:T(8,128)}, u32[]{:S(2)}, u32[]{:S(2)}) collective-permute-start(f32[1,256,256]{2,1,0:T(8,128)S(1)} %get-tuple-element.107), channel_id=1, source_target_pairs={{1,2},{3,4},{5,6},{7,8},{9,10},{11,12},{13,14},{15,16},{17,18},{19... | collective-permute-start | bytes 786440 | tf_op jit(solution)/shard_map/ppermute | solution.py:70
  34.9 37.2 %copy-start.19 = (f32[2,32,256]{2,1,0:T(8,128)}, f32[2,32,256]{2,1,0:T(8,128)S(1)}, u32[]{:S(2)}) copy-start(f32[2,32,256]{2,1,0:T(8,128)S(1)} %constant_dynamic-slice_fusion.5) | copy-start | bytes 196612
  72.1 21.4 %all-to-all-start.2 = ((bf16[8,2,2,32,256]{4,3,2,1,0:T(8,128)(2,1)}), bf16[8,2,2,32,256]{4,3,2,1,0:T(8,128)(2,1)S(1)}, u32[]{:S(2)}, u32[]{:S(2)}) async-start(bf16[8,2,2,32,256]{4,3,2,1,0:T(8,128)(2,1)} %broadcast_in_dim.18), calls=%async_computation.2 | async-start | bytes 1048576 | tf_op jit(solution)/shard_map/all_to_all | solution.py:105
  75.7 28.5 %copy-start.26 = (f32[128]{0:T(128)}, f32[128]{0:T(128)S(1)}, u32[]{:S(2)}) copy-start(f32[128]{0:T(128)S(1)} %reduce_sum.373) | copy-start | bytes 1540
  93.5 8.4 %copy-start.21 = (bf16[2,1,256,256]{3,2,1,0:T(8,128)(2,1)S(1)}, bf16[2,1,256,256]{3,2,1,0:T(8,128)(2,1)}, u32[]{:S(2)}) copy-start(bf16[2,1,256,256]{3,2,1,0:T(8,128)(2,1)} %copy-done.20) | copy-start | bytes 786436
  93.5 8.4 %copy-start.23 = (bf16[2,1,256,256]{3,2,1,0:T(8,128)(2,1)S(1)}, bf16[2,1,256,256]{3,2,1,0:T(8,128)(2,1)}, u32[]{:S(2)}) copy-start(bf16[2,1,256,256]{3,2,1,0:T(8,128)(2,1)} %copy-done.22) | copy-start | bytes 786436
  93.6 2.9 %collective-permute-start.6 = (bf16[2,1,256,256]{3,2,1,0:T(8,128)(2,1)S(1)}, bf16[2,1,256,256]{3,2,1,0:T(8,128)(2,1)S(1)}, u32[]{:S(2)}, u32[]{:S(2)}) collective-permute-start(bf16[2,1,256,256]{3,2,1,0:T(8,128)(2,1)S(1)} %get-tuple-element.104), channel_id=1, source_target_pairs={{0,1},{1,0},{2,3},{3,2},{4,5},{5,4},{6,7},{7,6},{8,9},{9,8},{10,11... | collective-permute-start | bytes 786440 | tf_op jit(solution)/shard_map/ppermute | solution.py:70
  94.2 7.7 %collective-permute-start.7 = (bf16[2,1,256,256]{3,2,1,0:T(8,128)(2,1)S(1)}, bf16[2,1,256,256]{3,2,1,0:T(8,128)(2,1)S(1)}, u32[]{:S(2)}, u32[]{:S(2)}) collective-permute-start(bf16[2,1,256,256]{3,2,1,0:T(8,128)(2,1)S(1)} %get-tuple-element.105), channel_id=1, source_target_pairs={{1,2},{3,4},{5,6},{7,8},{9,10},{11,12},{13,14},{15,16},{17,18},{19... | collective-permute-start | bytes 786440 | tf_op jit(solution)/shard_map/ppermute | solution.py:70
  107.9 15.7 %all-to-all-start.3 = ((bf16[8,2,2,32,256]{4,3,2,1,0:T(8,128)(2,1)}), bf16[8,2,2,32,256]{4,3,2,1,0:T(8,128)(2,1)}, u32[]{:S(2)}, u32[]{:S(2)}) async-start(bf16[8,2,2,32,256]{4,3,2,1,0:T(8,128)(2,1)} %shard_map.78), calls=%async_computation.3 | async-start | bytes 1048576 | tf_op jit(solution)/shard_map/all_to_all | solution.py:105
  128.2 43.0 %copy-start.31 = (f32[2]{0:T(128)S(1)}, f32[2]{0:T(128)}, u32[]{:S(2)}) copy-start(f32[2]{0:T(128)} %get-tuple-element.73) | copy-start | bytes 28
  128.2 43.5 %copy-start.30 = (f32[2]{0:T(128)S(1)}, f32[2]{0:T(128)}, u32[]{:S(2)}) copy-start(f32[2]{0:T(128)} %get-tuple-element.74) | copy-start | bytes 28
  140.0 18.1 %all-to-all-start.4 = ((bf16[8,2,2,32,256]{4,3,2,1,0:T(8,128)(2,1)}), bf16[8,2,2,32,256]{4,3,2,1,0:T(8,128)(2,1)}, u32[]{:S(2)}, u32[]{:S(2)}) async-start(bf16[8,2,2,32,256]{4,3,2,1,0:T(8,128)(2,1)} %broadcast_in_dim.19), calls=%async_computation.4 | async-start | bytes 1048576 | tf_op jit(solution)/shard_map/all_to_all | solution.py:105
  158.0 17.1 %copy-start.16 = (f32[4,256,256]{2,1,0:T(8,128)S(1)}, f32[4,256,256]{2,1,0:T(8,128)}, u32[]{:S(2)}) copy-start(f32[4,256,256]{2,1,0:T(8,128)} %pad_maximum_fusion.1) | copy-start | bytes 3145732
  159.3 13.1 %collective-permute-start.8 = (bf16[2,1,256,256]{3,2,1,0:T(8,128)(2,1)S(1)}, bf16[2,1,256,256]{3,2,1,0:T(8,128)(2,1)S(1)}, u32[]{:S(2)}, u32[]{:S(2)}) collective-permute-start(bf16[2,1,256,256]{3,2,1,0:T(8,128)(2,1)S(1)} %get-tuple-element.102), channel_id=1, source_target_pairs={{0,1},{1,0},{2,3},{3,2},{4,5},{5,4},{6,7},{7,6},{8,9},{9,8},{10,11... | collective-permute-start | bytes 786440 | tf_op jit(solution)/shard_map/ppermute | solution.py:70
  159.4 15.8 %collective-permute-start.9 = (bf16[2,1,256,256]{3,2,1,0:T(8,128)(2,1)S(1)}, bf16[2,1,256,256]{3,2,1,0:T(8,128)(2,1)S(1)}, u32[]{:S(2)}, u32[]{:S(2)}) collective-permute-start(bf16[2,1,256,256]{3,2,1,0:T(8,128)(2,1)S(1)} %get-tuple-element.103), channel_id=1, source_target_pairs={{1,2},{3,4},{5,6},{7,8},{9,10},{11,12},{13,14},{15,16},{17,18},{19... | collective-permute-start | bytes 786440 | tf_op jit(solution)/shard_map/ppermute | solution.py:70
  175.5 29.4 %copy-start.25 = (f32[2,2,32,256]{3,2,1,0:T(8,128)S(1)}, f32[2,2,32,256]{3,2,1,0:T(8,128)}, u32[]{:S(2)}) copy-start(f32[2,2,32,256]{3,2,1,0:T(8,128)} %get-tuple-element.92) | copy-start | bytes 393220
  (23 other events, 93.2 us)

commit v3 on v2

v3 whole, which is shorter than its diff:
```python
import functools

import jax
import jax.numpy as jnp
from jax import lax
from jax.experimental import pallas as pl
from jax.experimental.pallas import tpu as pltpu
from jax.sharding import PartitionSpec as P

BF = jnp.bfloat16
F32 = jnp.float32
PAIRS = [(i, j) for i in range(4) for j in range(i, 4)]
PLAIN = [(0, 0), (0, 1), (1, 1), (0, 2), (0, 3), (1, 2), (1, 3)]
EXTRA = 16


def fold(product):
    rows, cols = product.shape
    tile = jnp.sum(product.reshape(rows // 8, 8, cols), axis=0)
    return sum(tile[:, i : i + 128] for i in range(0, cols, 128))


def apply_kernel(count, slot_ref, x_ref, right_ref, left_ref, *refs):
    field_refs, paired_refs, rest = refs[: count[0]], refs[count[0] : sum(count)], refs[sum(count) :]
    out_ref, z_ref = rest[0], rest[-1]
    vecs, _, states, _ = x_ref.shape
    terms, blocks = left_ref.shape[:2]
    for k in range(terms):
        for b in range(blocks):
            slot = slot_ref[k, b]
            x = x_ref[:, slot].reshape(vecs * states, states)
            z = lax.dot_general(
                x, right_ref[k, slot], (((1,), (1,)), ((), ())), preferred_element_type=F32
            ).astype(BF)
            for u in range(vecs):
                z_ref[b, pl.ds(k * states, states), pl.ds(u * states, states)] = z[
                    u * states : (u + 1) * states
                ]
    if sum(count):
        dot_ref = rest[-2]
        dot_ref[...] = jnp.zeros_like(dot_ref)
    for b in range(blocks):
        wide = jnp.concatenate([left_ref[k, b] for k in range(terms)], axis=1)
        acc = jnp.dot(wide, z_ref[b], preferred_element_type=F32)
        for u in range(vecs):
            part = acc[:, u * states : (u + 1) * states]
            if not sum(count):
                groups, share = out_ref.shape[0], out_ref.shape[3]
                out_ref[:, u, b] = part.reshape(groups, share, states).astype(out_ref.dtype)
            elif len(rest) == 3:
                out_ref[u, b] = part.astype(out_ref.dtype)
            products = [part * f[u, b].astype(F32) for f in field_refs]
            products += [x_ref[u, b].astype(F32) * f[u, b].astype(F32) for f in paired_refs]
            for i, product in enumerate(products):
                dot_ref[i, u] = dot_ref[i, u] + fold(product)


def settle_kernel(factor, got_ref, mask_ref, *refs):
    h_ref, body_ref = refs[-2:]
    groups, vecs, blocks, share, states = got_ref.shape
    row = jnp.zeros((1, 128), F32)
    lane = lax.broadcasted_iota(jnp.int32, (1, 128), 1)
    for u in range(vecs):
        tiles = [jnp.zeros((8, 128), F32) for _ in range(8)]
        for b in range(blocks):
            h = got_ref[0, u, b].astype(F32)
            for t in range(1, groups):
                h = h + got_ref[t, u, b].astype(F32)
            h = h * mask_ref[b]
            h_ref[u, b] = h
            small = h.astype(BF)
            for t in range(groups):
                body_ref[t, pl.ds((u * blocks + b) * share, share), :] = small
            if len(refs) == 4:
                v, m = refs[0][u, b].astype(F32), refs[1][b]
                mv, mh = m * v, m * h
                products = [v * v, v * h, v * mv, v * mh, h * mh, mv * mv, mv * mh, mh * mh]
                tiles = [x + fold(y) for x, y in zip(tiles, products)]
        if len(refs) == 4:
            for i, tile in enumerate(tiles):
                row = row + jnp.where(lane == i * vecs + u, jnp.sum(tile) * factor, 0.0)
    if len(refs) == 4:
        high = row.astype(BF).astype(F32)
        middle = (row - high).astype(BF).astype(F32)
        low = row - high - middle
        index = lax.broadcasted_iota(jnp.int32, (EXTRA, 128), 0)
        tile = jnp.where(index == 0, high, jnp.where(index == 1, middle, jnp.where(index == 2, low, 0.0)))
        tile = tile.astype(BF)
        for t in range(groups):
            body_ref[t, pl.ds(vecs * blocks * share, EXTRA), pl.ds(0, 128)] = tile
            body_ref[t, pl.ds(vecs * blocks * share, EXTRA), pl.ds(128, states - 128)] = jnp.zeros(
                (EXTRA, states - 128), BF
            )


def block_of(got_ref, u, b, blocks, share):
    groups, _, states = got_ref.shape
    start = (u * blocks + b) * share
    if not isinstance(start, int):
        start = pl.multiple_of(start, share)
    return got_ref[:, pl.ds(start, share), :].reshape(groups * share, states)


def unpack_kernel(core_ref, got_ref, inner_ref, outer_ref, *row_refs):
    groups = got_ref.shape[0]
    vecs, states, _ = inner_ref.shape
    share = states // groups
    core = core_ref[0]
    for u in range(vecs):
        inner_ref[u] = block_of(got_ref, u, 1 - core, 2, share)
        outer_ref[u] = block_of(got_ref, u, core, 2, share)
    for row_ref in row_refs:
        tile = jnp.zeros((EXTRA, 128), F32)
        for t in range(groups):
            tile = tile + got_ref[t, pl.ds(vecs * states * 2 // groups, EXTRA), pl.ds(0, 128)].astype(F32)
        row_ref[...] = jnp.broadcast_to(jnp.sum(tile, axis=0, keepdims=True)[None], row_ref.shape)


def slot_blocks(own_ref, core_ref, chip_ref, u, share):
    own = [block_of(own_ref, u, b, 2, share) for b in range(2)]
    return own + [core_ref[u], chip_ref[u]]


def form_kernel(coef_ref, got_ref, core_ref, chip_ref, start_ref, pre_ref, pre_core, pre_chip, dir_ref, mdir_ref):
    vecs, slots, states, _ = dir_ref.shape
    share = states // got_ref.shape[0]
    for u in range(vecs):
        hs = slot_blocks(got_ref, core_ref, chip_ref, u, share)
        for i in range(slots):
            m = (pre_ref[0], pre_ref[1], pre_core[0], pre_chip[0])[i]
            v = start_ref[u, i].astype(F32)
            raw = m * (hs[i].astype(F32) - coef_ref[0, u] * v) - coef_ref[1, u] * v
            small = (raw * coef_ref[2, u]).astype(BF)
            dir_ref[u, i] = small
            mdir_ref[u, i] = (m * small.astype(F32)).astype(BF)


def lift_kernel(got_ref, core_ref, chip_ref, pre_ref, pre_core, pre_chip, out_ref):
    vecs, slots, states, _ = out_ref.shape
    share = states // got_ref.shape[0]
    for u in range(vecs):
        hs = slot_blocks(got_ref, core_ref, chip_ref, u, share)
        for i in range(slots):
            m = (pre_ref[0], pre_ref[1], pre_core[0], pre_chip[0])[i]
            out_ref[u, i] = (m * hs[i].astype(F32)).astype(BF)


def lift_start_kernel(start_ref, pre_ref, pre_core, pre_chip, out_ref):
    vecs, slots = out_ref.shape[:2]
    for u in range(vecs):
        for i in range(slots):
            m = (pre_ref[0], pre_ref[1], pre_core[0], pre_chip[0])[i]
            out_ref[u, i] = (m * start_ref[u, i].astype(F32)).astype(BF)


def gram_kernel(coef_ref, start_ref, h_ref, hd_ref, pre_ref, dot_ref, dir_ref):
    vecs, blocks = h_ref.shape[:2]
    for u in range(vecs):
        for b in range(blocks):
            m = pre_ref[b]
            v, h = start_ref[u, b].astype(F32), h_ref[u, b]
            d = (m * (h - coef_ref[0, u] * v) - coef_ref[1, u] * v) * coef_ref[2, u]
            dir_ref[u, b] = d
            basis = [v * coef_ref[3, u], d, h * coef_ref[3, u], hd_ref[u, b]]
            lifted = [m * x for x in basis]
            products = [basis[i] * basis[j] for i, j in PLAIN]
            products += [basis[i] * lifted[j] for i, j in PAIRS]
            products += [lifted[i] * lifted[j] for i, j in PAIRS]
            for i, product in enumerate(products):
                tile = fold(product)
                dot_ref[i, u] = tile if b == 0 else dot_ref[i, u] + tile


def call(kernel, outs, args, smem=0, scratch=(), flops=0):
    vmem = pl.BlockSpec(memory_space=pltpu.VMEM)
    specs = [pl.BlockSpec(memory_space=pltpu.SMEM)] * smem + [vmem] * (len(args) - smem)
    size = sum(x.size * x.dtype.itemsize for x in list(outs) + list(args))
    return pl.pallas_call(
        kernel,
        out_shape=[jax.ShapeDtypeStruct(x.shape, x.dtype) for x in outs],
        in_specs=specs,
        out_specs=[vmem] * len(outs),
        scratch_shapes=scratch,
        compiler_params=pltpu.CompilerParams(vmem_limit_bytes=24 << 20),
        cost_estimate=pl.CostEstimate(flops=flops, bytes_accessed=size, transcendentals=0),
    )(*args)


def shards(start_vectors, left_env, right_env, term_shift, precond, block_dims):
    vecs, blocks, states, _ = start_vectors.shape
    groups = lax.axis_size("term")
    sec = lax.axis_size("sec")
    share = states // groups
    core = lax.axis_index("sec") % 2
    core_id = core.reshape(1).astype(jnp.int32)
    term = lax.axis_index("term")
    factor = 1.0 / (blocks * sec * states * states)
    position = jnp.arange(states, dtype=jnp.int32)
    live_rows = position[None, :, None] < block_dims[:, None, None]
    live_cols = position[None, None, :] < block_dims[:, None, None]
    mask = live_rows & live_cols
    shape = jax.ShapeDtypeStruct

    core_pairs = [(i, i ^ 1) for i in range(sec)]
    chip_pairs = [(i, i + 1) for i in range(1, sec - 1, 2)]
    chip_pairs = chip_pairs + [(j, i) for i, j in chip_pairs]

    def swap(inner, outer):
        return lax.ppermute(inner, "sec", core_pairs), lax.ppermute(outer, "sec", chip_pairs)

    def edges(x, axis):
        inner = lax.dynamic_index_in_dim(x, 1 - core, axis, keepdims=True)
        outer = lax.dynamic_index_in_dim(x, core, axis, keepdims=True)
        return swap(inner, outer)

    def with_edges(x, axis):
        return jnp.concatenate([x, *edges(x, axis)], axis=axis)

    def rows(x, axis):
        return lax.dynamic_slice_in_dim(x, term * share, share, axis)

    at = jnp.arange(blocks, dtype=jnp.int32)[None, :] + term_shift[:, None]
    slot = jnp.where(at < 0, 3 - core, jnp.where(at > 1, 2 + core, at)).astype(jnp.int32)

    def apply_op(x, fields=(), paired=(), keep=True):
        outs = []
        if not fields:
            outs = [shape((groups, vecs, blocks, share, states), BF)]
        elif keep:
            outs = [shape((vecs, blocks, states, states), BF)]
        count = (len(fields), len(paired))
        if sum(count):
            outs.append(shape((sum(count), vecs, 8, 128), F32))
        result = call(
            functools.partial(apply_kernel, count),
            outs,
            [slot, x, right_all, left_env, *fields, *paired],
            smem=1,
            scratch=[pltpu.VMEM((blocks, left_env.shape[0] * states, vecs * states), BF)],
            flops=16 * vecs * blocks * states**3,
        )
        return result[0] if len(outs) == 1 else result

    def exchange(parts, axis="term"):
        return lax.all_to_all(parts, axis, 0, 0)

    start = jnp.where(mask[None], start_vectors, jnp.zeros((), BF))
    right_all = with_edges(right_env, 1)
    start_all = with_edges(start, 1)
    mask_rows = rows(mask.astype(F32), 1)
    pre = rows(precond, 1)
    vec = rows(start, 2)
    slice_shape = shape((vecs, blocks, share, states), F32)
    edge_shape = shape((vecs, states, states), BF)
    four_shape = shape((vecs, 4, states, states), BF)
    lines = vecs * blocks * share

    parts, pre_late = lax.optimization_barrier((apply_op(start_all), precond))
    got = exchange(parts)
    pre_core, pre_chip = edges(pre_late, 0)
    (m_start,) = call(lift_start_kernel, [four_shape], [start_all, precond, pre_core, pre_chip])
    got, m_start, pre_core, pre_chip = lax.optimization_barrier((got, m_start, pre_core, pre_chip))

    h_raw, body = call(
        functools.partial(settle_kernel, factor),
        [slice_shape, shape((groups, lines + EXTRA, states), BF)],
        [got, mask_rows, vec, pre],
    )
    got = exchange(body)
    inner, outer, row = call(
        unpack_kernel, [edge_shape, edge_shape, shape((sec, 8, 128), F32)], [core_id, got], smem=1
    )
    h_core, h_chip = swap(inner, outer)
    row = jnp.sum(exchange(row, "sec"), axis=0)[0, : 8 * vecs]
    total = row.reshape(8, vecs)
    scale = 1.0 / jnp.sqrt(total[0] + 1e-06)
    vv, vh, vmv, vmh, hmh, mvmv, mvmh, mhmh = total * scale**2
    correlation = vmh - vh * vmv
    square = (
        mhmh
        - 2.0 * vh * mvmh
        + vh**2 * mvmv
        - 2.0 * correlation * (vmh - vh * vmv)
        + correlation**2 * vv
    )
    dir_norm = jnp.sqrt(jnp.maximum(square, 0.0) + 1e-06)
    coupling = (hmh - vh * vmh - correlation * vh) / dir_norm
    rayleigh = vh
    coef = jnp.stack([rayleigh, correlation, scale / dir_norm, scale])

    dir_all, m_dir = call(
        form_kernel,
        [four_shape, four_shape],
        [coef, got, h_core, h_chip, start_all, precond, pre_core, pre_chip],
        smem=1,
    )
    got = exchange(apply_op(dir_all))
    known = [m_start, m_dir, dir_all, start_all]
    h_m_start, dots_start = apply_op(m_start, known)
    h_m_dir, dots_dir = apply_op(m_dir, known)
    got, h_m_start, h_m_dir, dots_start, dots_dir = lax.optimization_barrier(
        (got, h_m_start, h_m_dir, dots_start, dots_dir)
    )
    h_dir, body = call(
        functools.partial(settle_kernel, factor),
        [slice_shape, shape((groups, lines, states), BF)],
        [got, mask_rows],
    )
    got = exchange(body)
    gram, direction = call(
        gram_kernel,
        [shape((len(PLAIN) + 2 * len(PAIRS), vecs, 8, 128), F32), slice_shape],
        [coef, vec, h_raw, h_dir, pre],
        smem=1,
    )
    got, gram, direction = lax.optimization_barrier((got, gram, direction))
    inner, outer = call(unpack_kernel, [edge_shape, edge_shape], [core_id, got], smem=1)
    hd_core, hd_chip = swap(inner, outer)
    (m_hd,) = call(lift_kernel, [four_shape], [got, hd_core, hd_chip, precond, pre_core, pre_chip])
    dots_hd = apply_op(m_hd, [m_hd] + known, [h_m_start, h_m_dir], keep=False)

    tiles = jnp.concatenate([gram, dots_hd, dots_start, dots_dir])
    total = jnp.sum(tiles, axis=(2, 3)) * factor
    count = total.size
    everyone = groups * sec
    row = jnp.pad(total.reshape(-1), (0, 128 - count))[None]
    row = exchange(jnp.broadcast_to(row[None], (everyone,) + row.shape), ("term", "sec"))
    total = jnp.sum(row, axis=0)[0, :count].reshape(total.shape)
    one = {p: total[i] for i, p in enumerate(PLAIN)}
    first = {p: total[len(PLAIN) + i] for i, p in enumerate(PAIRS)}
    second = {p: total[len(PLAIN) + len(PAIRS) + i] for i, p in enumerate(PAIRS)}
    far = total[gram.shape[0] :]

    def form(table, left, right):
        result = 0.0
        for i, x in left:
            for j, y in right:
                result = result + x * y * table[(min(i, j), max(i, j))]
        return result

    curvature = one[(1, 3)]
    energy = 0.5 * (rayleigh + curvature) - jnp.sqrt(
        (0.5 * (rayleigh - curvature)) ** 2 + coupling**2
    )
    weight = energy - rayleigh
    size = jnp.sqrt(coupling**2 + weight**2)
    keep, mix = coupling / size, weight / size
    v_of, h_of = [(0, keep), (1, mix)], [(2, keep), (3, mix)]
    old_rayleigh, old_correlation, old_norm = rayleigh, correlation, dir_norm
    rayleigh = form(one, v_of, h_of)
    resid_of = h_of + [(i, -rayleigh * x) for i, x in v_of]
    correlation = form(first, v_of, resid_of)
    square = (
        form(second, resid_of, resid_of)
        - 2.0 * correlation * form(first, v_of, resid_of)
        + correlation**2 * form(one, v_of, v_of)
    )
    dir_norm = jnp.sqrt(jnp.maximum(square, 0.0) + 1e-06)
    coupling = (form(first, resid_of, h_of) - correlation * rayleigh) / dir_norm

    mult = [
        mix,
        scale * keep * (old_rayleigh - rayleigh),
        -rayleigh * mix,
        keep * old_norm - correlation * mix,
        scale * keep * (old_correlation - correlation),
    ]
    on_hd = far[:5]
    on_start = [far[5]] + [far[7 + i] for i in range(4)]
    on_dir = [far[6]] + [far[11 + i] for i in range(4)]
    on_d = [first[3, 3], first[0, 3] / scale, first[1, 3], one[1, 3], one[0, 3] / scale]
    on_v = [
        first[2, 3] / scale,
        first[0, 2] / scale**2,
        first[1, 2] / scale,
        one[1, 2] / scale,
        one[0, 2] / scale**2,
    ]
    curvature = 0.0
    for j, column in enumerate([on_hd, on_start, on_dir, on_d, on_v]):
        for i in range(5):
            curvature = curvature + mult[i] * mult[j] * column[i]
    curvature = curvature / dir_norm**2
    energy = 0.5 * (rayleigh + curvature) - jnp.sqrt(
        (0.5 * (rayleigh - curvature)) ** 2 + coupling**2
    )
    weight = energy - rayleigh
    size = jnp.sqrt(coupling**2 + weight**2)

    def expand(value):
        return value[:, None, None, None]

    new_v = expand(keep * scale) * vec.astype(F32) + expand(mix) * direction
    new_h = expand(keep * scale) * h_raw + expand(mix) * h_dir
    raw = pre[None] * (new_h - expand(rayleigh) * new_v) - expand(correlation) * new_v
    final = expand(coupling / size) * new_v + expand(weight / (dir_norm * size)) * raw
    return (final, energy)


def solution(mesh):
    return jax.shard_map(
        shards,
        mesh=mesh,
        in_specs=(
            P(None, "sec", None, None),
            P("term", "sec", None, None),
            P("term", "sec", None, None),
            P("term"),
            P("sec", None, None),
            P("sec"),
        ),
        out_specs=(P(None, "sec", "term", None), P()),
        check_vma=False,
    )
```

time: 208 us -> 192 us (0.923)
  other arithmetic: 33.8 us -> 5.79 us
  local copies, waits for them, and re-layouts: 14.7 us -> 35.8 us
  waiting for transfers between devices: 48.8 us -> 37.7 us
  Pallas kernels: 12.1 us -> 18.2 us
  blocking collectives: 49.7 us -> 46.3 us
    unnamed x68 -> x108, local copies, waits for them, and re-layouts: 2.81 us -> 30.7 us
    mul x34 -> x2, other arithmetic: 17.9 us -> 0.09 us  [the longest x1 0.09 us: shards(): scale * keep * (old_rayleigh - rayleigh)]
    ppermute x10, starting transfers between devices: 27.1 us -> 18.8 us  [the longest x5 14.2 us: swap(): lax.ppermute(outer, 'sec', chip_pairs)]
    all_to_all x4, starting transfers between devices: 19.1 us -> 26.2 us  [exchange(): return lax.all_to_all(parts, axis, 0, 0)]
    all_to_all x4, waiting for transfers between devices: 29.8 us -> 23.4 us  [exchange(): return lax.all_to_all(parts, axis, 0, 0)]
    pallas_call x5 -> x13, Pallas kernels: 12.1 us -> 18.2 us  [call(): pl.pallas_call(kernel, out_shape=[jax.ShapeDtypeStruct(x.shape, x.dtype)...]
    ppermute x10, waiting for transfers between devices: 19 us -> 14.3 us  [the longest x5 14.3 us: swap(): lax.ppermute(outer, 'sec', chip_pairs)]
    reduce_sum x7 -> x3, other arithmetic: 5.27 us -> 1.18 us  [the longest x1 0.94 us: shards(): row = jnp.sum(exchange(row, 'sec'), axis=0)[0, :8 * vecs]]
  transfers between devices with their start and end apart: 14 -> 14, of which waited for: 9 -> 8; matrix products, arithmetic and copies ran while one was open for 7% -> 4% of each run, Pallas kernels for 2% -> 3%
where the time goes in v3:
time: 192 us; the launch traced here: 190 us
  blocking collectives  46.3 us (24%)
  starting transfers between devices  45 us (23%)
  waiting for transfers between devices  37.7 us (20%)
  local copies, waits for them, and re-layouts  35.8 us (19%)
  Pallas kernels  18.2 us (9%)
  other arithmetic  5.79 us (3%)
    all_to_all x2, blocking collectives, exchange(): return lax.all_to_all(parts, axis, 0, 0)  46.3 us
    unnamed x108, local copies, waits for them, and re-layouts  30.7 us
    all_to_all x4, starting transfers between devices, exchange(): return lax.all_to_all(parts, axis, 0, 0)  26.2 us
    all_to_all x4, waiting for transfers between devices, exchange(): return lax.all_to_all(parts, axis, 0, 0)  23.4 us
    pallas_call x13, Pallas kernels, call(): pl.pallas_call(kernel, out_shape=[jax.ShapeDtypeStruct(x.shape, x.dtype)...  18.2 us
    ppermute x5, waiting for transfers between devices, swap(): lax.ppermute(outer, 'sec', chip_pairs)  14.3 us
    ppermute x5, starting transfers between devices, swap(): lax.ppermute(outer, 'sec', chip_pairs)  14.2 us
    ppermute x5, starting transfers between devices, swap(): lax.ppermute(inner, 'sec', core_pairs)  4.64 us
  transfers between devices with their start and end apart: 14, of which 8 were waited for; matrix products, arithmetic and copies ran while one was open for 4% of the time, Pallas kernels for 3%

profile of v3, /device:TPU:1, one launch (start us, length us, event | category | flops | bytes accessed | tf_op | source)
XLA Modules:
  0.0 190.1 jit_solution(11747254307015789528)
XLA Ops:
  2.1 3.3 %collective-permute-start.2 = (bf16[4,1,256,256]{3,2,1,0:T(8,128)(2,1)S(1)}, bf16[4,1,256,256]{3,2,1,0:T(8,128)(2,1)S(1)}, u32[]{:S(2)}, u32[]{:S(2)}) collective-permute-start(bf16[4,1,256,256]{3,2,1,0:T(8,128)(2,1)S(1)} %get-tuple-element.81), channel_id=1, source_target_pairs={{0,1},{1,0},{2,3},{3,2},{4,5},{5,4},{6,7},{7,6},{8,9},{9,8},{10,11... | collective-permute-start | bytes 1572872 | tf_op jit(solution)/shard_map/ppermute | solution.py:209
  5.9 1.9 %collective-permute-start.1 = (bf16[2,1,256,256]{3,2,1,0:T(8,128)(2,1)S(1)}, bf16[2,1,256,256]{3,2,1,0:T(8,128)(2,1)S(1)}, u32[]{:S(2)}, u32[]{:S(2)}) collective-permute-start(bf16[2,1,256,256]{3,2,1,0:T(8,128)(2,1)S(1)} %get-tuple-element.85), channel_id=1, source_target_pairs={{1,2},{3,4},{5,6},{7,8},{9,10},{11,12},{13,14},{15,16},{17,18},{19... | collective-permute-start | bytes 786440 | tf_op jit(solution)/shard_map/ppermute | solution.py:209
  7.8 3.6 %collective-permute-start.3 = (bf16[4,1,256,256]{3,2,1,0:T(8,128)(2,1)S(1)}, bf16[4,1,256,256]{3,2,1,0:T(8,128)(2,1)S(1)}, u32[]{:S(2)}, u32[]{:S(2)}) collective-permute-start(bf16[4,1,256,256]{3,2,1,0:T(8,128)(2,1)S(1)} %get-tuple-element.80), channel_id=1, source_target_pairs={{1,2},{3,4},{5,6},{7,8},{9,10},{11,12},{13,14},{15,16},{17,18},{19... | collective-permute-start | bytes 1572872 | tf_op jit(solution)/shard_map/ppermute | solution.py:209
  11.6 1.9 %collective-permute-done.1 = bf16[2,1,256,256]{3,2,1,0:T(8,128)(2,1)S(1)} collective-permute-done((bf16[2,1,256,256]{3,2,1,0:T(8,128)(2,1)S(1)}, bf16[2,1,256,256]{3,2,1,0:T(8,128)(2,1)S(1)}, u32[]{:S(2)}, u32[]{:S(2)}) %collective-permute-start.1) | collective-permute-done | bytes 262176 | tf_op jit(solution)/shard_map/ppermute | solution.py:209
  13.7 5.4 %collective-permute-done.3 = bf16[4,1,256,256]{3,2,1,0:T(8,128)(2,1)S(1)} collective-permute-done((bf16[4,1,256,256]{3,2,1,0:T(8,128)(2,1)S(1)}, bf16[4,1,256,256]{3,2,1,0:T(8,128)(2,1)S(1)}, u32[]{:S(2)}, u32[]{:S(2)}) %collective-permute-start.3) | collective-permute-done | bytes 524320 | tf_op jit(solution)/shard_map/ppermute | solution.py:209
  19.2 1.9 shard_map.77
  21.9 7.2 %all-to-all-start = ((bf16[8,2,2,32,256]{4,3,2,1,0:T(8,128)(2,1)}), bf16[8,2,2,32,256]{4,3,2,1,0:T(8,128)(2,1)}, u32[]{:S(2)}, u32[]{:S(2)}) async-start(bf16[8,2,2,32,256]{4,3,2,1,0:T(8,128)(2,1)} %copy-done.21), calls=%async_computation | async-start | bytes 1048576 | tf_op jit(solution)/shard_map/all_to_all | solution.py:245
  30.1 3.1 %collective-permute-start.5 = (f32[1,256,256]{2,1,0:T(8,128)S(1)}, f32[1,256,256]{2,1,0:T(8,128)S(1)}, u32[]{:S(2)}, u32[]{:S(2)}) collective-permute-start(f32[1,256,256]{2,1,0:T(8,128)S(1)} %get-tuple-element.82), channel_id=1, source_target_pairs={{1,2},{3,4},{5,6},{7,8},{9,10},{11,12},{13,14},{15,16},{17,18},{19... | collective-permute-start | bytes 786440 | tf_op jit(solution)/shard_map/ppermute | solution.py:209
  43.5 25.3 %all_to_all.30.got_ref = bf16[8,144,256]{2,1,0:T(8,128)(2,1)S(1)} all-to-all(bf16[8,144,256]{2,1,0:T(8,128)(2,1)S(1)} %get-tuple-element.36), channel_id=1, replica_groups=mesh['term'=8,'sec'=32] {'term'}, dimensions={0} | all-to-all | bytes 1179648 | tf_op jit(solution)/shard_map/all_to_all | solution.py:245
  71.8 10.8 %all-to-all-start.2 = ((f32[32,8,128]{2,1,0:T(8,128)}), f32[32,8,128]{2,1,0:T(8,128)}, u32[]{:S(2)}, u32[]{:S(2)}) async-start(f32[32,8,128]{2,1,0:T(8,128)} %copy-done.38), calls=%async_computation.2 | async-start | bytes 262144 | tf_op jit(solution)/shard_map/all_to_all | solution.py:245
  82.9 3.3 %collective-permute-start.7 = (bf16[2,256,256]{2,1,0:T(8,128)(2,1)}, bf16[2,256,256]{2,1,0:T(8,128)(2,1)}, u32[]{:S(2)}, u32[]{:S(2)}) collective-permute-start(bf16[2,256,256]{2,1,0:T(8,128)(2,1)} %copy-done.44), channel_id=1, source_target_pairs={{1,2},{3,4},{5,6},{7,8},{9,10},{11,12},{13,14},{15,16},{17,18},{19... | collective-permute-start | bytes 786440 | tf_op jit(solution)/shard_map/ppermute | solution.py:209
  86.3 3.9 %all-to-all-done.2 = f32[32,8,128]{2,1,0:T(8,128)} async-done(((f32[32,8,128]{2,1,0:T(8,128)}), f32[32,8,128]{2,1,0:T(8,128)}, u32[]{:S(2)}, u32[]{:S(2)}) %all-to-all-start.2) | async-done | bytes 131104 | tf_op jit(solution)/shard_map/all_to_all | solution.py:245
  95.6 1.8 shard_map.81
  98.5 1.9 shard_map.82
  102.1 4.1 %all-to-all-start.3 = ((bf16[8,2,2,32,256]{4,3,2,1,0:T(8,128)(2,1)}), bf16[8,2,2,32,256]{4,3,2,1,0:T(8,128)(2,1)}, u32[]{:S(2)}, u32[]{:S(2)}) async-start(bf16[8,2,2,32,256]{4,3,2,1,0:T(8,128)(2,1)} %copy-done.22), calls=%async_computation.3 | async-start | bytes 1048576 | tf_op jit(solution)/shard_map/all_to_all | solution.py:245
  111.2 2.1 %shard_map.84 = (bf16[2,2,256,256]{3,2,1,0:T(8,128)(2,1)S(1)}, f32[4,2,8,128]{3,2,1,0:T(8,128)S(1)}) custom-call(s32[4,2]{1,0:T(4,128)S(1)} %fusion.slot_ref, bf16[2,4,256,256]{3,2,1,0:T(8,128)(2,1)S(1)} %copy-done.8, bf16[4,4,256,256]{3,2,1,0:T(8,128)(2,1)S(1)} %constant_dynamic-update-slice_fusion.right_ref, bf16[4,2,256,256]{3,2,1,0:T(8,128)(2,1)S(1)} %copy-done.5, ...), custom_call_target="tpu_custom_call" | custom-call | flops 1073741824 | bytes 8945696 | tf_op jit(solution)/shard_map/pallas_call | solution.py:178
  114.7 2.1 %shard_map.83 = (bf16[2,2,256,256]{3,2,1,0:T(8,128)(2,1)S(1)}, f32[4,2,8,128]{3,2,1,0:T(8,128)S(1)}) custom-call(s32[4,2]{1,0:T(4,128)S(1)} %fusion.slot_ref, bf16[2,4,256,256]{3,2,1,0:T(8,128)(2,1)S(1)} %copy-done.1, bf16[4,4,256,256]{3,2,1,0:T(8,128)(2,1)S(1)} %constant_dynamic-update-slice_fusion.right_ref, bf16[4,2,256,256]{3,2,1,0:T(8,128)(2,1)S(1)} %copy-done.5, ...), custom_call_target="tpu_custom_call" | custom-call | flops 1073741824 | bytes 8945696 | tf_op jit(solution)/shard_map/pallas_call | solution.py:178
  118.2 6.0 %all-to-all-done.3.got_ref = bf16[8,2,2,32,256]{4,3,2,1,0:T(8,128)(2,1)} async-done(((bf16[8,2,2,32,256]{4,3,2,1,0:T(8,128)(2,1)}), bf16[8,2,2,32,256]{4,3,2,1,0:T(8,128)(2,1)}, u32[]{:S(2)}, u32[]{:S(2)}) %all-to-all-start.3) | async-done | bytes 524320 | tf_op jit(solution)/shard_map/all_to_all | solution.py:245
  126.8 4.1 %all-to-all-start.4 = ((bf16[8,128,256]{2,1,0:T(8,128)(2,1)}), bf16[8,128,256]{2,1,0:T(8,128)(2,1)}, u32[]{:S(2)}, u32[]{:S(2)}) async-start(bf16[8,128,256]{2,1,0:T(8,128)(2,1)} %copy-done.29), calls=%async_computation.4 | async-start | bytes 1048576 | tf_op jit(solution)/shard_map/all_to_all | solution.py:245
  136.0 13.0 %all-to-all-done.4.got_ref = bf16[8,128,256]{2,1,0:T(8,128)(2,1)} async-done(((bf16[8,128,256]{2,1,0:T(8,128)(2,1)}), bf16[8,128,256]{2,1,0:T(8,128)(2,1)}, u32[]{:S(2)}, u32[]{:S(2)}) %all-to-all-start.4) | async-done | bytes 524320 | tf_op jit(solution)/shard_map/all_to_all | solution.py:245
  150.9 2.2 %collective-permute-start.9 = (bf16[2,256,256]{2,1,0:T(8,128)(2,1)S(1)}, bf16[2,256,256]{2,1,0:T(8,128)(2,1)S(1)}, u32[]{:S(2)}, u32[]{:S(2)}) collective-permute-start(bf16[2,256,256]{2,1,0:T(8,128)(2,1)S(1)} %get-tuple-element.58), channel_id=1, source_target_pairs={{1,2},{3,4},{5,6},{7,8},{9,10},{11,12},{13,14},{15,16},{17,18},{19... | collective-permute-start | bytes 786440 | tf_op jit(solution)/shard_map/ppermute | solution.py:209
  153.1 5.5 %collective-permute-done.9.chip_ref = bf16[2,256,256]{2,1,0:T(8,128)(2,1)S(1)} collective-permute-done((bf16[2,256,256]{2,1,0:T(8,128)(2,1)S(1)}, bf16[2,256,256]{2,1,0:T(8,128)(2,1)S(1)}, u32[]{:S(2)}, u32[]{:S(2)}) %collective-permute-start.9) | collective-permute-done | bytes 262176 | tf_op jit(solution)/shard_map/ppermute | solution.py:209
  164.2 2.3 %shard_map.89 = f32[7,2,8,128]{3,2,1,0:T(8,128)S(1)} custom-call(s32[4,2]{1,0:T(4,128)S(1)} %fusion.slot_ref, bf16[2,4,256,256]{3,2,1,0:T(8,128)(2,1)S(1)} %shard_map.88.x_ref.refs_0_, bf16[4,4,256,256]{3,2,1,0:T(8,128)(2,1)S(1)} %constant_dynamic-update-slice_fusion.right_ref, bf16[4,2,256,256]{3,2,1,0:T(8,128)(2,1)S(1)} %copy-done.6, ...), custom_call_target="tpu_custom_call" | custom-call | flops 1073741824 | bytes 10543136 | tf_op jit(solution)/shard_map/pallas_call | solution.py:178
  166.9 21.0 %all_to_all.31 = f32[256,1,128]{2,1,0:T(1,128)S(1)} all-to-all(f32[256,1,128]{2,1,0:T(1,128)S(1)} %broadcast_in_dim.25), channel_id=1, replica_groups=mesh['term'=8,'sec'=32] {'term','sec'}, dimensions={0} | all-to-all | bytes 262144 | tf_op jit(solution)/shard_map/all_to_all | solution.py:245
  (157 shorter events, 51.2 us)
Async XLA Ops:
  0.7 10.8 %copy-start.47 = (bf16[4,2,256,256]{3,2,1,0:T(8,128)(2,1)S(1)}, bf16[4,2,256,256]{3,2,1,0:T(8,128)(2,1)}, u32[]{:S(2)}) copy-start(bf16[4,2,256,256]{3,2,1,0:T(8,128)(2,1)} %param.8) | copy-start | bytes 3145732
  2.1 11.6 %collective-permute-start.2 = (bf16[4,1,256,256]{3,2,1,0:T(8,128)(2,1)S(1)}, bf16[4,1,256,256]{3,2,1,0:T(8,128)(2,1)S(1)}, u32[]{:S(2)}, u32[]{:S(2)}) collective-permute-start(bf16[4,1,256,256]{3,2,1,0:T(8,128)(2,1)S(1)} %get-tuple-element.81), channel_id=1, source_target_pairs={{0,1},{1,0},{2,3},{3,2},{4,5},{5,4},{6,7},{7,6},{8,9},{9,8},{10,11... | collective-permute-start | bytes 1572872 | tf_op jit(solution)/shard_map/ppermute | solution.py:209
  5.7 8.0 %copy-start.46 = (bf16[2,2,256,256]{3,2,1,0:T(8,128)(2,1)}, bf16[2,2,256,256]{3,2,1,0:T(8,128)(2,1)S(1)}, u32[]{:S(2)}) copy-start(bf16[2,2,256,256]{3,2,1,0:T(8,128)(2,1)S(1)} %broadcast_select_fusion) | copy-start | bytes 1572868
  5.7 5.9 %collective-permute-start = (bf16[2,1,256,256]{3,2,1,0:T(8,128)(2,1)S(1)}, bf16[2,1,256,256]{3,2,1,0:T(8,128)(2,1)S(1)}, u32[]{:S(2)}, u32[]{:S(2)}) collective-permute-start(bf16[2,1,256,256]{3,2,1,0:T(8,128)(2,1)S(1)} %get-tuple-element.84), channel_id=1, source_target_pairs={{0,1},{1,0},{2,3},{3,2},{4,5},{5,4},{6,7},{7,6},{8,9},{9,8},{10,11... | collective-permute-start | bytes 786440 | tf_op jit(solution)/shard_map/ppermute | solution.py:209
  5.9 7.7 %collective-permute-start.1 = (bf16[2,1,256,256]{3,2,1,0:T(8,128)(2,1)S(1)}, bf16[2,1,256,256]{3,2,1,0:T(8,128)(2,1)S(1)}, u32[]{:S(2)}, u32[]{:S(2)}) collective-permute-start(bf16[2,1,256,256]{3,2,1,0:T(8,128)(2,1)S(1)} %get-tuple-element.85), channel_id=1, source_target_pairs={{1,2},{3,4},{5,6},{7,8},{9,10},{11,12},{13,14},{15,16},{17,18},{19... | collective-permute-start | bytes 786440 | tf_op jit(solution)/shard_map/ppermute | solution.py:209
  7.8 11.4 %collective-permute-start.3 = (bf16[4,1,256,256]{3,2,1,0:T(8,128)(2,1)S(1)}, bf16[4,1,256,256]{3,2,1,0:T(8,128)(2,1)S(1)}, u32[]{:S(2)}, u32[]{:S(2)}) collective-permute-start(bf16[4,1,256,256]{3,2,1,0:T(8,128)(2,1)S(1)} %get-tuple-element.80), channel_id=1, source_target_pairs={{1,2},{3,4},{5,6},{7,8},{9,10},{11,12},{13,14},{15,16},{17,18},{19... | collective-permute-start | bytes 1572872 | tf_op jit(solution)/shard_map/ppermute | solution.py:209
  11.6 7.6 %copy-start.3 = (bf16[4,2,256,256]{3,2,1,0:T(8,128)(2,1)S(1)}, bf16[4,2,256,256]{3,2,1,0:T(8,128)(2,1)}, u32[]{:S(2)}) copy-start(bf16[4,2,256,256]{3,2,1,0:T(8,128)(2,1)} %left_ref.9) | copy-start | bytes 3145732
  21.9 19.4 %all-to-all-start = ((bf16[8,2,2,32,256]{4,3,2,1,0:T(8,128)(2,1)}), bf16[8,2,2,32,256]{4,3,2,1,0:T(8,128)(2,1)}, u32[]{:S(2)}, u32[]{:S(2)}) async-start(bf16[8,2,2,32,256]{4,3,2,1,0:T(8,128)(2,1)} %copy-done.21), calls=%async_computation | async-start | bytes 1048576 | tf_op jit(solution)/shard_map/all_to_all | solution.py:245
  30.1 7.7 %collective-permute-start.5 = (f32[1,256,256]{2,1,0:T(8,128)S(1)}, f32[1,256,256]{2,1,0:T(8,128)S(1)}, u32[]{:S(2)}, u32[]{:S(2)}) collective-permute-start(f32[1,256,256]{2,1,0:T(8,128)S(1)} %get-tuple-element.82), channel_id=1, source_target_pairs={{1,2},{3,4},{5,6},{7,8},{9,10},{11,12},{13,14},{15,16},{17,18},{19... | collective-permute-start | bytes 786440 | tf_op jit(solution)/shard_map/ppermute | solution.py:209
  33.2 4.6 %collective-permute-start.4 = (f32[1,256,256]{2,1,0:T(8,128)S(1)}, f32[1,256,256]{2,1,0:T(8,128)S(1)}, u32[]{:S(2)}, u32[]{:S(2)}) collective-permute-start(f32[1,256,256]{2,1,0:T(8,128)S(1)} %get-tuple-element.83), channel_id=1, source_target_pairs={{0,1},{1,0},{2,3},{3,2},{4,5},{5,4},{6,7},{7,6},{8,9},{9,8},{10,11... | collective-permute-start | bytes 786440 | tf_op jit(solution)/shard_map/ppermute | solution.py:209
  43.5 25.4 %copy-start.30 = (f32[2,2,32,256]{3,2,1,0:T(8,128)}, f32[2,2,32,256]{3,2,1,0:T(8,128)S(1)}, u32[]{:S(2)}) copy-start(f32[2,2,32,256]{3,2,1,0:T(8,128)S(1)} %get-tuple-element.51.h_ref) | copy-start | bytes 393220
  71.8 18.4 %all-to-all-start.2 = ((f32[32,8,128]{2,1,0:T(8,128)}), f32[32,8,128]{2,1,0:T(8,128)}, u32[]{:S(2)}, u32[]{:S(2)}) async-start(f32[32,8,128]{2,1,0:T(8,128)} %copy-done.38), calls=%async_computation.2 | async-start | bytes 262144 | tf_op jit(solution)/shard_map/all_to_all | solution.py:245
  82.5 10.0 %collective-permute-start.6 = (bf16[2,256,256]{2,1,0:T(8,128)(2,1)}, bf16[2,256,256]{2,1,0:T(8,128)(2,1)}, u32[]{:S(2)}, u32[]{:S(2)}) collective-permute-start(bf16[2,256,256]{2,1,0:T(8,128)(2,1)} %copy-done.45), channel_id=1, source_target_pairs={{0,1},{1,0},{2,3},{3,2},{4,5},{5,4},{6,7},{7,6},{8,9},{9,8},{10,11... | collective-permute-start | bytes 786440 | tf_op jit(solution)/shard_map/ppermute | solution.py:209
  82.9 9.6 %collective-permute-start.7 = (bf16[2,256,256]{2,1,0:T(8,128)(2,1)}, bf16[2,256,256]{2,1,0:T(8,128)(2,1)}, u32[]{:S(2)}, u32[]{:S(2)}) collective-permute-start(bf16[2,256,256]{2,1,0:T(8,128)(2,1)} %copy-done.44), channel_id=1, source_target_pairs={{1,2},{3,4},{5,6},{7,8},{9,10},{11,12},{13,14},{15,16},{17,18},{19... | collective-permute-start | bytes 786440 | tf_op jit(solution)/shard_map/ppermute | solution.py:209
  91.8 6.7 %copy-start.4 = (bf16[4,2,256,256]{3,2,1,0:T(8,128)(2,1)S(1)}, bf16[4,2,256,256]{3,2,1,0:T(8,128)(2,1)}, u32[]{:S(2)}) copy-start(bf16[4,2,256,256]{3,2,1,0:T(8,128)(2,1)} %left_ref.9) | copy-start | bytes 3145732
  102.1 22.1 %all-to-all-start.3 = ((bf16[8,2,2,32,256]{4,3,2,1,0:T(8,128)(2,1)}), bf16[8,2,2,32,256]{4,3,2,1,0:T(8,128)(2,1)}, u32[]{:S(2)}, u32[]{:S(2)}) async-start(bf16[8,2,2,32,256]{4,3,2,1,0:T(8,128)(2,1)} %copy-done.22), calls=%async_computation.3 | async-start | bytes 1048576 | tf_op jit(solution)/shard_map/all_to_all | solution.py:245
  126.8 22.1 %all-to-all-start.4 = ((bf16[8,128,256]{2,1,0:T(8,128)(2,1)}), bf16[8,128,256]{2,1,0:T(8,128)(2,1)}, u32[]{:S(2)}, u32[]{:S(2)}) async-start(bf16[8,128,256]{2,1,0:T(8,128)(2,1)} %copy-done.29), calls=%async_computation.4 | async-start | bytes 1048576 | tf_op jit(solution)/shard_map/all_to_all | solution.py:245
  148.9 12.9 %copy-start.2 = (bf16[2,4,256,256]{3,2,1,0:T(8,128)(2,1)S(1)}, bf16[2,4,256,256]{3,2,1,0:T(8,128)(2,1)}, u32[]{:S(2)}) copy-start(bf16[2,4,256,256]{3,2,1,0:T(8,128)(2,1)} %copy-done) | copy-start | bytes 3145732
  148.9 13.0 %copy-start.6 = (bf16[4,2,256,256]{3,2,1,0:T(8,128)(2,1)S(1)}, bf16[4,2,256,256]{3,2,1,0:T(8,128)(2,1)}, u32[]{:S(2)}) copy-start(bf16[4,2,256,256]{3,2,1,0:T(8,128)(2,1)} %left_ref.9) | copy-start | bytes 3145732
  148.9 13.0 %copy-start.9 = (bf16[2,4,256,256]{3,2,1,0:T(8,128)(2,1)S(1)}, bf16[2,4,256,256]{3,2,1,0:T(8,128)(2,1)}, u32[]{:S(2)}) copy-start(bf16[2,4,256,256]{3,2,1,0:T(8,128)(2,1)} %copy-done.7) | copy-start | bytes 3145732
  150.2 3.0 %collective-permute-start.8 = (bf16[2,256,256]{2,1,0:T(8,128)(2,1)S(1)}, bf16[2,256,256]{2,1,0:T(8,128)(2,1)S(1)}, u32[]{:S(2)}, u32[]{:S(2)}) collective-permute-start(bf16[2,256,256]{2,1,0:T(8,128)(2,1)S(1)} %get-tuple-element.57), channel_id=1, source_target_pairs={{0,1},{1,0},{2,3},{3,2},{4,5},{5,4},{6,7},{7,6},{8,9},{9,8},{10,11... | collective-permute-start | bytes 786440 | tf_op jit(solution)/shard_map/ppermute | solution.py:209
  150.9 7.7 %collective-permute-start.9 = (bf16[2,256,256]{2,1,0:T(8,128)(2,1)S(1)}, bf16[2,256,256]{2,1,0:T(8,128)(2,1)S(1)}, u32[]{:S(2)}, u32[]{:S(2)}) collective-permute-start(bf16[2,256,256]{2,1,0:T(8,128)(2,1)S(1)} %get-tuple-element.58), channel_id=1, source_target_pairs={{1,2},{3,4},{5,6},{7,8},{9,10},{11,12},{13,14},{15,16},{17,18},{19... | collective-permute-start | bytes 786440 | tf_op jit(solution)/shard_map/ppermute | solution.py:209
  164.2 24.2 %copy-start.32 = (f32[2,2,32,256]{3,2,1,0:T(8,128)S(1)}, f32[2,2,32,256]{3,2,1,0:T(8,128)}, u32[]{:S(2)}) copy-start(f32[2,2,32,256]{3,2,1,0:T(8,128)} %copy-done.30) | copy-start | bytes 393220
  164.2 24.2 %copy-start.35 = (f32[2,2,32,256]{3,2,1,0:T(8,128)S(1)}, f32[2,2,32,256]{3,2,1,0:T(8,128)}, u32[]{:S(2)}) copy-start(f32[2,2,32,256]{3,2,1,0:T(8,128)} %copy-done.33) | copy-start | bytes 393220
  (43 other events, 58.5 us)

commit v4 on v3

--- a/solution.py
+++ b/solution.py
@@ -6,6 +6,7 @@
 from jax.experimental import pallas as pl
 from jax.experimental.pallas import tpu as pltpu
 from jax.sharding import PartitionSpec as P
+
 
 BF = jnp.bfloat16
 F32 = jnp.float32
@@ -121,18 +122,41 @@
     return own + [core_ref[u], chip_ref[u]]
 
 
-def form_kernel(coef_ref, got_ref, core_ref, chip_ref, start_ref, pre_ref, pre_core, pre_chip, dir_ref, mdir_ref):
+def form_kernel(row_ref, got_ref, core_ref, chip_ref, start_ref, pre_ref, pre_core, pre_chip, dir_ref, mdir_ref, coef_ref):
     vecs, slots, states, _ = dir_ref.shape
     share = states // got_ref.shape[0]
-    for u in range(vecs):
+    row = row_ref[0]
+    for i in range(1, row_ref.shape[0]):
+        row = row + row_ref[i]
+    row = row[0:1]
+    lane = lax.broadcasted_iota(jnp.int32, row.shape, 1)
+    index = lax.broadcasted_iota(jnp.int32, coef_ref.shape, 0)
+    lanes = lax.broadcasted_iota(jnp.int32, coef_ref.shape, 1)
+    table = jnp.zeros(coef_ref.shape, F32)
+    for u in range(vecs):
+        total = [
+            jnp.sum(jnp.where(lane == i * vecs + u, row, 0.0), axis=1, keepdims=True)
+            for i in range(8)
+        ]
+        scale = 1.0 / jnp.sqrt(total[0] + 1e-06)
+        vv, vh, vmv, vmh, hmh, mvmv, mvmh, mhmh = [x * (scale * scale) for x in total]
+        correlation = vmh - vh * vmv
+        square = mhmh - 2.0 * vh * mvmh + vh * vh * mvmv
+        square = square - 2.0 * correlation * (vmh - vh * vmv) + correlation * correlation * vv
+        norm = jnp.sqrt(jnp.maximum(square, 0.0) + 1e-06)
+        coupling = (hmh - vh * vmh - correlation * vh) / norm
+        alpha = scale / norm
+        for j, x in enumerate([vh, correlation, alpha, scale, coupling, norm]):
+            table = table + jnp.where((index == j) & (lanes == u), x, 0.0)
         hs = slot_blocks(got_ref, core_ref, chip_ref, u, share)
         for i in range(slots):
             m = (pre_ref[0], pre_ref[1], pre_core[0], pre_chip[0])[i]
             v = start_ref[u, i].astype(F32)
-            raw = m * (hs[i].astype(F32) - coef_ref[0, u] * v) - coef_ref[1, u] * v
-            small = (raw * coef_ref[2, u]).astype(BF)
+            raw = m * (hs[i].astype(F32) - vh * v) - correlation * v
+            small = (raw * alpha).astype(BF)
             dir_ref[u, i] = small
             mdir_ref[u, i] = (m * small.astype(F32)).astype(BF)
+    coef_ref[...] = table
 
 
 def lift_kernel(got_ref, core_ref, chip_ref, pre_ref, pre_core, pre_chip, out_ref):
@@ -156,12 +180,13 @@
 def gram_kernel(coef_ref, start_ref, h_ref, hd_ref, pre_ref, dot_ref, dir_ref):
     vecs, blocks = h_ref.shape[:2]
     for u in range(vecs):
+        rayleigh, correlation, alpha, scale = [coef_ref[j : j + 1, u : u + 1] for j in range(4)]
         for b in range(blocks):
             m = pre_ref[b]
             v, h = start_ref[u, b].astype(F32), h_ref[u, b]
-            d = (m * (h - coef_ref[0, u] * v) - coef_ref[1, u] * v) * coef_ref[2, u]
+            d = (m * (h - rayleigh * v) - correlation * v) * alpha
             dir_ref[u, b] = d
-            basis = [v * coef_ref[3, u], d, h * coef_ref[3, u], hd_ref[u, b]]
+            basis = [v * scale, d, h * scale, hd_ref[u, b]]
             lifted = [m * x for x in basis]
             products = [basis[i] * basis[j] for i, j in PLAIN]
             products += [basis[i] * lifted[j] for i, j in PAIRS]
@@ -206,15 +231,14 @@
     chip_pairs = chip_pairs + [(j, i) for i, j in chip_pairs]
 
     def swap(inner, outer):
-        return lax.ppermute(inner, "sec", core_pairs), lax.ppermute(outer, "sec", chip_pairs)
+        outer = lax.ppermute(outer, "sec", chip_pairs)
+        inner = lax.ppermute(inner, "sec", core_pairs)
+        return inner, outer
 
     def edges(x, axis):
         inner = lax.dynamic_index_in_dim(x, 1 - core, axis, keepdims=True)
         outer = lax.dynamic_index_in_dim(x, core, axis, keepdims=True)
-        return swap(inner, outer)
-
-    def with_edges(x, axis):
-        return jnp.concatenate([x, *edges(x, axis)], axis=axis)
+        return inner, outer
 
     def rows(x, axis):
         return lax.dynamic_slice_in_dim(x, term * share, share, axis)
@@ -244,23 +268,23 @@
     def exchange(parts, axis="term"):
         return lax.all_to_all(parts, axis, 0, 0)
 
-    start = jnp.where(mask[None], start_vectors, jnp.zeros((), BF))
-    right_all = with_edges(right_env, 1)
-    start_all = with_edges(start, 1)
-    mask_rows = rows(mask.astype(F32), 1)
-    pre = rows(precond, 1)
-    vec = rows(start, 2)
+    barrier = lax.optimization_barrier
+
     slice_shape = shape((vecs, blocks, share, states), F32)
     edge_shape = shape((vecs, states, states), BF)
     four_shape = shape((vecs, 4, states, states), BF)
     lines = vecs * blocks * share
 
-    parts, pre_late = lax.optimization_barrier((apply_op(start_all), precond))
+    right_all = jnp.concatenate([right_env, *swap(*edges(right_env, 1))], axis=1)
+    start = jnp.where(mask[None], start_vectors, jnp.zeros((), BF))
+    start_all = jnp.concatenate([start, *swap(*edges(start, 1))], axis=1)
+    early = (rows(mask.astype(F32), 1), rows(precond, 1), rows(start, 2), *edges(precond, 0))
+    start_all, right_all, early = barrier((start_all, right_all, early))
+    mask_rows, pre, vec, pre_inner, pre_outer = early
+
+    parts, pre_inner, pre_outer = barrier((apply_op(start_all), pre_inner, pre_outer))
+    pre_core, pre_chip = swap(pre_inner, pre_outer)
     got = exchange(parts)
-    pre_core, pre_chip = edges(pre_late, 0)
-    (m_start,) = call(lift_start_kernel, [four_shape], [start_all, precond, pre_core, pre_chip])
-    got, m_start, pre_core, pre_chip = lax.optimization_barrier((got, m_start, pre_core, pre_chip))
-
     h_raw, body = call(
         functools.partial(settle_kernel, factor),
         [slice_shape, shape((groups, lines + EXTRA, states), BF)],
@@ -271,60 +295,44 @@
         unpack_kernel, [edge_shape, edge_shape, shape((sec, 8, 128), F32)], [core_id, got], smem=1
     )
     h_core, h_chip = swap(inner, outer)
-    row = jnp.sum(exchange(row, "sec"), axis=0)[0, : 8 * vecs]
-    total = row.reshape(8, vecs)
-    scale = 1.0 / jnp.sqrt(total[0] + 1e-06)
-    vv, vh, vmv, vmh, hmh, mvmv, mvmh, mhmh = total * scale**2
-    correlation = vmh - vh * vmv
-    square = (
-        mhmh
-        - 2.0 * vh * mvmh
-        + vh**2 * mvmv
-        - 2.0 * correlation * (vmh - vh * vmv)
-        + correlation**2 * vv
-    )
-    dir_norm = jnp.sqrt(jnp.maximum(square, 0.0) + 1e-06)
-    coupling = (hmh - vh * vmh - correlation * vh) / dir_norm
-    rayleigh = vh
-    coef = jnp.stack([rayleigh, correlation, scale / dir_norm, scale])
-
-    dir_all, m_dir = call(
+    row = exchange(row, "sec")
+    row, pre_core, pre_chip = barrier((row, pre_core, pre_chip))
+    dir_all, m_dir, coef = call(
         form_kernel,
-        [four_shape, four_shape],
-        [coef, got, h_core, h_chip, start_all, precond, pre_core, pre_chip],
-        smem=1,
-    )
-    got = exchange(apply_op(dir_all))
-    known = [m_start, m_dir, dir_all, start_all]
-    h_m_start, dots_start = apply_op(m_start, known)
-    h_m_dir, dots_dir = apply_op(m_dir, known)
-    got, h_m_start, h_m_dir, dots_start, dots_dir = lax.optimization_barrier(
-        (got, h_m_start, h_m_dir, dots_start, dots_dir)
-    )
+        [four_shape, four_shape, shape((16, 128), F32)],
+        [row, got, h_core, h_chip, start_all, precond, pre_core, pre_chip],
+    )
+    parts, dir_all, m_dir = barrier((apply_op(dir_all), dir_all, m_dir))
+    got = exchange(parts)
     h_dir, body = call(
         functools.partial(settle_kernel, factor),
         [slice_shape, shape((groups, lines, states), BF)],
         [got, mask_rows],
     )
     got = exchange(body)
+    got, h_dir, m_dir, start_all = barrier((got, h_dir, m_dir, start_all))
+    inner, outer = call(unpack_kernel, [edge_shape, edge_shape], [core_id, got], smem=1)
+    hd_core, hd_chip = swap(inner, outer)
+    (m_start,) = call(lift_start_kernel, [four_shape], [start_all, precond, pre_core, pre_chip])
+    known = [m_start, m_dir, dir_all, start_all]
+    h_m_start, dots_start = apply_op(m_start, known)
+    h_m_dir, dots_dir = apply_op(m_dir, known)
     gram, direction = call(
         gram_kernel,
         [shape((len(PLAIN) + 2 * len(PAIRS), vecs, 8, 128), F32), slice_shape],
         [coef, vec, h_raw, h_dir, pre],
-        smem=1,
-    )
-    got, gram, direction = lax.optimization_barrier((got, gram, direction))
-    inner, outer = call(unpack_kernel, [edge_shape, edge_shape], [core_id, got], smem=1)
-    hd_core, hd_chip = swap(inner, outer)
+    )
     (m_hd,) = call(lift_kernel, [four_shape], [got, hd_core, hd_chip, precond, pre_core, pre_chip])
     dots_hd = apply_op(m_hd, [m_hd] + known, [h_m_start, h_m_dir], keep=False)
+    rayleigh, correlation, _, scale, coupling, dir_norm = [coef[j, :vecs] for j in range(6)]
 
     tiles = jnp.concatenate([gram, dots_hd, dots_start, dots_dir])
     total = jnp.sum(tiles, axis=(2, 3)) * factor
     count = total.size
     everyone = groups * sec
     row = jnp.pad(total.reshape(-1), (0, 128 - count))[None]
-    row = exchange(jnp.broadcast_to(row[None], (everyone,) + row.shape), ("term", "sec"))
+    row = jnp.broadcast_to(row[None], (everyone,) + row.shape)
+    row = exchange(row, ("term", "sec"))
     total = jnp.sum(row, axis=0)[0, :count].reshape(total.shape)
     one = {p: total[i] for i, p in enumerate(PLAIN)}
     first = {p: total[len(PLAIN) + i] for i, p in enumerate(PAIRS)}

time: 192 us -> 175 us (0.911)
  blocking collectives: 46.3 us -> 77.4 us
  local copies, waits for them, and re-layouts: 35.8 us -> 6.42 us
  waiting for transfers between devices: 37.7 us -> 18.1 us
  starting transfers between devices: 45 us -> 48.3 us
    all_to_all x2 -> x4, blocking collectives: 46.3 us -> 77.4 us  [exchange(): return lax.all_to_all(parts, axis, 0, 0)]
    unnamed x108 -> x36, local copies, waits for them, and re-layouts: 30.7 us -> 3.95 us
    ppermute x10, starting transfers between devices: 18.8 us -> 37 us  [the longest x5 32.4 us: swap(): outer = lax.ppermute(outer, 'sec', chip_pairs)]
    all_to_all x4 -> x2, starting transfers between devices: 26.2 us -> 11.2 us  [exchange(): return lax.all_to_all(parts, axis, 0, 0)]
    all_to_all x4 -> x2, waiting for transfers between devices: 23.4 us -> 11.8 us  [exchange(): return lax.all_to_all(parts, axis, 0, 0)]
    ppermute x10, waiting for transfers between devices: 14.3 us -> 6.29 us  [the longest x5 6.28 us: swap(): outer = lax.ppermute(outer, 'sec', chip_pairs)]
    dynamic_slice x2, local copies, waits for them, and re-layouts: 2.32 us -> 0.02 us  [rows(): return lax.dynamic_slice_in_dim(x, term * share, share, axis)]
  transfers between devices with their start and end apart: 14 -> 12, of which waited for: 8 -> 3; matrix products, arithmetic and copies ran while one was open for 4% -> 1% of each run, Pallas kernels for 3% -> 4%
where the time goes in v4:
time: 175 us; the launch traced here: 174 us
  blocking collectives  77.4 us (44%)
  starting transfers between devices  48.3 us (28%)
  Pallas kernels  18.2 us (10%)
  waiting for transfers between devices  18.1 us (10%)
  local copies, waits for them, and re-layouts  6.42 us (4%)
  other arithmetic  4.61 us (3%)
    all_to_all x4, blocking collectives, exchange(): return lax.all_to_all(parts, axis, 0, 0)  77.4 us
    ppermute x5, starting transfers between devices, swap(): outer = lax.ppermute(outer, 'sec', chip_pairs)  32.4 us
    pallas_call x13, Pallas kernels, call(): pl.pallas_call(kernel, out_shape=[jax.ShapeDtypeStruct(x.shape, x.dtype)...  18.2 us
    all_to_all x2, waiting for transfers between devices, exchange(): return lax.all_to_all(parts, axis, 0, 0)  11.8 us
    all_to_all x2, starting transfers between devices, exchange(): return lax.all_to_all(parts, axis, 0, 0)  11.2 us
    ppermute x5, waiting for transfers between devices, swap(): outer = lax.ppermute(outer, 'sec', chip_pairs)  6.28 us
    ppermute x5, starting transfers between devices, swap(): inner = lax.ppermute(inner, 'sec', core_pairs)  4.63 us
    unnamed x36, local copies, waits for them, and re-layouts  3.95 us
  transfers between devices with their start and end apart: 12, of which 3 were waited for; matrix products, arithmetic and copies ran while one was open for 1% of the time, Pallas kernels for 4%

profile of v4, /device:TPU:1, one launch (start us, length us, event | category | flops | bytes accessed | tf_op | source)
XLA Modules:
  0.0 174.1 jit_solution(13366081548919107067)
XLA Ops:
  2.1 3.3 %collective-permute-start.2 = (bf16[4,1,256,256]{3,2,1,0:T(8,128)(2,1)S(1)}, bf16[4,1,256,256]{3,2,1,0:T(8,128)(2,1)}, u32[]{:S(2)}, u32[]{:S(2)}) collective-permute-start(bf16[4,1,256,256]{3,2,1,0:T(8,128)(2,1)S(1)} %get-tuple-element.89), channel_id=1, source_target_pairs={{0,1},{1,0},{2,3},{3,2},{4,5},{5,4},{6,7},{7,6},{8,9},{9,8},{10,11... | collective-permute-start | bytes 1572872 | tf_op jit(solution)/shard_map/ppermute | solution.py:235
  5.3 1.9 %collective-permute-start.3 = (bf16[4,1,256,256]{3,2,1,0:T(8,128)(2,1)S(1)}, bf16[4,1,256,256]{3,2,1,0:T(8,128)(2,1)}, u32[]{:S(2)}, u32[]{:S(2)}) collective-permute-start(bf16[4,1,256,256]{3,2,1,0:T(8,128)(2,1)S(1)} %get-tuple-element.90), channel_id=1, source_target_pairs={{1,2},{3,4},{5,6},{7,8},{9,10},{11,12},{13,14},{15,16},{17,18},{19... | collective-permute-start | bytes 1572872 | tf_op jit(solution)/shard_map/ppermute | solution.py:234
  7.7 3.6 %collective-permute-start.1 = (bf16[2,1,256,256]{3,2,1,0:T(8,128)(2,1)S(1)}, bf16[2,1,256,256]{3,2,1,0:T(8,128)(2,1)S(1)}, u32[]{:S(2)}, u32[]{:S(2)}) collective-permute-start(bf16[2,1,256,256]{3,2,1,0:T(8,128)(2,1)S(1)} %get-tuple-element.94), channel_id=1, source_target_pairs={{1,2},{3,4},{5,6},{7,8},{9,10},{11,12},{13,14},{15,16},{17,18},{19... | collective-permute-start | bytes 786440 | tf_op jit(solution)/shard_map/ppermute | solution.py:234
  12.4 6.3 %collective-permute-done.1 = bf16[2,1,256,256]{3,2,1,0:T(8,128)(2,1)S(1)} collective-permute-done((bf16[2,1,256,256]{3,2,1,0:T(8,128)(2,1)S(1)}, bf16[2,1,256,256]{3,2,1,0:T(8,128)(2,1)S(1)}, u32[]{:S(2)}, u32[]{:S(2)}) %collective-permute-start.1) | collective-permute-done | bytes 262176 | tf_op jit(solution)/shard_map/ppermute | solution.py:234
  18.8 1.9 %pad_maximum_fusion.right_ref = bf16[4,4,256,256]{3,2,1,0:T(8,128)(2,1)S(1)} fusion(bf16[4,1,256,256]{3,2,1,0:T(8,128)(2,1)} %collective-permute-done.3, bf16[4,1,256,256]{3,2,1,0:T(8,128)(2,1)} %collective-permute-done.2, bf16[4,2,256,256]{3,2,1,0:T(8,128)(2,1)} %param.8), kind=kLoop, calls=%fused_computation | loop fusion | flops 2097152 | bytes 4194304 | tf_op jit(solution)/shard_map/concatenate | solution.py:278
  20.7 1.9 %shard_map.77 = bf16[8,2,2,32,256]{4,3,2,1,0:T(8,128)(2,1)S(1)} custom-call(s32[4,2]{1,0:T(4,128)S(1)} %fusion.slot_ref, bf16[2,4,256,256]{3,2,1,0:T(8,128)(2,1)S(1)} %pad_maximum_fusion.1.x_ref.start_ref.refs_3_.refs_4_, bf16[4,4,256,256]{3,2,1,0:T(8,128)(2,1)S(1)} %pad_maximum_fusion.right_ref, bf16[4,2,256,256]{3,2,1,0:T(8,128)(2,1)S(1)} %copy-done), custom_call_target="tpu_custom_call" | custom-call | flops 1073741824 | bytes 4718624 | tf_op jit(solution)/shard_map/pallas_call | solution.py:203
  22.5 18.4 %all_to_all.30.got_ref = bf16[8,2,2,32,256]{4,3,2,1,0:T(8,128)(2,1)S(1)} all-to-all(bf16[8,2,2,32,256]{4,3,2,1,0:T(8,128)(2,1)S(1)} %shard_map.77), channel_id=1, replica_groups=mesh['term'=8,'sec'=32] {'term'}, dimensions={0} | all-to-all | bytes 1048576 | tf_op jit(solution)/shard_map/all_to_all | solution.py:269
  42.8 4.2 %all-to-all-start.1 = ((bf16[8,144,256]{2,1,0:T(8,128)(2,1)}), bf16[8,144,256]{2,1,0:T(8,128)(2,1)}, u32[]{:S(2)}, u32[]{:S(2)}) async-start(bf16[8,144,256]{2,1,0:T(8,128)(2,1)} %copy-done.4), calls=%async_computation.1 | async-start | bytes 1179648 | tf_op jit(solution)/shard_map/all_to_all | solution.py:269
  47.1 9.3 %collective-permute-start.5 = (f32[1,256,256]{2,1,0:T(8,128)}, f32[1,256,256]{2,1,0:T(8,128)}, u32[]{:S(2)}, u32[]{:S(2)}) collective-permute-start(f32[1,256,256]{2,1,0:T(8,128)} %get-tuple-element.51), channel_id=1, source_target_pairs={{1,2},{3,4},{5,6},{7,8},{9,10},{11,12},{13,14},{15,16},{17,18},{19... | collective-permute-start | bytes 786440 | tf_op jit(solution)/shard_map/ppermute | solution.py:234
  56.4 4.2 %all-to-all-done.1.got_ref = bf16[8,144,256]{2,1,0:T(8,128)(2,1)} async-done(((bf16[8,144,256]{2,1,0:T(8,128)(2,1)}), bf16[8,144,256]{2,1,0:T(8,128)(2,1)}, u32[]{:S(2)}, u32[]{:S(2)}) %all-to-all-start.1) | async-done | bytes 589856 | tf_op jit(solution)/shard_map/all_to_all | solution.py:269
  60.6 1.9 %shard_map.79 = (bf16[2,256,256]{2,1,0:T(8,128)(2,1)}, bf16[2,256,256]{2,1,0:T(8,128)(2,1)}, f32[32,8,128]{2,1,0:T(8,128)S(1)}) custom-call(s32[1]{0:T(128)} %bitcast.core_ref, bf16[8,144,256]{2,1,0:T(8,128)(2,1)} %all-to-all-done.1.got_ref), custom_call_target="tpu_custom_call" | custom-call | bytes 1245188 | tf_op jit(solution)/shard_map/pallas_call | solution.py:203
  63.1 15.1 %collective-permute-start.7 = (bf16[2,256,256]{2,1,0:T(8,128)(2,1)}, bf16[2,256,256]{2,1,0:T(8,128)(2,1)}, u32[]{:S(2)}, u32[]{:S(2)}) collective-permute-start(bf16[2,256,256]{2,1,0:T(8,128)(2,1)} %get-tuple-element.54), channel_id=1, source_target_pairs={{1,2},{3,4},{5,6},{7,8},{9,10},{11,12},{13,14},{15,16},{17,18},{19... | collective-permute-start | bytes 786440 | tf_op jit(solution)/shard_map/ppermute | solution.py:234
  78.3 7.0 %all-to-all-start.2 = ((f32[32,8,128]{2,1,0:T(8,128)}), f32[32,8,128]{2,1,0:T(8,128)}, u32[]{:S(2)}, u32[]{:S(2)}) async-start(f32[32,8,128]{2,1,0:T(8,128)} %copy-done.13), calls=%async_computation.2 | async-start | bytes 262144 | tf_op jit(solution)/shard_map/all_to_all | solution.py:269
  85.3 7.6 %all-to-all-done.2.row_ref = f32[32,8,128]{2,1,0:T(8,128)} async-done(((f32[32,8,128]{2,1,0:T(8,128)}), f32[32,8,128]{2,1,0:T(8,128)}, u32[]{:S(2)}, u32[]{:S(2)}) %all-to-all-start.2) | async-done | bytes 131104 | tf_op jit(solution)/shard_map/all_to_all | solution.py:269
  94.1 2.8 %shard_map.80 = (bf16[2,4,256,256]{3,2,1,0:T(8,128)(2,1)S(1)}, bf16[2,4,256,256]{3,2,1,0:T(8,128)(2,1)S(1)}, f32[16,128]{1,0:T(8,128)S(1)}) custom-call(f32[32,8,128]{2,1,0:T(8,128)} %all-to-all-done.2.row_ref, bf16[8,144,256]{2,1,0:T(8,128)(2,1)} %all-to-all-done.1.got_ref, bf16[2,256,256]{2,1,0:T(8,128)(2,1)} %collective-permute-done.6.core_ref, ...), custom_call_target="tpu_custom_call" | custom-call | bytes 5447680 | tf_op jit(solution)/shard_map/pallas_call | solution.py:203
  96.9 1.9 %shard_map.81 = bf16[8,2,2,32,256]{4,3,2,1,0:T(8,128)(2,1)S(1)} custom-call(s32[4,2]{1,0:T(4,128)S(1)} %fusion.slot_ref, bf16[2,4,256,256]{3,2,1,0:T(8,128)(2,1)S(1)} %get-tuple-element.72.x_ref.refs_2_.refs_3_, bf16[4,4,256,256]{3,2,1,0:T(8,128)(2,1)S(1)} %pad_maximum_fusion.right_ref, bf16[4,2,256,256]{3,2,1,0:T(8,128)(2,1)S(1)} %copy-done.1), custom_call_target="tpu_custom_call" | custom-call | flops 1073741824 | bytes 4718624 | tf_op jit(solution)/shard_map/pallas_call | solution.py:203
  98.8 20.3 %all_to_all.31.got_ref = bf16[8,2,2,32,256]{4,3,2,1,0:T(8,128)(2,1)S(1)} all-to-all(bf16[8,2,2,32,256]{4,3,2,1,0:T(8,128)(2,1)S(1)} %shard_map.81), channel_id=1, replica_groups=mesh['term'=8,'sec'=32] {'term'}, dimensions={0} | all-to-all | bytes 1048576 | tf_op jit(solution)/shard_map/all_to_all | solution.py:269
  119.2 19.8 %all_to_all.32.got_ref = bf16[8,128,256]{2,1,0:T(8,128)(2,1)S(1)} all-to-all(bf16[8,128,256]{2,1,0:T(8,128)(2,1)S(1)} %get-tuple-element.62), channel_id=1, replica_groups=mesh['term'=8,'sec'=32] {'term'}, dimensions={0} | all-to-all | bytes 1048576 | tf_op jit(solution)/shard_map/all_to_all | solution.py:269
  140.2 2.4 %collective-permute-start.9 = (bf16[2,256,256]{2,1,0:T(8,128)(2,1)S(1)}, bf16[2,256,256]{2,1,0:T(8,128)(2,1)S(1)}, u32[]{:S(2)}, u32[]{:S(2)}) collective-permute-start(bf16[2,256,256]{2,1,0:T(8,128)(2,1)S(1)} %get-tuple-element.69), channel_id=1, source_target_pairs={{1,2},{3,4},{5,6},{7,8},{9,10},{11,12},{13,14},{15,16},{17,18},{19... | collective-permute-start | bytes 786440 | tf_op jit(solution)/shard_map/ppermute | solution.py:234
  144.9 2.1 %shard_map.87 = (bf16[2,2,256,256]{3,2,1,0:T(8,128)(2,1)S(1)}, f32[4,2,8,128]{3,2,1,0:T(8,128)S(1)}) custom-call(s32[4,2]{1,0:T(4,128)S(1)} %fusion.slot_ref, bf16[2,4,256,256]{3,2,1,0:T(8,128)(2,1)S(1)} %shard_map.86.x_ref.refs_0_.refs_1_, bf16[4,4,256,256]{3,2,1,0:T(8,128)(2,1)S(1)} %pad_maximum_fusion.right_ref, bf16[4,2,256,256]{3,2,1,0:T(8,128)(2,1)S(1)} %copy-done.1, ...), custom_call_target="tpu_custom_call" | custom-call | flops 1073741824 | bytes 8945696 | tf_op jit(solution)/shard_map/pallas_call | solution.py:203
  147.0 2.1 %shard_map.88 = (bf16[2,2,256,256]{3,2,1,0:T(8,128)(2,1)S(1)}, f32[4,2,8,128]{3,2,1,0:T(8,128)S(1)}) custom-call(s32[4,2]{1,0:T(4,128)S(1)} %fusion.slot_ref, bf16[2,4,256,256]{3,2,1,0:T(8,128)(2,1)S(1)} %get-tuple-element.71.refs_1_.x_ref.refs_2_, bf16[4,4,256,256]{3,2,1,0:T(8,128)(2,1)S(1)} %pad_maximum_fusion.right_ref, ...), custom_call_target="tpu_custom_call" | custom-call | flops 1073741824 | bytes 8945696 | tf_op jit(solution)/shard_map/pallas_call | solution.py:203
  150.4 2.3 %shard_map.89 = f32[7,2,8,128]{3,2,1,0:T(8,128)S(1)} custom-call(s32[4,2]{1,0:T(4,128)S(1)} %fusion.slot_ref, bf16[2,4,256,256]{3,2,1,0:T(8,128)(2,1)S(1)} %shard_map.85.x_ref.refs_0_, bf16[4,4,256,256]{3,2,1,0:T(8,128)(2,1)S(1)} %pad_maximum_fusion.right_ref, bf16[4,2,256,256]{3,2,1,0:T(8,128)(2,1)S(1)} %copy-done.1, ...), custom_call_target="tpu_custom_call" | custom-call | flops 1073741824 | bytes 10543136 | tf_op jit(solution)/shard_map/pallas_call | solution.py:203
  153.1 18.8 %all_to_all.33 = f32[256,1,128]{2,1,0:T(1,128)S(1)} all-to-all(f32[256,1,128]{2,1,0:T(1,128)S(1)} %broadcast_in_dim.25), channel_id=1, replica_groups=mesh['term'=8,'sec'=32] {'term','sec'}, dimensions={0} | all-to-all | bytes 262144 | tf_op jit(solution)/shard_map/all_to_all | solution.py:269
  172.4 1.7 multiply_add_fusion
  (76 shorter events, 12.0 us)
Async XLA Ops:
  0.6 6.6 %copy-start.17 = (s32[2]{0:T(128)S(1)}, s32[2]{0:T(128)}, u32[]{:S(2)}) copy-start(s32[2]{0:T(128)} %param.11) | copy-start | bytes 28
  0.6 6.9 %copy-start.14 = (bf16[2,2,256,256]{3,2,1,0:T(8,128)(2,1)S(1)}, bf16[2,2,256,256]{3,2,1,0:T(8,128)(2,1)}, u32[]{:S(2)}) copy-start(bf16[2,2,256,256]{3,2,1,0:T(8,128)(2,1)} %param.6) | copy-start | bytes 1572868
  0.7 10.7 %copy-start.2 = (f32[2,256,256]{2,1,0:T(8,128)S(1)}, f32[2,256,256]{2,1,0:T(8,128)}, u32[]{:S(2)}) copy-start(f32[2,256,256]{2,1,0:T(8,128)} %pre_ref.5) | copy-start | bytes 1572868
  2.0 10.2 %copy-start.16 = (s32[4]{0:T(128)S(1)}, s32[4]{0:T(128)}, u32[]{:S(2)}) copy-start(s32[4]{0:T(128)} %param.9) | copy-start | bytes 52
  2.1 16.7 %collective-permute-start.2 = (bf16[4,1,256,256]{3,2,1,0:T(8,128)(2,1)S(1)}, bf16[4,1,256,256]{3,2,1,0:T(8,128)(2,1)}, u32[]{:S(2)}, u32[]{:S(2)}) collective-permute-start(bf16[4,1,256,256]{3,2,1,0:T(8,128)(2,1)S(1)} %get-tuple-element.89), channel_id=1, source_target_pairs={{0,1},{1,0},{2,3},{3,2},{4,5},{5,4},{6,7},{7,6},{8,9},{9,8},{10,11... | collective-permute-start | bytes 1572872 | tf_op jit(solution)/shard_map/ppermute | solution.py:235
  5.3 13.4 %collective-permute-start.3 = (bf16[4,1,256,256]{3,2,1,0:T(8,128)(2,1)S(1)}, bf16[4,1,256,256]{3,2,1,0:T(8,128)(2,1)}, u32[]{:S(2)}, u32[]{:S(2)}) collective-permute-start(bf16[4,1,256,256]{3,2,1,0:T(8,128)(2,1)S(1)} %get-tuple-element.90), channel_id=1, source_target_pairs={{1,2},{3,4},{5,6},{7,8},{9,10},{11,12},{13,14},{15,16},{17,18},{19... | collective-permute-start | bytes 1572872 | tf_op jit(solution)/shard_map/ppermute | solution.py:234
  7.6 4.8 %collective-permute-start = (bf16[2,1,256,256]{3,2,1,0:T(8,128)(2,1)S(1)}, bf16[2,1,256,256]{3,2,1,0:T(8,128)(2,1)S(1)}, u32[]{:S(2)}, u32[]{:S(2)}) collective-permute-start(bf16[2,1,256,256]{3,2,1,0:T(8,128)(2,1)S(1)} %get-tuple-element.93), channel_id=1, source_target_pairs={{0,1},{1,0},{2,3},{3,2},{4,5},{5,4},{6,7},{7,6},{8,9},{9,8},{10,11... | collective-permute-start | bytes 786440 | tf_op jit(solution)/shard_map/ppermute | solution.py:235
  7.7 10.9 %collective-permute-start.1 = (bf16[2,1,256,256]{3,2,1,0:T(8,128)(2,1)S(1)}, bf16[2,1,256,256]{3,2,1,0:T(8,128)(2,1)S(1)}, u32[]{:S(2)}, u32[]{:S(2)}) collective-permute-start(bf16[2,1,256,256]{3,2,1,0:T(8,128)(2,1)S(1)} %get-tuple-element.94), channel_id=1, source_target_pairs={{1,2},{3,4},{5,6},{7,8},{9,10},{11,12},{13,14},{15,16},{17,18},{19... | collective-permute-start | bytes 786440 | tf_op jit(solution)/shard_map/ppermute | solution.py:234
  12.3 28.7 %copy-start.5 = (f32[2,32,256]{2,1,0:T(8,128)}, f32[2,32,256]{2,1,0:T(8,128)S(1)}, u32[]{:S(2)}) copy-start(f32[2,32,256]{2,1,0:T(8,128)S(1)} %dynamic-slice_convert_fusion.mask_ref) | copy-start | bytes 196612
  18.8 1.9 %copy-start = (bf16[4,2,256,256]{3,2,1,0:T(8,128)(2,1)S(1)}, bf16[4,2,256,256]{3,2,1,0:T(8,128)(2,1)}, u32[]{:S(2)}) copy-start(bf16[4,2,256,256]{3,2,1,0:T(8,128)(2,1)} %left_ref.9) | copy-start | bytes 3145732
  42.8 17.8 %all-to-all-start.1 = ((bf16[8,144,256]{2,1,0:T(8,128)(2,1)}), bf16[8,144,256]{2,1,0:T(8,128)(2,1)}, u32[]{:S(2)}, u32[]{:S(2)}) async-start(bf16[8,144,256]{2,1,0:T(8,128)(2,1)} %copy-done.4), calls=%async_computation.1 | async-start | bytes 1179648 | tf_op jit(solution)/shard_map/all_to_all | solution.py:269
  47.0 38.3 %collective-permute-start.4 = (f32[1,256,256]{2,1,0:T(8,128)}, f32[1,256,256]{2,1,0:T(8,128)S(1)}, u32[]{:S(2)}, u32[]{:S(2)}) collective-permute-start(f32[1,256,256]{2,1,0:T(8,128)} %get-tuple-element.50), channel_id=1, source_target_pairs={{0,1},{1,0},{2,3},{3,2},{4,5},{5,4},{6,7},{7,6},{8,9},{9,8},{10,11... | collective-permute-start | bytes 786440 | tf_op jit(solution)/shard_map/ppermute | solution.py:235
  47.1 38.2 %collective-permute-start.5 = (f32[1,256,256]{2,1,0:T(8,128)}, f32[1,256,256]{2,1,0:T(8,128)}, u32[]{:S(2)}, u32[]{:S(2)}) collective-permute-start(f32[1,256,256]{2,1,0:T(8,128)} %get-tuple-element.51), channel_id=1, source_target_pairs={{1,2},{3,4},{5,6},{7,8},{9,10},{11,12},{13,14},{15,16},{17,18},{19... | collective-permute-start | bytes 786440 | tf_op jit(solution)/shard_map/ppermute | solution.py:234
  63.1 29.8 %collective-permute-start.6 = (bf16[2,256,256]{2,1,0:T(8,128)(2,1)}, bf16[2,256,256]{2,1,0:T(8,128)(2,1)}, u32[]{:S(2)}, u32[]{:S(2)}) collective-permute-start(bf16[2,256,256]{2,1,0:T(8,128)(2,1)} %get-tuple-element.53), channel_id=1, source_target_pairs={{0,1},{1,0},{2,3},{3,2},{4,5},{5,4},{6,7},{7,6},{8,9},{9,8},{10,11... | collective-permute-start | bytes 786440 | tf_op jit(solution)/shard_map/ppermute | solution.py:235
  63.1 29.8 %collective-permute-start.7 = (bf16[2,256,256]{2,1,0:T(8,128)(2,1)}, bf16[2,256,256]{2,1,0:T(8,128)(2,1)}, u32[]{:S(2)}, u32[]{:S(2)}) collective-permute-start(bf16[2,256,256]{2,1,0:T(8,128)(2,1)} %get-tuple-element.54), channel_id=1, source_target_pairs={{1,2},{3,4},{5,6},{7,8},{9,10},{11,12},{13,14},{15,16},{17,18},{19... | collective-permute-start | bytes 786440 | tf_op jit(solution)/shard_map/ppermute | solution.py:234
  78.3 14.7 %all-to-all-start.2 = ((f32[32,8,128]{2,1,0:T(8,128)}), f32[32,8,128]{2,1,0:T(8,128)}, u32[]{:S(2)}, u32[]{:S(2)}) async-start(f32[32,8,128]{2,1,0:T(8,128)} %copy-done.13), calls=%async_computation.2 | async-start | bytes 262144 | tf_op jit(solution)/shard_map/all_to_all | solution.py:269
  92.9 3.9 %copy-start.1 = (bf16[4,2,256,256]{3,2,1,0:T(8,128)(2,1)S(1)}, bf16[4,2,256,256]{3,2,1,0:T(8,128)(2,1)}, u32[]{:S(2)}) copy-start(bf16[4,2,256,256]{3,2,1,0:T(8,128)(2,1)} %left_ref.9) | copy-start | bytes 3145732
  96.9 22.2 %copy-start.6 = (f32[2,32,256]{2,1,0:T(8,128)S(1)}, f32[2,32,256]{2,1,0:T(8,128)}, u32[]{:S(2)}) copy-start(f32[2,32,256]{2,1,0:T(8,128)} %copy-done.5) | copy-start | bytes 196612
  119.2 24.6 %copy-start.10 = (f32[2,2,32,256]{3,2,1,0:T(8,128)}, f32[2,2,32,256]{3,2,1,0:T(8,128)S(1)}, u32[]{:S(2)}) copy-start(f32[2,2,32,256]{3,2,1,0:T(8,128)S(1)} %get-tuple-element.65.hd_ref) | copy-start | bytes 393220
  139.0 4.8 %copy-start.8 = (f32[2,2,32,256]{3,2,1,0:T(8,128)S(1)}, f32[2,2,32,256]{3,2,1,0:T(8,128)}, u32[]{:S(2)}) copy-start(f32[2,2,32,256]{3,2,1,0:T(8,128)} %copy-done.7) | copy-start | bytes 393220
  139.0 10.2 %collective-permute-start.8 = (bf16[2,256,256]{2,1,0:T(8,128)(2,1)S(1)}, bf16[2,256,256]{2,1,0:T(8,128)(2,1)S(1)}, u32[]{:S(2)}, u32[]{:S(2)}) collective-permute-start(bf16[2,256,256]{2,1,0:T(8,128)(2,1)S(1)} %get-tuple-element.68), channel_id=1, source_target_pairs={{0,1},{1,0},{2,3},{3,2},{4,5},{5,4},{6,7},{7,6},{8,9},{9,8},{10,11... | collective-permute-start | bytes 786440 | tf_op jit(solution)/shard_map/ppermute | solution.py:235
  140.2 9.0 %collective-permute-start.9 = (bf16[2,256,256]{2,1,0:T(8,128)(2,1)S(1)}, bf16[2,256,256]{2,1,0:T(8,128)(2,1)S(1)}, u32[]{:S(2)}, u32[]{:S(2)}) collective-permute-start(bf16[2,256,256]{2,1,0:T(8,128)(2,1)S(1)} %get-tuple-element.69), channel_id=1, source_target_pairs={{1,2},{3,4},{5,6},{7,8},{9,10},{11,12},{13,14},{15,16},{17,18},{19... | collective-permute-start | bytes 786440 | tf_op jit(solution)/shard_map/ppermute | solution.py:234
  150.4 22.0 %copy-start.9 = (f32[2,2,32,256]{3,2,1,0:T(8,128)S(1)}, f32[2,2,32,256]{3,2,1,0:T(8,128)}, u32[]{:S(2)}) copy-start(f32[2,2,32,256]{3,2,1,0:T(8,128)} %copy-done.7) | copy-start | bytes 393220
  150.4 22.0 %copy-start.11 = (f32[2,2,32,256]{3,2,1,0:T(8,128)S(1)}, f32[2,2,32,256]{3,2,1,0:T(8,128)}, u32[]{:S(2)}) copy-start(f32[2,2,32,256]{3,2,1,0:T(8,128)} %copy-done.10) | copy-start | bytes 393220
  (6 other events, 5.7 us)

commit v5 on v4

--- a/solution.py
+++ b/solution.py
@@ -122,41 +122,42 @@
     return own + [core_ref[u], chip_ref[u]]
 
 
+def pick(row, i, vecs):
+    return row if i == 0 else pltpu.roll(row, 128 - i * vecs, 1)
+
+
+def lane_of(row, u):
+    lane = lax.broadcasted_iota(jnp.int32, row.shape, 1)
+    return jnp.sum(jnp.where(lane == u, row, 0.0), axis=1, keepdims=True)
+
+
 def form_kernel(row_ref, got_ref, core_ref, chip_ref, start_ref, pre_ref, pre_core, pre_chip, dir_ref, mdir_ref, coef_ref):
     vecs, slots, states, _ = dir_ref.shape
     share = states // got_ref.shape[0]
     row = row_ref[0]
     for i in range(1, row_ref.shape[0]):
         row = row + row_ref[i]
-    row = row[0:1]
-    lane = lax.broadcasted_iota(jnp.int32, row.shape, 1)
-    index = lax.broadcasted_iota(jnp.int32, coef_ref.shape, 0)
-    lanes = lax.broadcasted_iota(jnp.int32, coef_ref.shape, 1)
-    table = jnp.zeros(coef_ref.shape, F32)
-    for u in range(vecs):
-        total = [
-            jnp.sum(jnp.where(lane == i * vecs + u, row, 0.0), axis=1, keepdims=True)
-            for i in range(8)
-        ]
-        scale = 1.0 / jnp.sqrt(total[0] + 1e-06)
-        vv, vh, vmv, vmh, hmh, mvmv, mvmh, mhmh = [x * (scale * scale) for x in total]
-        correlation = vmh - vh * vmv
-        square = mhmh - 2.0 * vh * mvmh + vh * vh * mvmv
-        square = square - 2.0 * correlation * (vmh - vh * vmv) + correlation * correlation * vv
-        norm = jnp.sqrt(jnp.maximum(square, 0.0) + 1e-06)
-        coupling = (hmh - vh * vmh - correlation * vh) / norm
-        alpha = scale / norm
-        for j, x in enumerate([vh, correlation, alpha, scale, coupling, norm]):
-            table = table + jnp.where((index == j) & (lanes == u), x, 0.0)
+    total = [pick(row, i, vecs) for i in range(8)]
+    scale = 1.0 / jnp.sqrt(total[0] + 1e-06)
+    vv, vh, vmv, vmh, hmh, mvmv, mvmh, mhmh = [x * (scale * scale) for x in total]
+    correlation = vmh - vh * vmv
+    square = mhmh - 2.0 * vh * mvmh + vh * vh * mvmv
+    square = square - 2.0 * correlation * (vmh - vh * vmv) + correlation * correlation * vv
+    norm = jnp.sqrt(jnp.maximum(square, 0.0) + 1e-06)
+    coupling = (hmh - vh * vmh - correlation * vh) / norm
+    alpha = scale / norm
+    for j, x in enumerate([vh, correlation, alpha, scale, coupling, norm]):
+        coef_ref[j] = x
+    for u in range(vecs):
+        ray, corr, mult = [lane_of(x[0:1], u) for x in (vh, correlation, alpha)]
         hs = slot_blocks(got_ref, core_ref, chip_ref, u, share)
         for i in range(slots):
             m = (pre_ref[0], pre_ref[1], pre_core[0], pre_chip[0])[i]
             v = start_ref[u, i].astype(F32)
-            raw = m * (hs[i].astype(F32) - vh * v) - correlation * v
-            small = (raw * alpha).astype(BF)
+            raw = m * (hs[i].astype(F32) - ray * v) - corr * v
+            small = (raw * mult).astype(BF)
             dir_ref[u, i] = small
             mdir_ref[u, i] = (m * small.astype(F32)).astype(BF)
-    coef_ref[...] = table
 
 
 def lift_kernel(got_ref, core_ref, chip_ref, pre_ref, pre_core, pre_chip, out_ref):
@@ -180,7 +181,7 @@
 def gram_kernel(coef_ref, start_ref, h_ref, hd_ref, pre_ref, dot_ref, dir_ref):
     vecs, blocks = h_ref.shape[:2]
     for u in range(vecs):
-        rayleigh, correlation, alpha, scale = [coef_ref[j : j + 1, u : u + 1] for j in range(4)]
+        rayleigh, correlation, alpha, scale = [lane_of(coef_ref[j, 0:1], u) for j in range(4)]
         for b in range(blocks):
             m = pre_ref[b]
             v, h = start_ref[u, b].astype(F32), h_ref[u, b]
@@ -196,7 +197,100 @@
                 dot_ref[i, u] = tile if b == 0 else dot_ref[i, u] + tile
 
 
-def call(kernel, outs, args, smem=0, scratch=(), flops=0):
+def tally_kernel(factor, *refs):
+    out_ref = refs[-1]
+    lines = []
+    for ref in refs[:-1]:
+        for i in range(ref.shape[0]):
+            lines += [jnp.sum(ref[i, u], axis=0, keepdims=True) for u in range(ref.shape[1])]
+    lines.append(jnp.zeros((128 - len(lines), 128), F32))
+    table = jnp.concatenate(lines, axis=0)
+    row = lax.dot_general(
+        jnp.ones((8, 128), F32),
+        table,
+        (((1,), (1,)), ((), ())),
+        precision=lax.Precision.HIGHEST,
+        preferred_element_type=F32,
+    )
+    out_ref[...] = jnp.broadcast_to((row[0:1] * factor)[None], out_ref.shape)
+
+
+def form(table, left, right):
+    result = None
+    for i, x in left:
+        for j, y in right:
+            term = x * y * table[(min(i, j), max(i, j))]
+            result = term if result is None else result + term
+    return result
+
+
+def lowest(rayleigh, curvature, coupling):
+    half = 0.5 * (rayleigh - curvature)
+    energy = 0.5 * (rayleigh + curvature) - jnp.sqrt(half * half + coupling * coupling)
+    weight = energy - rayleigh
+    return energy, weight, jnp.sqrt(coupling * coupling + weight * weight)
+
+
+def finish_kernel(row_ref, coef_ref, start_ref, dir_ref, h_ref, hd_ref, pre_ref, out_ref, energy_ref):
+    vecs, blocks = out_ref.shape[:2]
+    row = row_ref[0]
+    for i in range(1, row_ref.shape[0]):
+        row = row + row_ref[i]
+    count = len(PLAIN) + 2 * len(PAIRS) + 15
+    total = [pick(row, i, vecs) for i in range(count)]
+    one = {p: total[i] for i, p in enumerate(PLAIN)}
+    first = {p: total[len(PLAIN) + i] for i, p in enumerate(PAIRS)}
+    second = {p: total[len(PLAIN) + len(PAIRS) + i] for i, p in enumerate(PAIRS)}
+    far = total[len(PLAIN) + 2 * len(PAIRS) :]
+    old_ray, old_corr, _, scale, coupling, old_norm = [coef_ref[j, 0:1] for j in range(6)]
+
+    _, weight, size = lowest(old_ray, one[(1, 3)], coupling)
+    keep, mix = coupling / size, weight / size
+    v_of, h_of = [(0, keep), (1, mix)], [(2, keep), (3, mix)]
+    rayleigh = form(one, v_of, h_of)
+    resid_of = h_of + [(i, -rayleigh * x) for i, x in v_of]
+    correlation = form(first, v_of, resid_of)
+    square = form(second, resid_of, resid_of) - 2.0 * correlation * form(first, v_of, resid_of)
+    square = square + correlation * correlation * form(one, v_of, v_of)
+    norm = jnp.sqrt(jnp.maximum(square, 0.0) + 1e-06)
+    coupling = (form(first, resid_of, h_of) - correlation * rayleigh) / norm
+
+    mult = [
+        mix,
+        scale * keep * (old_ray - rayleigh),
+        -rayleigh * mix,
+        keep * old_norm - correlation * mix,
+        scale * keep * (old_corr - correlation),
+    ]
+    back = 1.0 / scale
+    on_hd = far[:5]
+    on_start = [far[5]] + [far[7 + i] for i in range(4)]
+    on_dir = [far[6]] + [far[11 + i] for i in range(4)]
+    on_d = [first[3, 3], first[0, 3] * back, first[1, 3], one[1, 3], one[0, 3] * back]
+    on_v = [first[2, 3], first[0, 2] * back, first[1, 2], one[1, 2], one[0, 2] * back]
+    curvature = None
+    for j, column in enumerate([on_hd, on_start, on_dir, on_d, on_v]):
+        line = None
+        for i in range(5):
+            term = mult[i] * column[i]
+            line = term if line is None else line + term
+        line = line * (mult[j] * back if j == 4 else mult[j])
+        curvature = line if curvature is None else curvature + line
+    curvature = curvature / (norm * norm)
+    energy, weight, size = lowest(rayleigh, curvature, coupling)
+    of_v, of_raw = coupling / size, weight / (norm * size)
+    values = (keep * scale, mix, rayleigh, correlation, of_v, of_raw)
+    for u in range(vecs):
+        energy_ref[u] = lane_of(energy, u)[0, 0]
+        first_v, then_d, ray, corr, use_v, use_raw = [lane_of(x, u) for x in values]
+        for b in range(blocks):
+            new_v = first_v * start_ref[u, b].astype(F32) + then_d * dir_ref[u, b]
+            new_h = first_v * h_ref[u, b] + then_d * hd_ref[u, b]
+            raw = pre_ref[b] * (new_h - ray * new_v) - corr * new_v
+            out_ref[u, b] = use_v * new_v + use_raw * raw
+
+
+def call(kernel, outs, args, smem=0, scratch=(), flops=0, smem_outs=0):
     vmem = pl.BlockSpec(memory_space=pltpu.VMEM)
     specs = [pl.BlockSpec(memory_space=pltpu.SMEM)] * smem + [vmem] * (len(args) - smem)
     size = sum(x.size * x.dtype.itemsize for x in list(outs) + list(args))
@@ -204,7 +298,8 @@
         kernel,
         out_shape=[jax.ShapeDtypeStruct(x.shape, x.dtype) for x in outs],
         in_specs=specs,
-        out_specs=[vmem] * len(outs),
+        out_specs=[vmem] * (len(outs) - smem_outs)
+        + [pl.BlockSpec(memory_space=pltpu.SMEM)] * smem_outs,
         scratch_shapes=scratch,
         compiler_params=pltpu.CompilerParams(vmem_limit_bytes=24 << 20),
         cost_estimate=pl.CostEstimate(flops=flops, bytes_accessed=size, transcendentals=0),
@@ -278,12 +373,11 @@
     right_all = jnp.concatenate([right_env, *swap(*edges(right_env, 1))], axis=1)
     start = jnp.where(mask[None], start_vectors, jnp.zeros((), BF))
     start_all = jnp.concatenate([start, *swap(*edges(start, 1))], axis=1)
-    early = (rows(mask.astype(F32), 1), rows(precond, 1), rows(start, 2), *edges(precond, 0))
-    start_all, right_all, early = barrier((start_all, right_all, early))
-    mask_rows, pre, vec, pre_inner, pre_outer = early
-
-    parts, pre_inner, pre_outer = barrier((apply_op(start_all), pre_inner, pre_outer))
-    pre_core, pre_chip = swap(pre_inner, pre_outer)
+    pre_core, pre_chip = swap(*edges(precond, 0))
+    early = (rows(mask.astype(F32), 1), rows(precond, 1), rows(start, 2))
+    start_all, early = barrier((start_all, early))
+    mask_rows, pre, vec = early
+    parts, pre_core, pre_chip = barrier((apply_op(start_all), pre_core, pre_chip))
     got = exchange(parts)
     h_raw, body = call(
         functools.partial(settle_kernel, factor),
@@ -296,10 +390,9 @@
     )
     h_core, h_chip = swap(inner, outer)
     row = exchange(row, "sec")
-    row, pre_core, pre_chip = barrier((row, pre_core, pre_chip))
     dir_all, m_dir, coef = call(
         form_kernel,
-        [four_shape, four_shape, shape((16, 128), F32)],
+        [four_shape, four_shape, shape((6, 8, 128), F32)],
         [row, got, h_core, h_chip, start_all, precond, pre_core, pre_chip],
     )
     parts, dir_all, m_dir = barrier((apply_op(dir_all), dir_all, m_dir))
@@ -324,84 +417,19 @@
     )
     (m_hd,) = call(lift_kernel, [four_shape], [got, hd_core, hd_chip, precond, pre_core, pre_chip])
     dots_hd = apply_op(m_hd, [m_hd] + known, [h_m_start, h_m_dir], keep=False)
-    rayleigh, correlation, _, scale, coupling, dir_norm = [coef[j, :vecs] for j in range(6)]
-
-    tiles = jnp.concatenate([gram, dots_hd, dots_start, dots_dir])
-    total = jnp.sum(tiles, axis=(2, 3)) * factor
-    count = total.size
     everyone = groups * sec
-    row = jnp.pad(total.reshape(-1), (0, 128 - count))[None]
-    row = jnp.broadcast_to(row[None], (everyone,) + row.shape)
+    (row,) = call(
+        functools.partial(tally_kernel, factor),
+        [shape((everyone, 1, 128), F32)],
+        [gram, dots_hd, dots_start, dots_dir],
+    )
     row = exchange(row, ("term", "sec"))
-    total = jnp.sum(row, axis=0)[0, :count].reshape(total.shape)
-    one = {p: total[i] for i, p in enumerate(PLAIN)}
-    first = {p: total[len(PLAIN) + i] for i, p in enumerate(PAIRS)}
-    second = {p: total[len(PLAIN) + len(PAIRS) + i] for i, p in enumerate(PAIRS)}
-    far = total[gram.shape[0] :]
-
-    def form(table, left, right):
-        result = 0.0
-        for i, x in left:
-            for j, y in right:
-                result = result + x * y * table[(min(i, j), max(i, j))]
-        return result
-
-    curvature = one[(1, 3)]
-    energy = 0.5 * (rayleigh + curvature) - jnp.sqrt(
-        (0.5 * (rayleigh - curvature)) ** 2 + coupling**2
-    )
-    weight = energy - rayleigh
-    size = jnp.sqrt(coupling**2 + weight**2)
-    keep, mix = coupling / size, weight / size
-    v_of, h_of = [(0, keep), (1, mix)], [(2, keep), (3, mix)]
-    old_rayleigh, old_correlation, old_norm = rayleigh, correlation, dir_norm
-    rayleigh = form(one, v_of, h_of)
-    resid_of = h_of + [(i, -rayleigh * x) for i, x in v_of]
-    correlation = form(first, v_of, resid_of)
-    square = (
-        form(second, resid_of, resid_of)
-        - 2.0 * correlation * form(first, v_of, resid_of)
-        + correlation**2 * form(one, v_of, v_of)
-    )
-    dir_norm = jnp.sqrt(jnp.maximum(square, 0.0) + 1e-06)
-    coupling = (form(first, resid_of, h_of) - correlation * rayleigh) / dir_norm
-
-    mult = [
-        mix,
-        scale * keep * (old_rayleigh - rayleigh),
-        -rayleigh * mix,
-        keep * old_norm - correlation * mix,
-        scale * keep * (old_correlation - correlation),
-    ]
-    on_hd = far[:5]
-    on_start = [far[5]] + [far[7 + i] for i in range(4)]
-    on_dir = [far[6]] + [far[11 + i] for i in range(4)]
-    on_d = [first[3, 3], first[0, 3] / scale, first[1, 3], one[1, 3], one[0, 3] / scale]
-    on_v = [
-        first[2, 3] / scale,
-        first[0, 2] / scale**2,
-        first[1, 2] / scale,
-        one[1, 2] / scale,
-        one[0, 2] / scale**2,
-    ]
-    curvature = 0.0
-    for j, column in enumerate([on_hd, on_start, on_dir, on_d, on_v]):
-        for i in range(5):
-            curvature = curvature + mult[i] * mult[j] * column[i]
-    curvature = curvature / dir_norm**2
-    energy = 0.5 * (rayleigh + curvature) - jnp.sqrt(
-        (0.5 * (rayleigh - curvature)) ** 2 + coupling**2
-    )
-    weight = energy - rayleigh
-    size = jnp.sqrt(coupling**2 + weight**2)
-
-    def expand(value):
-        return value[:, None, None, None]
-
-    new_v = expand(keep * scale) * vec.astype(F32) + expand(mix) * direction
-    new_h = expand(keep * scale) * h_raw + expand(mix) * h_dir
-    raw = pre[None] * (new_h - expand(rayleigh) * new_v) - expand(correlation) * new_v
-    final = expand(coupling / size) * new_v + expand(weight / (dir_norm * size)) * raw
+    final, energy = call(
+        finish_kernel,
+        [slice_shape, shape((vecs,), F32)],
+        [row, coef, vec, direction, h_raw, h_dir, pre],
+        smem_outs=1,
+    )
     return (final, energy)
 
 

time: 175 us -> 168 us (0.960)
  blocking collectives: 77.4 us -> 114 us
  starting transfers between devices: 48.3 us -> 23.7 us
  waiting for transfers between devices: 18.1 us -> 5.95 us
  Pallas kernels: 18.2 us -> 14.9 us
    all_to_all x4 -> x6, blocking collectives: 77.4 us -> 114 us  [exchange(): return lax.all_to_all(parts, axis, 0, 0)]
    ppermute x5, starting transfers between devices: 32.4 us -> 18.6 us  [swap(): outer = lax.ppermute(outer, 'sec', chip_pairs)]
    all_to_all x2 -> x0, waiting for transfers between devices: 11.8 us -> none  [exchange(): return lax.all_to_all(parts, axis, 0, 0)]
    all_to_all x2 -> x0, starting transfers between devices: 11.2 us -> none  [exchange(): return lax.all_to_all(parts, axis, 0, 0)]
    pallas_call x13 -> x15, Pallas kernels: 18.2 us -> 14.9 us  [call(): pl.pallas_call(kernel, out_shape=[jax.ShapeDtypeStruct(x.shape, x.dtype)...]
    unnamed x36 -> x12, local copies, waits for them, and re-layouts: 3.95 us -> 1.17 us
    concatenate x1 -> x0, other arithmetic: 1.86 us -> none  [shards(): jnp.concatenate([right_env, *swap(*edges(right_env, 1))], axis=1)]
  transfers between devices with their start and end apart: 12 -> 10, of which waited for: 3 -> 3; matrix products, arithmetic and copies ran while one was open for 1% -> 3% of each run, Pallas kernels for 4% -> 4%
where the time goes in v5:
time: 168 us
  blocking collectives  114 us (68%)
  starting transfers between devices  23.7 us (14%)
  Pallas kernels  14.9 us (9%)
  waiting for transfers between devices  5.95 us (4%)
  local copies, waits for them, and re-layouts  5 us (3%)
  other arithmetic  3.32 us (2%)
    all_to_all x6, blocking collectives, exchange(): return lax.all_to_all(parts, axis, 0, 0)  114 us
    ppermute x5, starting transfers between devices, swap(): outer = lax.ppermute(outer, 'sec', chip_pairs)  18.6 us
    pallas_call x15, Pallas kernels, call(): pl.pallas_call(kernel, out_shape=[jax.ShapeDtypeStruct(x.shape, x.dtype)...  14.9 us
    ppermute x5, waiting for transfers between devices, swap(): outer = lax.ppermute(outer, 'sec', chip_pairs)  5.66 us
    ppermute x5, starting transfers between devices, swap(): inner = lax.ppermute(inner, 'sec', core_pairs)  5.08 us
  transfers between devices with their start and end apart: 10, of which 3 were waited for; matrix products, arithmetic and copies ran while one was open for 3% of the time, Pallas kernels for 4%

profile of v5, /device:TPU:1, one launch (start us, length us, event | category | flops | bytes accessed | tf_op | source)
XLA Modules:
  0.0 167.7 jit_solution(17201639956563197610)
XLA Ops:
  1.7 1.1 broadcast_select_fusion
  3.6 3.2 %collective-permute-start = (bf16[2,1,256,256]{3,2,1,0:T(8,128)(2,1)}, bf16[2,1,256,256]{3,2,1,0:T(8,128)(2,1)}, u32[]{:S(2)}, u32[]{:S(2)}) collective-permute-start(bf16[2,1,256,256]{3,2,1,0:T(8,128)(2,1)} %get-tuple-element.70), channel_id=1, source_target_pairs={{0,1},{1,0},{2,3},{3,2},{4,5},{5,4},{6,7},{7,6},{8,9},{9,8},{10,11... | collective-permute-start | bytes 786440 | tf_op jit(solution)/shard_map/ppermute | solution.py:330
  6.8 1.9 %collective-permute-start.1 = (bf16[2,1,256,256]{3,2,1,0:T(8,128)(2,1)}, bf16[2,1,256,256]{3,2,1,0:T(8,128)(2,1)}, u32[]{:S(2)}, u32[]{:S(2)}) collective-permute-start(bf16[2,1,256,256]{3,2,1,0:T(8,128)(2,1)} %get-tuple-element.71), channel_id=1, source_target_pairs={{1,2},{3,4},{5,6},{7,8},{9,10},{11,12},{13,14},{15,16},{17,18},{19... | collective-permute-start | bytes 786440 | tf_op jit(solution)/shard_map/ppermute | solution.py:329
  9.6 3.8 %collective-permute-start.5 = (f32[1,256,256]{2,1,0:T(8,128)}, f32[1,256,256]{2,1,0:T(8,128)S(1)}, u32[]{:S(2)}, u32[]{:S(2)}) collective-permute-start(f32[1,256,256]{2,1,0:T(8,128)} %get-tuple-element.68), channel_id=1, source_target_pairs={{1,2},{3,4},{5,6},{7,8},{9,10},{11,12},{13,14},{15,16},{17,18},{19... | collective-permute-start | bytes 786440 | tf_op jit(solution)/shard_map/ppermute | solution.py:329
  14.4 1.9 %collective-permute-start.3 = (bf16[4,1,256,256]{3,2,1,0:T(8,128)(2,1)}, bf16[4,1,256,256]{3,2,1,0:T(8,128)(2,1)}, u32[]{:S(2)}, u32[]{:S(2)}) collective-permute-start(bf16[4,1,256,256]{3,2,1,0:T(8,128)(2,1)} %get-tuple-element.66), channel_id=1, source_target_pairs={{1,2},{3,4},{5,6},{7,8},{9,10},{11,12},{13,14},{15,16},{17,18},{19... | collective-permute-start | bytes 1572872 | tf_op jit(solution)/shard_map/ppermute | solution.py:329
  17.2 1.1 pad_maximum_fusion.x_ref.start_ref.refs_3_.refs_4_
  18.7 1.1 constant_dynamic-update-slice_fusion.1
  19.8 5.5 %collective-permute-done.3 = bf16[4,1,256,256]{3,2,1,0:T(8,128)(2,1)} collective-permute-done((bf16[4,1,256,256]{3,2,1,0:T(8,128)(2,1)}, bf16[4,1,256,256]{3,2,1,0:T(8,128)(2,1)}, u32[]{:S(2)}, u32[]{:S(2)}) %collective-permute-start.3) | collective-permute-done | bytes 524320 | tf_op jit(solution)/shard_map/ppermute | solution.py:329
  26.3 1.9 %shard_map.77 = bf16[8,2,2,32,256]{4,3,2,1,0:T(8,128)(2,1)S(1)} custom-call(s32[4,2]{1,0:T(4,128)S(1)} %fusion.slot_ref, bf16[2,4,256,256]{3,2,1,0:T(8,128)(2,1)S(1)} %pad_maximum_fusion.x_ref.start_ref.refs_3_.refs_4_, bf16[4,4,256,256]{3,2,1,0:T(8,128)(2,1)S(1)} %constant_dynamic-update-slice_fusion.right_ref, bf16[4,2,256,256]{3,2,1,0:T(8,128)(2,1)S(1)} %copy-done), custom_call_target="tpu_custom_call" | custom-call | flops 1073741824 | bytes 4718624 | tf_op jit(solution)/shard_map/pallas_call | solution.py:297
  28.2 20.5 %all_to_all.30.got_ref = bf16[8,2,2,32,256]{4,3,2,1,0:T(8,128)(2,1)S(1)} all-to-all(bf16[8,2,2,32,256]{4,3,2,1,0:T(8,128)(2,1)S(1)} %shard_map.77), channel_id=1, replica_groups=mesh['term'=8,'sec'=32] {'term'}, dimensions={0} | all-to-all | bytes 1048576 | tf_op jit(solution)/shard_map/all_to_all | solution.py:364
  49.1 20.4 %all_to_all.31.got_ref = bf16[8,144,256]{2,1,0:T(8,128)(2,1)S(1)} all-to-all(bf16[8,144,256]{2,1,0:T(8,128)(2,1)S(1)} %get-tuple-element.39), channel_id=1, replica_groups=mesh['term'=8,'sec'=32] {'term'}, dimensions={0} | all-to-all | bytes 1179648 | tf_op jit(solution)/shard_map/all_to_all | solution.py:364
  69.6 8.6 %collective-permute-start.7 = (bf16[2,256,256]{2,1,0:T(8,128)(2,1)S(1)}, bf16[2,256,256]{2,1,0:T(8,128)(2,1)S(1)}, u32[]{:S(2)}, u32[]{:S(2)}) collective-permute-start(bf16[2,256,256]{2,1,0:T(8,128)(2,1)S(1)} %get-tuple-element.42), channel_id=1, source_target_pairs={{1,2},{3,4},{5,6},{7,8},{9,10},{11,12},{13,14},{15,16},{17,18},{19... | collective-permute-start | bytes 786440 | tf_op jit(solution)/shard_map/ppermute | solution.py:329
  78.2 14.0 %all_to_all.32.row_ref = f32[32,8,128]{2,1,0:T(8,128)S(1)} all-to-all(f32[32,8,128]{2,1,0:T(8,128)S(1)} %get-tuple-element.40), channel_id=1, replica_groups=mesh['term'=8,'sec'=32] {'sec'}, dimensions={0} | all-to-all | bytes 262144 | tf_op jit(solution)/shard_map/all_to_all | solution.py:364
  92.2 1.5 shard_map.80
  93.7 1.9 %shard_map.81 = bf16[8,2,2,32,256]{4,3,2,1,0:T(8,128)(2,1)S(1)} custom-call(s32[4,2]{1,0:T(4,128)S(1)} %fusion.slot_ref, bf16[2,4,256,256]{3,2,1,0:T(8,128)(2,1)S(1)} %get-tuple-element.60.x_ref.refs_2_.refs_3_, bf16[4,4,256,256]{3,2,1,0:T(8,128)(2,1)S(1)} %constant_dynamic-update-slice_fusion.right_ref, bf16[4,2,256,256]{3,2,1,0:T(8,128)(2,1)S(1)} %copy-done), custom_call_target="tpu_custom_call" | custom-call | flops 1073741824 | bytes 4718624 | tf_op jit(solution)/shard_map/pallas_call | solution.py:297
  95.6 20.3 %all_to_all.33.got_ref = bf16[8,2,2,32,256]{4,3,2,1,0:T(8,128)(2,1)S(1)} all-to-all(bf16[8,2,2,32,256]{4,3,2,1,0:T(8,128)(2,1)S(1)} %shard_map.81), channel_id=1, replica_groups=mesh['term'=8,'sec'=32] {'term'}, dimensions={0} | all-to-all | bytes 1048576 | tf_op jit(solution)/shard_map/all_to_all | solution.py:364
  116.0 19.8 %all_to_all.34.got_ref = bf16[8,128,256]{2,1,0:T(8,128)(2,1)S(1)} all-to-all(bf16[8,128,256]{2,1,0:T(8,128)(2,1)S(1)} %get-tuple-element.50), channel_id=1, replica_groups=mesh['term'=8,'sec'=32] {'term'}, dimensions={0} | all-to-all | bytes 1048576 | tf_op jit(solution)/shard_map/all_to_all | solution.py:364
  135.9 1.2 collective-permute-start.8
  137.0 2.4 %collective-permute-start.9 = (bf16[2,256,256]{2,1,0:T(8,128)(2,1)S(1)}, bf16[2,256,256]{2,1,0:T(8,128)(2,1)S(1)}, u32[]{:S(2)}, u32[]{:S(2)}) collective-permute-start(bf16[2,256,256]{2,1,0:T(8,128)(2,1)S(1)} %get-tuple-element.57), channel_id=1, source_target_pairs={{1,2},{3,4},{5,6},{7,8},{9,10},{11,12},{13,14},{15,16},{17,18},{19... | collective-permute-start | bytes 786440 | tf_op jit(solution)/shard_map/ppermute | solution.py:329
  140.1 2.2 %shard_map.88 = (bf16[2,2,256,256]{3,2,1,0:T(8,128)(2,1)S(1)}, f32[4,2,8,128]{3,2,1,0:T(8,128)S(1)}) custom-call(s32[4,2]{1,0:T(4,128)S(1)} %fusion.slot_ref, bf16[2,4,256,256]{3,2,1,0:T(8,128)(2,1)S(1)} %get-tuple-element.59.refs_1_.x_ref.refs_2_, bf16[4,4,256,256]{3,2,1,0:T(8,128)(2,1)S(1)} %constant_dynamic-update-slice_fusion.right_ref, ...), custom_call_target="tpu_custom_call" | custom-call | flops 1073741824 | bytes 8945696 | tf_op jit(solution)/shard_map/pallas_call | solution.py:297
  142.3 2.2 %shard_map.87 = (bf16[2,2,256,256]{3,2,1,0:T(8,128)(2,1)S(1)}, f32[4,2,8,128]{3,2,1,0:T(8,128)S(1)}) custom-call(s32[4,2]{1,0:T(4,128)S(1)} %fusion.slot_ref, bf16[2,4,256,256]{3,2,1,0:T(8,128)(2,1)S(1)} %shard_map.86.x_ref.refs_0_.refs_1_, bf16[4,4,256,256]{3,2,1,0:T(8,128)(2,1)S(1)} %constant_dynamic-update-slice_fusion.right_ref, ...), custom_call_target="tpu_custom_call" | custom-call | flops 1073741824 | bytes 8945696 | tf_op jit(solution)/shard_map/pallas_call | solution.py:297
  144.9 2.4 %shard_map.89.refs_1_ = f32[7,2,8,128]{3,2,1,0:T(8,128)S(1)} custom-call(s32[4,2]{1,0:T(4,128)S(1)} %fusion.slot_ref, bf16[2,4,256,256]{3,2,1,0:T(8,128)(2,1)S(1)} %shard_map.85.x_ref.refs_0_, bf16[4,4,256,256]{3,2,1,0:T(8,128)(2,1)S(1)} %constant_dynamic-update-slice_fusion.right_ref, bf16[4,2,256,256]{3,2,1,0:T(8,128)(2,1)S(1)} %copy-done, ...), custom_call_target="tpu_custom_call" | custom-call | flops 1073741824 | bytes 10543136 | tf_op jit(solution)/shard_map/pallas_call | solution.py:297
  147.6 18.7 %all_to_all.35.row_ref = f32[256,1,128]{2,1,0:T(1,128)S(1)} all-to-all(f32[256,1,128]{2,1,0:T(1,128)S(1)} %shard_map.90), channel_id=1, replica_groups=mesh['term'=8,'sec'=32] {'term','sec'}, dimensions={0} | all-to-all | bytes 262144 | tf_op jit(solution)/shard_map/all_to_all | solution.py:364
  166.3 1.2 shard_map.91
  (41 shorter events, 7.9 us)
Async XLA Ops:
  0.6 8.1 %copy-start.1 = (f32[2,256,256]{2,1,0:T(8,128)S(1)}, f32[2,256,256]{2,1,0:T(8,128)}, u32[]{:S(2)}) copy-start(f32[2,256,256]{2,1,0:T(8,128)} %pre_ref.5) | copy-start | bytes 1572868
  0.6 12.7 %copy-start.2 = (bf16[4,2,256,256]{3,2,1,0:T(8,128)(2,1)S(1)}, bf16[4,2,256,256]{3,2,1,0:T(8,128)(2,1)}, u32[]{:S(2)}) copy-start(bf16[4,2,256,256]{3,2,1,0:T(8,128)(2,1)} %param.8) | copy-start | bytes 3145732
  2.8 13.7 %copy-start.3 = (bf16[4,2,256,256]{3,2,1,0:T(8,128)(2,1)S(1)}, bf16[4,2,256,256]{3,2,1,0:T(8,128)(2,1)}, u32[]{:S(2)}) copy-start(bf16[4,2,256,256]{3,2,1,0:T(8,128)(2,1)} %param.8) | copy-start | bytes 3145732
  3.6 13.1 %collective-permute-start = (bf16[2,1,256,256]{3,2,1,0:T(8,128)(2,1)}, bf16[2,1,256,256]{3,2,1,0:T(8,128)(2,1)}, u32[]{:S(2)}, u32[]{:S(2)}) collective-permute-start(bf16[2,1,256,256]{3,2,1,0:T(8,128)(2,1)} %get-tuple-element.70), channel_id=1, source_target_pairs={{0,1},{1,0},{2,3},{3,2},{4,5},{5,4},{6,7},{7,6},{8,9},{9,8},{10,11... | collective-permute-start | bytes 786440 | tf_op jit(solution)/shard_map/ppermute | solution.py:330
  6.8 10.4 %collective-permute-start.1 = (bf16[2,1,256,256]{3,2,1,0:T(8,128)(2,1)}, bf16[2,1,256,256]{3,2,1,0:T(8,128)(2,1)}, u32[]{:S(2)}, u32[]{:S(2)}) collective-permute-start(bf16[2,1,256,256]{3,2,1,0:T(8,128)(2,1)} %get-tuple-element.71), channel_id=1, source_target_pairs={{1,2},{3,4},{5,6},{7,8},{9,10},{11,12},{13,14},{15,16},{17,18},{19... | collective-permute-start | bytes 786440 | tf_op jit(solution)/shard_map/ppermute | solution.py:329
  9.6 7.0 %copy-start.4 = (s32[4]{0:T(128)S(1)}, s32[4]{0:T(128)}, u32[]{:S(2)}) copy-start(s32[4]{0:T(128)} %param.9) | copy-start | bytes 52
  9.6 18.6 %collective-permute-start.5 = (f32[1,256,256]{2,1,0:T(8,128)}, f32[1,256,256]{2,1,0:T(8,128)S(1)}, u32[]{:S(2)}, u32[]{:S(2)}) collective-permute-start(f32[1,256,256]{2,1,0:T(8,128)} %get-tuple-element.68), channel_id=1, source_target_pairs={{1,2},{3,4},{5,6},{7,8},{9,10},{11,12},{13,14},{15,16},{17,18},{19... | collective-permute-start | bytes 786440 | tf_op jit(solution)/shard_map/ppermute | solution.py:329
  14.4 10.8 %collective-permute-start.3 = (bf16[4,1,256,256]{3,2,1,0:T(8,128)(2,1)}, bf16[4,1,256,256]{3,2,1,0:T(8,128)(2,1)}, u32[]{:S(2)}, u32[]{:S(2)}) collective-permute-start(bf16[4,1,256,256]{3,2,1,0:T(8,128)(2,1)} %get-tuple-element.66), channel_id=1, source_target_pairs={{1,2},{3,4},{5,6},{7,8},{9,10},{11,12},{13,14},{15,16},{17,18},{19... | collective-permute-start | bytes 1572872 | tf_op jit(solution)/shard_map/ppermute | solution.py:329
  16.3 2.3 %collective-permute-start.2 = (bf16[4,1,256,256]{3,2,1,0:T(8,128)(2,1)}, bf16[4,1,256,256]{3,2,1,0:T(8,128)(2,1)}, u32[]{:S(2)}, u32[]{:S(2)}) collective-permute-start(bf16[4,1,256,256]{3,2,1,0:T(8,128)(2,1)} %get-tuple-element.67), channel_id=1, source_target_pairs={{0,1},{1,0},{2,3},{3,2},{4,5},{5,4},{6,7},{7,6},{8,9},{9,8},{10,11... | collective-permute-start | bytes 1572872 | tf_op jit(solution)/shard_map/ppermute | solution.py:330
  16.7 9.6 %copy-start = (bf16[4,2,256,256]{3,2,1,0:T(8,128)(2,1)S(1)}, bf16[4,2,256,256]{3,2,1,0:T(8,128)(2,1)}, u32[]{:S(2)}) copy-start(bf16[4,2,256,256]{3,2,1,0:T(8,128)(2,1)} %left_ref.9) | copy-start | bytes 3145732
  16.7 11.5 %collective-permute-start.4 = (f32[1,256,256]{2,1,0:T(8,128)}, f32[1,256,256]{2,1,0:T(8,128)S(1)}, u32[]{:S(2)}, u32[]{:S(2)}) collective-permute-start(f32[1,256,256]{2,1,0:T(8,128)} %get-tuple-element.69), channel_id=1, source_target_pairs={{0,1},{1,0},{2,3},{3,2},{4,5},{5,4},{6,7},{7,6},{8,9},{9,8},{10,11... | collective-permute-start | bytes 786440 | tf_op jit(solution)/shard_map/ppermute | solution.py:330
  69.5 22.8 %collective-permute-start.6 = (bf16[2,256,256]{2,1,0:T(8,128)(2,1)S(1)}, bf16[2,256,256]{2,1,0:T(8,128)(2,1)S(1)}, u32[]{:S(2)}, u32[]{:S(2)}) collective-permute-start(bf16[2,256,256]{2,1,0:T(8,128)(2,1)S(1)} %get-tuple-element.41), channel_id=1, source_target_pairs={{0,1},{1,0},{2,3},{3,2},{4,5},{5,4},{6,7},{7,6},{8,9},{9,8},{10,11... | collective-permute-start | bytes 786440 | tf_op jit(solution)/shard_map/ppermute | solution.py:330
  69.6 22.7 %collective-permute-start.7 = (bf16[2,256,256]{2,1,0:T(8,128)(2,1)S(1)}, bf16[2,256,256]{2,1,0:T(8,128)(2,1)S(1)}, u32[]{:S(2)}, u32[]{:S(2)}) collective-permute-start(bf16[2,256,256]{2,1,0:T(8,128)(2,1)S(1)} %get-tuple-element.42), channel_id=1, source_target_pairs={{1,2},{3,4},{5,6},{7,8},{9,10},{11,12},{13,14},{15,16},{17,18},{19... | collective-permute-start | bytes 786440 | tf_op jit(solution)/shard_map/ppermute | solution.py:329
  135.9 8.6 %collective-permute-start.8 = (bf16[2,256,256]{2,1,0:T(8,128)(2,1)S(1)}, bf16[2,256,256]{2,1,0:T(8,128)(2,1)S(1)}, u32[]{:S(2)}, u32[]{:S(2)}) collective-permute-start(bf16[2,256,256]{2,1,0:T(8,128)(2,1)S(1)} %get-tuple-element.56), channel_id=1, source_target_pairs={{0,1},{1,0},{2,3},{3,2},{4,5},{5,4},{6,7},{7,6},{8,9},{9,8},{10,11... | collective-permute-start | bytes 786440 | tf_op jit(solution)/shard_map/ppermute | solution.py:330
  137.0 7.7 %collective-permute-start.9 = (bf16[2,256,256]{2,1,0:T(8,128)(2,1)S(1)}, bf16[2,256,256]{2,1,0:T(8,128)(2,1)S(1)}, u32[]{:S(2)}, u32[]{:S(2)}) collective-permute-start(bf16[2,256,256]{2,1,0:T(8,128)(2,1)S(1)} %get-tuple-element.57), channel_id=1, source_target_pairs={{1,2},{3,4},{5,6},{7,8},{9,10},{11,12},{13,14},{15,16},{17,18},{19... | collective-permute-start | bytes 786440 | tf_op jit(solution)/shard_map/ppermute | solution.py:329

commit v6 on v5

--- a/solution.py
+++ b/solution.py
@@ -21,14 +21,19 @@
     return sum(tile[:, i : i + 128] for i in range(0, cols, 128))
 
 
-def apply_kernel(count, slot_ref, x_ref, right_ref, left_ref, *refs):
+def slot_of(core_ref, shift_ref, k, b):
+    at, core = b + shift_ref[k], core_ref[0]
+    return jnp.where(at < 0, 3 - core, jnp.where(at > 1, 2 + core, at))
+
+
+def apply_kernel(count, core_ref, shift_ref, x_ref, right_ref, left_ref, *refs):
     field_refs, paired_refs, rest = refs[: count[0]], refs[count[0] : sum(count)], refs[sum(count) :]
     out_ref, z_ref = rest[0], rest[-1]
     vecs, _, states, _ = x_ref.shape
     terms, blocks = left_ref.shape[:2]
     for k in range(terms):
         for b in range(blocks):
-            slot = slot_ref[k, b]
+            slot = slot_of(core_ref, shift_ref, k, b)
             x = x_ref[:, slot].reshape(vecs * states, states)
             z = lax.dot_general(
                 x, right_ref[k, slot], (((1,), (1,)), ((), ())), preferred_element_type=F32
@@ -131,6 +136,13 @@
     return jnp.sum(jnp.where(lane == u, row, 0.0), axis=1, keepdims=True)
 
 
+def weight_of(own_ref, core_ref, chip_ref, i):
+    if i < 2:
+        return own_ref[i]
+    ref = (core_ref, chip_ref)[i - 2]
+    return ref[ref.shape[0] - 1].astype(F32)
+
+
 def form_kernel(row_ref, got_ref, core_ref, chip_ref, start_ref, pre_ref, pre_core, pre_chip, dir_ref, mdir_ref, coef_ref):
     vecs, slots, states, _ = dir_ref.shape
     share = states // got_ref.shape[0]
@@ -147,12 +159,12 @@
     coupling = (hmh - vh * vmh - correlation * vh) / norm
     alpha = scale / norm
     for j, x in enumerate([vh, correlation, alpha, scale, coupling, norm]):
-        coef_ref[j] = x
+        coef_ref[j] = jnp.broadcast_to(x, coef_ref.shape[1:])
     for u in range(vecs):
         ray, corr, mult = [lane_of(x[0:1], u) for x in (vh, correlation, alpha)]
         hs = slot_blocks(got_ref, core_ref, chip_ref, u, share)
         for i in range(slots):
-            m = (pre_ref[0], pre_ref[1], pre_core[0], pre_chip[0])[i]
+            m = weight_of(pre_ref, pre_core, pre_chip, i)
             v = start_ref[u, i].astype(F32)
             raw = m * (hs[i].astype(F32) - ray * v) - corr * v
             small = (raw * mult).astype(BF)
@@ -166,7 +178,7 @@
     for u in range(vecs):
         hs = slot_blocks(got_ref, core_ref, chip_ref, u, share)
         for i in range(slots):
-            m = (pre_ref[0], pre_ref[1], pre_core[0], pre_chip[0])[i]
+            m = weight_of(pre_ref, pre_core, pre_chip, i)
             out_ref[u, i] = (m * hs[i].astype(F32)).astype(BF)
 
 
@@ -174,7 +186,7 @@
     vecs, slots = out_ref.shape[:2]
     for u in range(vecs):
         for i in range(slots):
-            m = (pre_ref[0], pre_ref[1], pre_core[0], pre_chip[0])[i]
+            m = weight_of(pre_ref, pre_core, pre_chip, i)
             out_ref[u, i] = (m * start_ref[u, i].astype(F32)).astype(BF)
 
 
@@ -213,6 +225,64 @@
         preferred_element_type=F32,
     )
     out_ref[...] = jnp.broadcast_to((row[0:1] * factor)[None], out_ref.shape)
+
+
+def pack_kernel(core_ref, dims_hbm, start_ref, right_ref, pre_ref, out_ref, dims_ref, raw, weights, sem):
+    terms, vecs = right_ref.shape[0], start_ref.shape[0]
+    states = out_ref.shape[1]
+    b = core_ref[0]
+    copies = [pltpu.make_async_copy(dims_hbm, dims_ref, sem.at[0])]
+    copies += [pltpu.make_async_copy(start_ref.at[u, b], raw.at[u], sem.at[1 + u]) for u in range(vecs)]
+    copies.append(pltpu.make_async_copy(pre_ref.at[b], weights, sem.at[1 + vecs]))
+    for k in range(terms):
+        copies.append(pltpu.make_async_copy(right_ref.at[k, b], out_ref.at[k], sem.at[2 + vecs + k]))
+    for copy in copies:
+        copy.start()
+    for copy in copies[: vecs + 2]:
+        copy.wait()
+    row = lax.broadcasted_iota(jnp.int32, (states, states), 0)
+    col = lax.broadcasted_iota(jnp.int32, (states, states), 1)
+    keep = (row < dims_ref[b]) & (col < dims_ref[b])
+    for u in range(vecs):
+        out_ref[terms + u] = jnp.where(keep, raw[u].astype(F32), 0.0).astype(BF)
+    out_ref[terms + vecs] = weights[...].astype(BF)
+    for copy in copies[vecs + 2 :]:
+        copy.wait()
+
+
+def load_kernel(core_ref, term_ref, dims_ref, start_ref, left_ref, right_ref, pre_ref, own_ref, left_out, right_out, mask_out, pre_out, vec_out, near_out, raw, weights, sem):
+    vecs, blocks, states, _ = own_ref.shape
+    terms = left_ref.shape[0]
+    share = vec_out.shape[2]
+    core = core_ref[0]
+    first = pltpu.make_async_copy(start_ref, raw, sem.at[0])
+    second = pltpu.make_async_copy(pre_ref, weights, sem.at[1])
+    rest = []
+    for k in range(terms):
+        rest.append(pltpu.make_async_copy(right_ref.at[k, 1 - core], near_out.at[k], sem.at[2 + 3 * k]))
+        rest.append(pltpu.make_async_copy(right_ref.at[k], right_out.at[k], sem.at[3 + 3 * k]))
+        rest.append(pltpu.make_async_copy(left_ref.at[k], left_out.at[k], sem.at[4 + 3 * k]))
+    for copy in [first, second] + rest:
+        copy.start()
+    here = pl.ds(pl.multiple_of(term_ref[0] * share, share), share)
+    row = lax.broadcasted_iota(jnp.int32, (states, states), 0)
+    col = lax.broadcasted_iota(jnp.int32, (states, states), 1)
+    first.wait()
+    for b in range(blocks):
+        keep = (row < dims_ref[b]) & (col < dims_ref[b])
+        for u in range(vecs):
+            own_ref[u, b] = jnp.where(keep, raw[u, b].astype(F32), 0.0).astype(BF)
+            vec_out[u, b] = own_ref[u, b, here, :]
+        low = row[:share] + term_ref[0] * share
+        mask_out[b] = jnp.where((low < dims_ref[b]) & (col[:share] < dims_ref[b]), 1.0, 0.0)
+    second.wait()
+    for b in range(blocks):
+        pre_out[b] = weights[b, here, :]
+    for u in range(vecs):
+        near_out[terms + u] = own_ref[u, 1 - core]
+    near_out[terms + vecs] = weights[1 - core].astype(BF)
+    for copy in rest:
+        copy.wait()
 
 
 def form(table, left, right):
@@ -290,9 +360,10 @@
             out_ref[u, b] = use_v * new_v + use_raw * raw
 
 
-def call(kernel, outs, args, smem=0, scratch=(), flops=0, smem_outs=0):
+def call(kernel, outs, args, smem=0, scratch=(), flops=0, smem_outs=0, anywhere=False):
     vmem = pl.BlockSpec(memory_space=pltpu.VMEM)
-    specs = [pl.BlockSpec(memory_space=pltpu.SMEM)] * smem + [vmem] * (len(args) - smem)
+    bulk = pl.BlockSpec(memory_space=pltpu.HBM) if anywhere else vmem
+    specs = [pl.BlockSpec(memory_space=pltpu.SMEM)] * smem + [bulk] * (len(args) - smem)
     size = sum(x.size * x.dtype.itemsize for x in list(outs) + list(args))
     return pl.pallas_call(
         kernel,
@@ -311,35 +382,20 @@
     groups = lax.axis_size("term")
     sec = lax.axis_size("sec")
     share = states // groups
-    core = lax.axis_index("sec") % 2
-    core_id = core.reshape(1).astype(jnp.int32)
-    term = lax.axis_index("term")
+    core_id = (lax.axis_index("sec") & 1).reshape(1)
+    term_id = lax.axis_index("term").reshape(1)
     factor = 1.0 / (blocks * sec * states * states)
-    position = jnp.arange(states, dtype=jnp.int32)
-    live_rows = position[None, :, None] < block_dims[:, None, None]
-    live_cols = position[None, None, :] < block_dims[:, None, None]
-    mask = live_rows & live_cols
     shape = jax.ShapeDtypeStruct
 
     core_pairs = [(i, i ^ 1) for i in range(sec)]
     chip_pairs = [(i, i + 1) for i in range(1, sec - 1, 2)]
     chip_pairs = chip_pairs + [(j, i) for i, j in chip_pairs]
 
-    def swap(inner, outer):
-        outer = lax.ppermute(outer, "sec", chip_pairs)
-        inner = lax.ppermute(inner, "sec", core_pairs)
-        return inner, outer
-
-    def edges(x, axis):
-        inner = lax.dynamic_index_in_dim(x, 1 - core, axis, keepdims=True)
-        outer = lax.dynamic_index_in_dim(x, core, axis, keepdims=True)
-        return inner, outer
-
-    def rows(x, axis):
-        return lax.dynamic_slice_in_dim(x, term * share, share, axis)
-
-    at = jnp.arange(blocks, dtype=jnp.int32)[None, :] + term_shift[:, None]
-    slot = jnp.where(at < 0, 3 - core, jnp.where(at > 1, 2 + core, at)).astype(jnp.int32)
+    def far(x):
+        return lax.ppermute(x, "sec", chip_pairs)
+
+    def near(x):
+        return lax.ppermute(x, "sec", core_pairs)
 
     def apply_op(x, fields=(), paired=(), keep=True):
         outs = []
@@ -353,8 +409,8 @@
         result = call(
             functools.partial(apply_kernel, count),
             outs,
-            [slot, x, right_all, left_env, *fields, *paired],
-            smem=1,
+            [core_id, term_shift, x, right_all, left_here, *fields, *paired],
+            smem=2,
             scratch=[pltpu.VMEM((blocks, left_env.shape[0] * states, vecs * states), BF)],
             flops=16 * vecs * blocks * states**3,
         )
@@ -369,16 +425,54 @@
     edge_shape = shape((vecs, states, states), BF)
     four_shape = shape((vecs, 4, states, states), BF)
     lines = vecs * blocks * share
-
-    right_all = jnp.concatenate([right_env, *swap(*edges(right_env, 1))], axis=1)
-    start = jnp.where(mask[None], start_vectors, jnp.zeros((), BF))
-    start_all = jnp.concatenate([start, *swap(*edges(start, 1))], axis=1)
-    pre_core, pre_chip = swap(*edges(precond, 0))
-    early = (rows(mask.astype(F32), 1), rows(precond, 1), rows(start, 2))
-    start_all, early = barrier((start_all, early))
-    mask_rows, pre, vec = early
-    parts, pre_core, pre_chip = barrier((apply_op(start_all), pre_core, pre_chip))
-    got = exchange(parts)
+    terms = right_env.shape[0]
+
+    def in_hbm(x):
+        return pltpu.with_memory_space_constraint(x, pltpu.HBM)
+
+    start_hbm, left_hbm, right_hbm, pre_hbm = [
+        in_hbm(x) for x in (start_vectors, left_env, right_env, precond)
+    ]
+
+    (pack_chip,) = call(
+        pack_kernel,
+        [shape((terms + vecs + 1, states, states), BF)],
+        [core_id, in_hbm(block_dims), start_hbm, right_hbm, pre_hbm],
+        smem=1,
+        scratch=[
+            pltpu.SMEM(block_dims.shape, jnp.int32),
+            pltpu.VMEM((vecs, states, states), BF),
+            pltpu.VMEM((states, states), F32),
+            pltpu.SemaphoreType.DMA((2 + vecs + terms,)),
+        ],
+        anywhere=True,
+    )
+    pack_chip = far(pack_chip)
+    start, left_here, right_here, mask_rows, pre, vec, pack_core = call(
+        load_kernel,
+        [
+            shape(start_vectors.shape, BF),
+            shape(left_env.shape, BF),
+            shape(right_env.shape, BF),
+            shape((blocks, share, states), F32),
+            shape((blocks, share, states), F32),
+            shape((vecs, blocks, share, states), BF),
+            shape((terms + vecs + 1, states, states), BF),
+        ],
+        [core_id, term_id, block_dims, start_hbm, left_hbm, right_hbm, pre_hbm],
+        smem=3,
+        scratch=[
+            pltpu.VMEM(start_vectors.shape, BF),
+            pltpu.VMEM(precond.shape, F32),
+            pltpu.SemaphoreType.DMA((2 + 3 * terms,)),
+        ],
+        anywhere=True,
+    )
+    pack_core = near(pack_core)
+    packs = [pack_core, pack_chip]
+    right_all = jnp.concatenate([right_here] + [x[:terms, None] for x in packs], axis=1)
+    start_all = jnp.concatenate([start] + [x[terms : terms + vecs, None] for x in packs], axis=1)
+    got = exchange(apply_op(start_all))
     h_raw, body = call(
         functools.partial(settle_kernel, factor),
         [slice_shape, shape((groups, lines + EXTRA, states), BF)],
@@ -386,14 +480,14 @@
     )
     got = exchange(body)
     inner, outer, row = call(
-        unpack_kernel, [edge_shape, edge_shape, shape((sec, 8, 128), F32)], [core_id, got], smem=1
-    )
-    h_core, h_chip = swap(inner, outer)
+        unpack_kernel, [edge_shape, edge_shape, shape((sec, 1, 128), F32)], [core_id, got], smem=1
+    )
+    h_chip, h_core = far(outer), near(inner)
     row = exchange(row, "sec")
     dir_all, m_dir, coef = call(
         form_kernel,
         [four_shape, four_shape, shape((6, 8, 128), F32)],
-        [row, got, h_core, h_chip, start_all, precond, pre_core, pre_chip],
+        [row, got, h_core, h_chip, start_all, precond, *packs],
     )
     parts, dir_all, m_dir = barrier((apply_op(dir_all), dir_all, m_dir))
     got = exchange(parts)
@@ -405,8 +499,8 @@
     got = exchange(body)
     got, h_dir, m_dir, start_all = barrier((got, h_dir, m_dir, start_all))
     inner, outer = call(unpack_kernel, [edge_shape, edge_shape], [core_id, got], smem=1)
-    hd_core, hd_chip = swap(inner, outer)
-    (m_start,) = call(lift_start_kernel, [four_shape], [start_all, precond, pre_core, pre_chip])
+    hd_chip, hd_core = far(outer), near(inner)
+    (m_start,) = call(lift_start_kernel, [four_shape], [start_all, precond, *packs])
     known = [m_start, m_dir, dir_all, start_all]
     h_m_start, dots_start = apply_op(m_start, known)
     h_m_dir, dots_dir = apply_op(m_dir, known)
@@ -415,7 +509,7 @@
         [shape((len(PLAIN) + 2 * len(PAIRS), vecs, 8, 128), F32), slice_shape],
         [coef, vec, h_raw, h_dir, pre],
     )
-    (m_hd,) = call(lift_kernel, [four_shape], [got, hd_core, hd_chip, precond, pre_core, pre_chip])
+    (m_hd,) = call(lift_kernel, [four_shape], [got, hd_core, hd_chip, precond, *packs])
     dots_hd = apply_op(m_hd, [m_hd] + known, [h_m_start, h_m_dir], keep=False)
     everyone = groups * sec
     (row,) = call(

time: 168 us -> 161 us (0.958)
  local copies, waits for them, and re-layouts: 5 us -> 0.52 us
  blocking collectives: 114 us -> 110 us
  Pallas kernels: 14.9 us -> 18.5 us
  other arithmetic: 3.32 us -> 0.36 us
  waiting for transfers between devices: 5.95 us -> 8.74 us
  starting transfers between devices: 23.7 us -> 21.8 us
    all_to_all x6, blocking collectives: 114 us -> 110 us  [exchange(): return lax.all_to_all(parts, axis, 0, 0)]
    pallas_call x15 -> x17, Pallas kernels: 14.9 us -> 18.5 us  [call(): pl.pallas_call(kernel, out_shape=[jax.ShapeDtypeStruct(x.shape, x.dtype)...]
    ppermute x10 -> x6, waiting for transfers between devices: 5.95 us -> 8.74 us  [the longest x3 8.74 us: far(): return lax.ppermute(x, 'sec', chip_pairs)]
    dynamic_slice x5 -> x0, local copies, waits for them, and re-layouts: 2.75 us -> none  [the longest x2 1.89 us: edges(): outer = lax.dynamic_index_in_dim(x, core, axis, keepdims=True)]
    ppermute x10 -> x6, starting transfers between devices: 23.7 us -> 21.8 us  [the longest x3 18.2 us: far(): return lax.ppermute(x, 'sec', chip_pairs)]
  transfers between devices with their start and end apart: 10 -> 6, of which waited for: 3 -> 2; matrix products, arithmetic and copies ran while one was open for 3% -> 0% of each run, Pallas kernels for 4% -> 5%
where the time goes in v6:
time: 161 us
  blocking collectives  110 us (68%)
  starting transfers between devices  21.8 us (14%)
  Pallas kernels  18.5 us (11%)
  waiting for transfers between devices  8.74 us (5%)
    all_to_all x6, blocking collectives, exchange(): return lax.all_to_all(parts, axis, 0, 0)  110 us
    pallas_call x17, Pallas kernels, call(): pl.pallas_call(kernel, out_shape=[jax.ShapeDtypeStruct(x.shape, x.dtype)...  18.5 us
    ppermute x3, starting transfers between devices, far(): return lax.ppermute(x, 'sec', chip_pairs)  18.2 us
    ppermute x3, waiting for transfers between devices, far(): return lax.ppermute(x, 'sec', chip_pairs)  8.74 us
    ppermute x3, starting transfers between devices, near(): return lax.ppermute(x, 'sec', core_pairs)  3.58 us
  transfers between devices with their start and end apart: 6, of which 2 were waited for; matrix products, arithmetic and copies ran while one was open for 0% of the time, Pallas kernels for 5%

profile of v6, /device:TPU:1, one launch (start us, length us, event | category | flops | bytes accessed | tf_op | source)
XLA Modules:
  0.0 161.0 jit_solution(4363084346766494970)
XLA Ops:
  0.6 1.3 shard_map.78
  2.0 4.5 %collective-permute-start.1 = (bf16[7,256,256]{2,1,0:T(8,128)(2,1)S(1)}, bf16[7,256,256]{2,1,0:T(8,128)(2,1)S(1)}, u32[]{:S(2)}, u32[]{:S(2)}) collective-permute-start(bf16[7,256,256]{2,1,0:T(8,128)(2,1)S(1)} %shard_map.78), channel_id=1, source_target_pairs={{1,2},{3,4},{5,6},{7,8},{9,10},{11,12},{13,14},{15,16},{17,18},{19... | collective-permute-start | bytes 2752520 | tf_op jit(solution)/shard_map/ppermute | solution.py:395
  6.5 2.6 %shard_map.77 = (bf16[2,2,256,256]{3,2,1,0:T(8,128)(2,1)S(1)}, bf16[4,2,256,256]{3,2,1,0:T(8,128)(2,1)S(1)}, bf16[4,2,256,256]{3,2,1,0:T(8,128)(2,1)S(1)}, f32[2...) custom-call(s32[1]{0:T(128)} %bitcast.core_ref, ...), custom_call_target="tpu_custom_call" | custom-call | bytes 6881296 | tf_op jit(solution)/shard_map/pallas_call | solution.py:368
  9.2 8.3 %collective-permute-done.1.pre_chip = bf16[7,256,256]{2,1,0:T(8,128)(2,1)S(1)} collective-permute-done((bf16[7,256,256]{2,1,0:T(8,128)(2,1)S(1)}, bf16[7,256,256]{2,1,0:T(8,128)(2,1)S(1)}, u32[]{:S(2)}, u32[]{:S(2)}) %collective-permute-start.1) | collective-permute-done | bytes 917536 | tf_op jit(solution)/shard_map/ppermute | solution.py:395
  18.1 0.4 copy-done.1
  18.5 1.8 %shard_map.79 = bf16[8,2,2,32,256]{4,3,2,1,0:T(8,128)(2,1)S(1)} custom-call(s32[1]{0:T(128)} %bitcast.core_ref, s32[4]{0:T(128)S(1)} %copy-done.1, bf16[2,4,256,256]{3,2,1,0:T(8,128)(2,1)S(1)} %pad_maximum_fusion.1.x_ref.start_ref.refs_3_.refs_4_, bf16[4,4,256,256]{3,2,1,0:T(8,128)(2,1)S(1)} %pad_maximum_fusion.right_ref, ...), custom_call_target="tpu_custom_call" | custom-call | flops 1073741824 | bytes 4718612 | tf_op jit(solution)/shard_map/pallas_call | solution.py:368
  20.3 20.9 %all_to_all.30.got_ref = bf16[8,2,2,32,256]{4,3,2,1,0:T(8,128)(2,1)S(1)} all-to-all(bf16[8,2,2,32,256]{4,3,2,1,0:T(8,128)(2,1)S(1)} %shard_map.79), channel_id=1, replica_groups=mesh['term'=8,'sec'=32] {'term'}, dimensions={0} | all-to-all | bytes 1048576 | tf_op jit(solution)/shard_map/all_to_all | solution.py:420
  41.5 18.0 %all_to_all.31.got_ref = bf16[8,144,256]{2,1,0:T(8,128)(2,1)S(1)} all-to-all(bf16[8,144,256]{2,1,0:T(8,128)(2,1)S(1)} %get-tuple-element.41), channel_id=1, replica_groups=mesh['term'=8,'sec'=32] {'term'}, dimensions={0} | all-to-all | bytes 1179648 | tf_op jit(solution)/shard_map/all_to_all | solution.py:420
  59.6 11.4 %collective-permute-start.3 = (bf16[2,256,256]{2,1,0:T(8,128)(2,1)S(1)}, bf16[2,256,256]{2,1,0:T(8,128)(2,1)S(1)}, u32[]{:S(2)}, u32[]{:S(2)}) collective-permute-start(bf16[2,256,256]{2,1,0:T(8,128)(2,1)S(1)} %get-tuple-element.44), channel_id=1, source_target_pairs={{1,2},{3,4},{5,6},{7,8},{9,10},{11,12},{13,14},{15,16},{17,18},{19... | collective-permute-start | bytes 786440 | tf_op jit(solution)/shard_map/ppermute | solution.py:395
  71.0 16.0 %all_to_all.32.row_ref = f32[32,1,128]{2,1,0:T(1,128)S(1)} all-to-all(f32[32,1,128]{2,1,0:T(1,128)S(1)} %get-tuple-element.42), channel_id=1, replica_groups=mesh['term'=8,'sec'=32] {'sec'}, dimensions={0} | all-to-all | bytes 32768 | tf_op jit(solution)/shard_map/all_to_all | solution.py:420
  87.0 1.5 shard_map.82
  88.5 1.8 %shard_map.83 = bf16[8,2,2,32,256]{4,3,2,1,0:T(8,128)(2,1)S(1)} custom-call(s32[1]{0:T(128)} %bitcast.core_ref, s32[4]{0:T(128)S(1)} %copy-done.1, bf16[2,4,256,256]{3,2,1,0:T(8,128)(2,1)S(1)} %get-tuple-element.60.x_ref.refs_2_.refs_3_, bf16[4,4,256,256]{3,2,1,0:T(8,128)(2,1)S(1)} %pad_maximum_fusion.right_ref, ...), custom_call_target="tpu_custom_call" | custom-call | flops 1073741824 | bytes 4718612 | tf_op jit(solution)/shard_map/pallas_call | solution.py:368
  90.4 19.1 %all_to_all.33.got_ref = bf16[8,2,2,32,256]{4,3,2,1,0:T(8,128)(2,1)S(1)} all-to-all(bf16[8,2,2,32,256]{4,3,2,1,0:T(8,128)(2,1)S(1)} %shard_map.83), channel_id=1, replica_groups=mesh['term'=8,'sec'=32] {'term'}, dimensions={0} | all-to-all | bytes 1048576 | tf_op jit(solution)/shard_map/all_to_all | solution.py:420
  109.6 17.5 %all_to_all.34.got_ref = bf16[8,128,256]{2,1,0:T(8,128)(2,1)S(1)} all-to-all(bf16[8,128,256]{2,1,0:T(8,128)(2,1)S(1)} %get-tuple-element.50), channel_id=1, replica_groups=mesh['term'=8,'sec'=32] {'term'}, dimensions={0} | all-to-all | bytes 1048576 | tf_op jit(solution)/shard_map/all_to_all | solution.py:420
  127.2 3.4 %collective-permute-start.4 = (bf16[2,256,256]{2,1,0:T(8,128)(2,1)S(1)}, bf16[2,256,256]{2,1,0:T(8,128)(2,1)S(1)}, u32[]{:S(2)}, u32[]{:S(2)}) collective-permute-start(bf16[2,256,256]{2,1,0:T(8,128)(2,1)S(1)} %get-tuple-element.56), channel_id=1, source_target_pairs={{0,1},{1,0},{2,3},{3,2},{4,5},{5,4},{6,7},{7,6},{8,9},{9,8},{10,11... | collective-permute-start | bytes 786440 | tf_op jit(solution)/shard_map/ppermute | solution.py:398
  130.6 2.3 %collective-permute-start.5 = (bf16[2,256,256]{2,1,0:T(8,128)(2,1)S(1)}, bf16[2,256,256]{2,1,0:T(8,128)(2,1)S(1)}, u32[]{:S(2)}, u32[]{:S(2)}) collective-permute-start(bf16[2,256,256]{2,1,0:T(8,128)(2,1)S(1)} %get-tuple-element.57), channel_id=1, source_target_pairs={{1,2},{3,4},{5,6},{7,8},{9,10},{11,12},{13,14},{15,16},{17,18},{19... | collective-permute-start | bytes 786440 | tf_op jit(solution)/shard_map/ppermute | solution.py:395
  132.9 0.5 shard_map.85
  133.6 2.1 %shard_map.90 = (bf16[2,2,256,256]{3,2,1,0:T(8,128)(2,1)S(1)}, f32[4,2,8,128]{3,2,1,0:T(8,128)S(1)}) custom-call(s32[1]{0:T(128)} %bitcast.core_ref, s32[4]{0:T(128)S(1)} %copy-done.1, bf16[2,4,256,256]{3,2,1,0:T(8,128)(2,1)S(1)} %get-tuple-element.59.refs_1_.x_ref.refs_2_, bf16[4,4,256,256]{3,2,1,0:T(8,128)(2,1)S(1)} %pad_maximum_fusion.right_ref, ...), custom_call_target="tpu_custom_call" | custom-call | flops 1073741824 | bytes 8945684 | tf_op jit(solution)/shard_map/pallas_call | solution.py:368
  135.7 2.1 %shard_map.89 = (bf16[2,2,256,256]{3,2,1,0:T(8,128)(2,1)S(1)}, f32[4,2,8,128]{3,2,1,0:T(8,128)S(1)}) custom-call(s32[1]{0:T(128)} %bitcast.core_ref, s32[4]{0:T(128)S(1)} %copy-done.1, bf16[2,4,256,256]{3,2,1,0:T(8,128)(2,1)S(1)} %shard_map.88.x_ref.refs_0_.refs_1_, bf16[4,4,256,256]{3,2,1,0:T(8,128)(2,1)S(1)} %pad_maximum_fusion.right_ref, ...), custom_call_target="tpu_custom_call" | custom-call | flops 1073741824 | bytes 8945684 | tf_op jit(solution)/shard_map/pallas_call | solution.py:368
  137.8 0.4 collective-permute-done.5.chip_ref
  138.5 2.3 %shard_map.91.refs_1_ = f32[7,2,8,128]{3,2,1,0:T(8,128)S(1)} custom-call(s32[1]{0:T(128)} %bitcast.core_ref, s32[4]{0:T(128)S(1)} %copy-done.1, bf16[2,4,256,256]{3,2,1,0:T(8,128)(2,1)S(1)} %shard_map.87.x_ref.refs_0_, bf16[4,4,256,256]{3,2,1,0:T(8,128)(2,1)S(1)} %pad_maximum_fusion.right_ref, bf16[4,2,256,256]{3,2,1,0:T(8,128)(2,1)S(1)} %get-tuple-element.37.left_ref, ...), custom_call_target="tpu_custom_call" | custom-call | flops 1073741824 | bytes 10543124 | tf_op jit(solution)/shard_map/pallas_call | solution.py:368
  140.8 0.3 shard_map.92
  141.1 18.5 %all_to_all.35.row_ref = f32[256,1,128]{2,1,0:T(1,128)S(1)} all-to-all(f32[256,1,128]{2,1,0:T(1,128)S(1)} %shard_map.92), channel_id=1, replica_groups=mesh['term'=8,'sec'=32] {'term','sec'}, dimensions={0} | all-to-all | bytes 262144 | tf_op jit(solution)/shard_map/all_to_all | solution.py:420
  159.6 1.2 shard_map.93
  (23 shorter events, 1.6 us)
Async XLA Ops:
  0.6 5.8 %copy-start.2 = (s32[2]{0:T(128)S(1)}, s32[2]{0:T(128)}, u32[]{:S(2)}) copy-start(s32[2]{0:T(128)} %dims_hbm.1) | copy-start | bytes 28
  2.0 15.6 %collective-permute-start.1 = (bf16[7,256,256]{2,1,0:T(8,128)(2,1)S(1)}, bf16[7,256,256]{2,1,0:T(8,128)(2,1)S(1)}, u32[]{:S(2)}, u32[]{:S(2)}) collective-permute-start(bf16[7,256,256]{2,1,0:T(8,128)(2,1)S(1)} %shard_map.78), channel_id=1, source_target_pairs={{1,2},{3,4},{5,6},{7,8},{9,10},{11,12},{13,14},{15,16},{17,18},{19... | collective-permute-start | bytes 2752520 | tf_op jit(solution)/shard_map/ppermute | solution.py:395
  9.1 8.4 %collective-permute-start = (bf16[7,256,256]{2,1,0:T(8,128)(2,1)S(1)}, bf16[7,256,256]{2,1,0:T(8,128)(2,1)S(1)}, u32[]{:S(2)}, u32[]{:S(2)}) collective-permute-start(bf16[7,256,256]{2,1,0:T(8,128)(2,1)S(1)} %get-tuple-element.35), channel_id=1, source_target_pairs={{0,1},{1,0},{2,3},{3,2},{4,5},{5,4},{6,7},{7,6},{8,9},{9,8},{10,11... | collective-permute-start | bytes 2752520 | tf_op jit(solution)/shard_map/ppermute | solution.py:398
  17.8 0.7 copy-start.1
  20.3 66.7 %copy-start = (f32[2,256,256]{2,1,0:T(8,128)S(1)}, f32[2,256,256]{2,1,0:T(8,128)}, u32[]{:S(2)}) copy-start(f32[2,256,256]{2,1,0:T(8,128)} %pre_ref.9) | copy-start | bytes 1572868
  59.5 27.5 %collective-permute-start.2 = (bf16[2,256,256]{2,1,0:T(8,128)(2,1)S(1)}, bf16[2,256,256]{2,1,0:T(8,128)(2,1)S(1)}, u32[]{:S(2)}, u32[]{:S(2)}) collective-permute-start(bf16[2,256,256]{2,1,0:T(8,128)(2,1)S(1)} %get-tuple-element.43), channel_id=1, source_target_pairs={{0,1},{1,0},{2,3},{3,2},{4,5},{5,4},{6,7},{7,6},{8,9},{9,8},{10,11... | collective-permute-start | bytes 786440 | tf_op jit(solution)/shard_map/ppermute | solution.py:398
  59.6 27.4 %collective-permute-start.3 = (bf16[2,256,256]{2,1,0:T(8,128)(2,1)S(1)}, bf16[2,256,256]{2,1,0:T(8,128)(2,1)S(1)}, u32[]{:S(2)}, u32[]{:S(2)}) collective-permute-start(bf16[2,256,256]{2,1,0:T(8,128)(2,1)S(1)} %get-tuple-element.44), channel_id=1, source_target_pairs={{1,2},{3,4},{5,6},{7,8},{9,10},{11,12},{13,14},{15,16},{17,18},{19... | collective-permute-start | bytes 786440 | tf_op jit(solution)/shard_map/ppermute | solution.py:395
  127.2 10.6 %collective-permute-start.4 = (bf16[2,256,256]{2,1,0:T(8,128)(2,1)S(1)}, bf16[2,256,256]{2,1,0:T(8,128)(2,1)S(1)}, u32[]{:S(2)}, u32[]{:S(2)}) collective-permute-start(bf16[2,256,256]{2,1,0:T(8,128)(2,1)S(1)} %get-tuple-element.56), channel_id=1, source_target_pairs={{0,1},{1,0},{2,3},{3,2},{4,5},{5,4},{6,7},{7,6},{8,9},{9,8},{10,11... | collective-permute-start | bytes 786440 | tf_op jit(solution)/shard_map/ppermute | solution.py:398
  130.6 7.7 %collective-permute-start.5 = (bf16[2,256,256]{2,1,0:T(8,128)(2,1)S(1)}, bf16[2,256,256]{2,1,0:T(8,128)(2,1)S(1)}, u32[]{:S(2)}, u32[]{:S(2)}) collective-permute-start(bf16[2,256,256]{2,1,0:T(8,128)(2,1)S(1)} %get-tuple-element.57), channel_id=1, source_target_pairs={{1,2},{3,4},{5,6},{7,8},{9,10},{11,12},{13,14},{15,16},{17,18},{19... | collective-permute-start | bytes 786440 | tf_op jit(solution)/shard_map/ppermute | solution.py:395
